TPU v7x, 256 devices: a whole 4x4x8 slice. The times are simulated.
256 devices in a mesh: dp: 32 (over z_lo, x, core), shard: 8 (over z_hi, y).
Axes of the slice: x: 4, y: 4, z: 8 (z_hi: 2, z_lo: 4; z = z_hi * 4 + z_lo), core: 2. Of those that a mesh axis runs over, the one named last changes fastest.
Arguments:
- tokens: bfloat16 [32768, 1024], P(('dp', 'shard')), may hold values from -6 to 6
- cotangent: bfloat16 [32768, 1024], P(('dp', 'shard')), may hold values from -6 to 6
- assign: int32 [32768], P('dp'), may hold values from 0 to 1
- prob: float32 [32768], P('dp'), may hold values from 0.2 to 1
- w_gate: bfloat16 [2, 1024, 4096], P(None, None, 'shard'), may hold values from -0.1875 to 0.1875
- w_up: bfloat16 [2, 1024, 4096], P(None, None, 'shard'), may hold values from -0.1875 to 0.1875
- w_down: bfloat16 [2, 4096, 1024], P(None, 'shard'), may hold values from -0.09375 to 0.09375
Outputs:
- output: bfloat16 [32768, 1024], P(('dp', 'shard'))
- input_grad: bfloat16 [32768, 1024], P(('dp', 'shard'))
- grad_gate: float32 [2, 1024, 4096], P(None, 'dp', 'shard')
- grad_up: float32 [2, 1024, 4096], P(None, 'dp', 'shard')
- grad_down: float32 [2, 4096, 1024], P(None, 'shard', 'dp')
All inputs are finite; a program needn't handle non-finite values.
Results may differ from a plain program's by a relative error of at most 0.0057.
Values may be sent and summed in bfloat16 or wider, within the bound.
No kernel may reach another device: no remote copies, remote signals or barrier semaphores. Data moves between devices by JAX's collectives and lax.ppermute only.
A program may use at most 128 MiB of HBM per device.

v0:
```python
import jax
import jax.numpy as jnp
from jax import lax
from jax.experimental import pallas as pl
from jax.experimental.pallas import tpu as pltpu
from jax.sharding import Mesh, PartitionSpec as P

EXP = 2
AXES = ("zlo", "x", "core", "zhi", "y")
SIZES = {"zlo": 4, "x": 4, "core": 2, "zhi": 2, "y": 4}
F32, BF16 = jnp.float32, jnp.bfloat16
TILE = 256


def send(value, axis, step):
    n = SIZES[axis]
    return lax.ppermute(value, axis, [(i, (i + step) % n) for i in range(n)])


def relative(values):
    rows = values.shape[0] // 8
    blocks = values.reshape(2, 4, rows)[:, ::-1]
    doubled = jnp.tile(blocks, (2, 2, 1))
    start = (lax.axis_index("zhi"), 3 - lax.axis_index("y"), 0)
    return lax.dynamic_slice(doubled, start, (2, 4, rows)).reshape(-1, 1)


def gather_group(block):
    far = send(block, "zhi", 1)
    parts = []
    for b in (block, far):
        parts += [b, send(b, "y", 1), send(b, "y", 2), send(b, "y", 3)]
    return parts


def scatter_group(own, *pieces):
    total = own
    for k, piece in enumerate(pieces, 1):
        total = total + send(piece, "y", -k).astype(F32)
    return total[0] + send(total[1].astype(BF16), "zhi", 1).astype(F32)


def scatter_rows(own, other):
    total = own + send(other, "core", 1).astype(F32)
    for axis in ("x", "zlo"):
        g = total
        n = SIZES[axis]
        me = lax.axis_index(axis)
        total = lax.dynamic_index_in_dim(g, me, 0, keepdims=False)
        for k in range(1, n):
            piece = lax.dynamic_index_in_dim(g, (me + k) % n, 0, keepdims=False)
            total = total + send(piece.astype(BF16), axis, k).astype(F32)
    return total


def dot(a, b, ca, cb):
    return lax.dot_general(a, b, (((ca,), (cb,)), ((), ())), preferred_element_type=F32)


def split(value, second):
    zero = jnp.zeros_like(value)
    return jnp.where(second, zero, value), jnp.where(second, value, zero)


def put_rows(value, own, s1, s2, s3):
    i = pl.program_id(0)
    half = value.shape[0] // 2

    @pl.when(i % 2 == 0)
    def _():
        own[pl.ds(i // 2, 1)] = value[:half][None]
        s1[pl.ds(i // 2, 1)] = value[half:].astype(BF16)[None]

    @pl.when(i % 2 == 1)
    def _():
        s2[pl.ds(i // 2, 1)] = value[:half].astype(BF16)[None]
        s3[pl.ds(i // 2, 1)] = value[half:].astype(BF16)[None]


def put_grad(value, core, own, other):
    v = value.reshape(4, 2, value.shape[0] // 8, value.shape[1])
    first = core == 0
    own[...] = jnp.where(first, v[:, 0], v[:, 1])[:, None]
    other[...] = jnp.where(first, v[:, 1], v[:, 0]).astype(BF16)[:, None]


def forward_kernel(second_ref, *refs):
    blocks = refs[:8]
    wg, wu, wd, x_ref, hh_ref, a_ref, s_ref = refs[8:15]
    i = pl.program_id(0)
    n = blocks[0].shape[0]

    @pl.when(i == 0)
    def _():
        for b, block in enumerate(blocks):
            x_ref[b * n : (b + 1) * n] = block[...]

    rows = pl.ds(pl.multiple_of(i * TILE, TILE), TILE)
    second = second_ref[rows] > 0
    x0, x1 = split(x_ref[rows], second)
    xx = jnp.concatenate([x0, x1], axis=1)
    gate = dot(xx, wg[...], 1, 0)
    up = dot(xx, wu[...], 1, 0)
    sigma = 1.0 / (1.0 + jnp.exp(-gate))
    silu = gate * sigma
    a_ref[...] = up * sigma * (1.0 + gate * (1.0 - sigma))
    s_ref[...] = silu
    hidden = (silu * up).astype(BF16)
    hh = jnp.concatenate(split(hidden, second), axis=1)
    hh_ref[...] = hh
    put_rows(dot(hh, wd[...], 1, 0), *refs[15:19])


def down_kernel(core_ref, scale_ref, *refs):
    blocks = refs[:8]
    hh, dout, own, other = refs[8:]
    i = pl.program_id(0)
    n = blocks[0].shape[0]

    @pl.when(i == 0)
    def _():
        for b, block in enumerate(blocks):
            at = slice(b * n, (b + 1) * n)
            dout[at] = (scale_ref[at] * block[...].astype(F32)).astype(BF16)

    columns = pl.ds(pl.multiple_of(i * TILE, TILE), TILE)
    put_grad(dot(dout[:, columns], hh[...], 0, 0), core_ref[0], own, other)


def back_kernel(second_ref, dout, wd, a_ref, s_ref, gu_ref):
    second = second_ref[...] > 0
    ff = a_ref.shape[1]
    both = dot(dout[...], wd[...], 1, 1)
    back = jnp.where(second, both[:, ff:], both[:, :ff])
    gate_grad = (back * a_ref[...]).astype(BF16)
    up_grad = (back * s_ref[...]).astype(BF16)
    gu_ref[...] = jnp.concatenate(split(gate_grad, second) + split(up_grad, second), axis=1)


def weight_kernel(core_ref, x_ref, gu, own, other):
    put_grad(dot(x_ref[...], gu[...], 0, 0), core_ref[0], own, other)


def input_kernel(gu, wg, wu, *outs):
    ff = wg.shape[2]
    total = None
    for j, w in enumerate((wg, wu)):
        for e in range(EXP):
            c = (j * EXP + e) * ff
            term = dot(gu[:, c : c + ff], w[e], 1, 1)
            total = term if total is None else total + term
    put_rows(total, *outs)


def call(kernel, grid, ins, outs, flops, scalars=0):
    moved = sum(a.size * a.dtype.itemsize for *_, a in ins + outs)
    return pl.pallas_call(
        kernel,
        out_shape=[jax.ShapeDtypeStruct(a.shape, a.dtype) for *_, a in outs],
        grid_spec=pltpu.PrefetchScalarGridSpec(
            num_scalar_prefetch=scalars,
            grid=(grid,),
            in_specs=[pl.BlockSpec(b, m) for b, m, _ in ins],
            out_specs=[pl.BlockSpec(b, m) for b, m, _ in outs],
        ),
        compiler_params=pltpu.CompilerParams(vmem_limit_bytes=56 << 20),
        cost_estimate=pl.CostEstimate(flops=flops, bytes_accessed=moved, transcendentals=0),
    )


def whole(a):
    return (a.shape, lambda i, *_: (0,) * len(a.shape), a)


def tiled(a, axis, size):
    block = tuple(size if d == axis else n for d, n in enumerate(a.shape))
    return (block, lambda i, *_: tuple(i if d == axis else 0 for d in range(len(a.shape))), a)


def sds(shape, dtype):
    return jax.ShapeDtypeStruct(shape, dtype)


def per_device(tokens, cotangent, assign, prob, w_gate, w_up, w_down):
    block, width = tokens.shape
    rows = assign.shape[0]
    ff = w_gate.shape[2]
    steps = rows // TILE
    own_rows = width // 32
    wide = EXP * ff
    unit = 2 * rows * width * ff * EXP
    second = relative(assign)
    scale = relative(prob)
    core = lax.axis_index("core").astype(jnp.int32).reshape(1)
    xs = gather_group(tokens)
    ds = gather_group(cotangent)
    wg2, wu2 = (w.reshape(EXP * width, ff) for w in (w_gate, w_up))
    wd2 = w_down.reshape(wide, width)
    pieces = [whole(sds((2, block, width), t)) for t in (F32, BF16, BF16, BF16)]

    def grads(columns):
        return [tiled(sds((4, 4, own_rows, columns), t), 1, 1) for t in (F32, BF16)]

    ins = [whole(a) for a in (second, *xs, wg2, wu2, wd2)]
    outs = [
        whole(sds((rows, width), BF16)),
        tiled(sds((rows, wide), BF16), 0, TILE),
        tiled(sds((rows, ff), F32), 0, TILE),
        tiled(sds((rows, ff), F32), 0, TILE),
        *pieces,
    ]
    x, hh, act, silu, *out_pieces = call(forward_kernel, steps, ins, outs, 3 * unit)(*(a for *_, a in ins))

    ins = [whole(a) for a in (scale, *ds, hh)]
    outs = [whole(sds((rows, width), BF16)), *grads(wide)]
    dout, *down = call(down_kernel, 4, ins, outs, unit, 1)(core, *(a for *_, a in ins))

    ins = [tiled(second, 0, TILE), tiled(dout, 0, TILE), whole(wd2), tiled(act, 0, TILE), tiled(silu, 0, TILE)]
    outs = [tiled(sds((rows, 2 * wide), BF16), 0, TILE)]
    (gu,) = call(back_kernel, steps, ins, outs, unit)(*(a for *_, a in ins))

    ins = [tiled(x, 1, TILE), whole(gu)]
    gate_up = call(weight_kernel, 4, ins, grads(2 * wide), 2 * unit, 1)(core, *(a for *_, a in ins))

    gu, gate_up = lax.optimization_barrier((gu, gate_up))
    ins = [tiled(gu, 0, TILE), whole(w_gate), whole(w_up)]
    in_pieces = call(input_kernel, steps, ins, pieces, 2 * unit)(*(a for *_, a in ins))

    output = scatter_group(*out_pieces) * scale[:block]
    grad_down = scatter_rows(*down).reshape(own_rows, EXP, ff)
    both = scatter_rows(*gate_up).reshape(own_rows, 2, EXP, ff)
    input_grad = scatter_group(*in_pieces)
    return (
        output.astype(BF16),
        input_grad.astype(BF16),
        both[:, 0].swapaxes(0, 1),
        both[:, 1].swapaxes(0, 1),
        grad_down.transpose(1, 2, 0),
    )


def solution(mesh):
    fine = Mesh(mesh.devices.reshape(*SIZES.values()), AXES)
    dp, shard = ("zlo", "x", "core"), ("zhi", "y")
    return jax.shard_map(
        per_device,
        mesh=fine,
        in_specs=(
            P(AXES, None),
            P(AXES, None),
            P(dp),
            P(dp),
            P(None, None, shard),
            P(None, None, shard),
            P(None, shard, None),
        ),
        out_specs=(
            P(AXES, None),
            P(AXES, None),
            P(None, dp, shard),
            P(None, dp, shard),
            P(None, shard, dp),
        ),
        check_vma=False,
    )
```

profile of v0, /device:TPU:6, one launch (start us, length us, event | category | flops | bytes accessed | tf_op | source)
XLA Modules:
  0.0 189.0 jit_solution(10443073499976777664)
XLA Ops:
  2.3 7.2 %collective-permute-start.3 = (bf16[128,1024]{1,0:T(8,128)(2,1)}, bf16[128,1024]{1,0:T(8,128)(2,1)S(1)}, u32[]{:S(2)}, u32[]{:S(2)}) collective-permute-start(bf16[128,1024]{1,0:T(8,128)(2,1)} %refs_0_.2), channel_id=1, source_target_pairs={{0,4},{4,0},{1,5},{5,1},{2,6},{6,2},{3,7},{7,3},{8,12},{12,8},{9,1... | collective-permute-start | bytes 786440 | tf_op jit(solution)/shard_map/ppermute | solution.py:17
  9.5 2.9 %collective-permute-start.1 = (bf16[128,1024]{1,0:T(8,128)(2,1)}, bf16[128,1024]{1,0:T(8,128)(2,1)S(1)}, u32[]{:S(2)}, u32[]{:S(2)}) collective-permute-start(bf16[128,1024]{1,0:T(8,128)(2,1)} %refs_0_.2), channel_id=1, source_target_pairs={{0,2},{1,3},{2,0},{3,1},{4,6},{5,7},{6,4},{7,5},{8,10},{9,11},{10,... | collective-permute-start | bytes 786440 | tf_op jit(solution)/shard_map/ppermute | solution.py:17
  15.9 2.8 %collective-permute-start.14 = (bf16[128,1024]{1,0:T(8,128)(2,1)}, bf16[128,1024]{1,0:T(8,128)(2,1)S(1)}, u32[]{:S(2)}, u32[]{:S(2)}) collective-permute-start(bf16[128,1024]{1,0:T(8,128)(2,1)} %refs_0_.3), channel_id=1, source_target_pairs={{0,4},{4,0},{1,5},{5,1},{2,6},{6,2},{3,7},{7,3},{8,12},{12,8},{9,1... | collective-permute-start | bytes 786440 | tf_op jit(solution)/shard_map/ppermute | solution.py:17
  18.7 4.6 %collective-permute-start.4 = (bf16[128,1024]{1,0:T(8,128)(2,1)S(1)}, bf16[128,1024]{1,0:T(8,128)(2,1)S(1)}, u32[]{:S(2)}, u32[]{:S(2)}) collective-permute-start(bf16[128,1024]{1,0:T(8,128)(2,1)S(1)} %collective-permute-done.3.refs_4_), channel_id=1, source_target_pairs={{0,1},{1,2},{2,3},{3,0},{4,5},{5,6},{6,7},{7,4},{8,9},{9,10},{10,1... | collective-permute-start | bytes 786440 | tf_op jit(solution)/shard_map/ppermute | solution.py:17
  23.3 3.0 %collective-permute-start.5 = (bf16[128,1024]{1,0:T(8,128)(2,1)S(1)}, bf16[128,1024]{1,0:T(8,128)(2,1)S(1)}, u32[]{:S(2)}, u32[]{:S(2)}) collective-permute-start(bf16[128,1024]{1,0:T(8,128)(2,1)S(1)} %collective-permute-done.3.refs_4_), channel_id=1, source_target_pairs={{0,2},{1,3},{2,0},{3,1},{4,6},{5,7},{6,4},{7,5},{8,10},{9,11},{10,... | collective-permute-start | bytes 786440 | tf_op jit(solution)/shard_map/ppermute | solution.py:17
  26.2 2.5 %collective-permute-start.6 = (bf16[128,1024]{1,0:T(8,128)(2,1)S(1)}, bf16[128,1024]{1,0:T(8,128)(2,1)S(1)}, u32[]{:S(2)}, u32[]{:S(2)}) collective-permute-start(bf16[128,1024]{1,0:T(8,128)(2,1)S(1)} %collective-permute-done.3.refs_4_), channel_id=1, source_target_pairs={{0,3},{1,0},{2,1},{3,2},{4,7},{5,4},{6,5},{7,6},{8,11},{9,8},{10,9... | collective-permute-start | bytes 786440 | tf_op jit(solution)/shard_map/ppermute | solution.py:17
  30.9 5.0 %collective-permute-done.14.refs_4_ = bf16[128,1024]{1,0:T(8,128)(2,1)S(1)} collective-permute-done((bf16[128,1024]{1,0:T(8,128)(2,1)}, bf16[128,1024]{1,0:T(8,128)(2,1)S(1)}, u32[]{:S(2)}, u32[]{:S(2)}) %collective-permute-start.14) | collective-permute-done | bytes 262176 | tf_op jit(solution)/shard_map/ppermute | solution.py:17
  35.9 2.5 %collective-permute-start.13 = (bf16[128,1024]{1,0:T(8,128)(2,1)}, bf16[128,1024]{1,0:T(8,128)(2,1)S(1)}, u32[]{:S(2)}, u32[]{:S(2)}) collective-permute-start(bf16[128,1024]{1,0:T(8,128)(2,1)} %refs_0_.3), channel_id=1, source_target_pairs={{0,3},{1,0},{2,1},{3,2},{4,7},{5,4},{6,5},{7,6},{8,11},{9,8},{10,9... | collective-permute-start | bytes 786440 | tf_op jit(solution)/shard_map/ppermute | solution.py:17
  41.8 4.0 %collective-permute-start.17 = (bf16[128,1024]{1,0:T(8,128)(2,1)S(1)}, bf16[128,1024]{1,0:T(8,128)(2,1)S(1)}, u32[]{:S(2)}, u32[]{:S(2)}) collective-permute-start(bf16[128,1024]{1,0:T(8,128)(2,1)S(1)} %collective-permute-done.14.refs_4_), channel_id=1, source_target_pairs={{0,3},{1,0},{2,1},{3,2},{4,7},{5,4},{6,5},{7,6},{8,11},{9,8},{10,9... | collective-permute-start | bytes 786440 | tf_op jit(solution)/shard_map/ppermute | solution.py:17
  45.8 15.1 %shard_map.110 = (bf16[1024,1024]{1,0:T(8,128)(2,1)}, bf16[1024,1024]{1,0:T(8,128)(2,1)}, f32[1024,512]{1,0:T(8,128)}, f32[1024,512]{1,0:T(8,128)}, f32[2,128,10...) custom-call(s32[1024,1]{1,0:T(8,128)} %copy.15.second_ref, ...), custom_call_target="tpu_custom_call" | custom-call | flops 6442450944 | bytes 19402752 | tf_op jit(solution)/shard_map/pallas_call | solution.py:212
  65.5 7.1 %shard_map.111 = (bf16[1024,1024]{1,0:T(8,128)(2,1)}, f32[4,4,32,1024]{3,2,1,0:T(8,128)}, bf16[4,4,32,1024]{3,2,1,0:T(8,128)(2,1)}) custom-call(s32[1]{0:T(128)} %bitcast.12.core_ref, f32[1024,1]{1,0:T(8,128)} %copy.16.scale_ref, bf16[128,1024]{1,0:T(8,128)(2,1)} %refs_0_.3, bf16[128,1024]{1,0:T(8,128)(2,1)} %copy-done.5, bf16[128,1024]{1,0:T(8,128)(2,1)} %copy-done.14, ...), custom_call_target="tpu_custom_call" | custom-call | flops 2147483648 | bytes 9441280 | tf_op jit(solution)/shard_map/pallas_call | solution.py:216
  72.6 7.9 %shard_map.112.gu = bf16[1024,2048]{1,0:T(8,128)(2,1)} custom-call(s32[1024,1]{1,0:T(8,128)} %copy.15.second_ref, bf16[1024,1024]{1,0:T(8,128)(2,1)} %get-tuple-element.30.dout, bf16[1024,1024]{1,0:T(8,128)(2,1)} %bitcast.94, f32[1024,512]{1,0:T(8,128)} %get-tuple-element.31.a_ref, f32[1024,512]{1,0:T(8,128)} %get-tuple-element.32.s_ref), custom_call_target="tpu_custom_call" | custom-call | flops 2147483648 | bytes 12587008 | tf_op jit(solution)/shard_map/pallas_call | solution.py:220
  80.5 9.0 %shard_map.113 = (f32[4,4,32,2048]{3,2,1,0:T(8,128)}, bf16[4,4,32,2048]{3,2,1,0:T(8,128)(2,1)}) custom-call(s32[1]{0:T(128)} %bitcast.12.core_ref, bf16[1024,1024]{1,0:T(8,128)(2,1)} %get-tuple-element.33.x_ref, bf16[1024,2048]{1,0:T(8,128)(2,1)} %shard_map.112.gu), custom_call_target="tpu_custom_call" | custom-call | flops 4294967296 | bytes 12582912 | tf_op jit(solution)/shard_map/pallas_call | solution.py:223
  89.6 9.6 %shard_map.114 = (f32[2,128,1024]{2,1,0:T(8,128)}, bf16[2,128,1024]{2,1,0:T(8,128)(2,1)}, bf16[2,128,1024]{2,1,0:T(8,128)(2,1)}, bf16[2,128,1024]{2,1,0:T(8,128)(2,1)}) custom-call(bf16[1024,2048]{1,0:T(8,128)(2,1)} %shard_map.112.gu, bf16[2,1024,512]{2,1,0:T(8,128)(2,1)} %wg.1, bf16[2,1024,512]{2,1,0:T(8,128)(2,1)} %wu.1), custom_call_target="tpu_custom_call" | custom-call | flops 4294967296 | bytes 11010048 | tf_op jit(solution)/shard_map/pallas_call | solution.py:227
  102.1 2.5 %collective-permute-start.18 = (bf16[2,128,1024]{2,1,0:T(8,128)(2,1)}, bf16[2,128,1024]{2,1,0:T(8,128)(2,1)S(1)}, u32[]{:S(2)}, u32[]{:S(2)}) collective-permute-start(bf16[2,128,1024]{2,1,0:T(8,128)(2,1)} %get-tuple-element.38), channel_id=1, source_target_pairs={{0,3},{1,0},{2,1},{3,2},{4,7},{5,4},{6,5},{7,6},{8,11},{9,8},{10,9... | collective-permute-start | bytes 1572872 | tf_op jit(solution)/shard_map/ppermute | solution.py:17
  105.0 21.0 %collective-permute-done.20 = bf16[2,128,1024]{2,1,0:T(8,128)(2,1)S(1)} collective-permute-done((bf16[2,128,1024]{2,1,0:T(8,128)(2,1)}, bf16[2,128,1024]{2,1,0:T(8,128)(2,1)S(1)}, u32[]{:S(2)}, u32[]{:S(2)}) %collective-permute-start.20) | collective-permute-done | bytes 524320 | tf_op jit(solution)/shard_map/ppermute | solution.py:17
  127.7 4.7 %collective-permute-start.21 = (bf16[128,1024]{1,0:T(8,128)(2,1)S(1)}, bf16[128,1024]{1,0:T(8,128)(2,1)S(1)}, u32[]{:S(2)}, u32[]{:S(2)}) collective-permute-start(bf16[128,1024]{1,0:T(8,128)(2,1)S(1)} %fusion.16), channel_id=1, source_target_pairs={{0,4},{4,0},{1,5},{5,1},{2,6},{6,2},{3,7},{7,3},{8,12},{12,8},{9,1... | collective-permute-start | bytes 786440 | tf_op jit(solution)/shard_map/ppermute | solution.py:17
  132.4 6.1 %collective-permute-done.10 = bf16[128,1024]{1,0:T(8,128)(2,1)S(1)} collective-permute-done((bf16[128,1024]{1,0:T(8,128)(2,1)S(1)}, bf16[128,1024]{1,0:T(8,128)(2,1)S(1)}, u32[]{:S(2)}, u32[]{:S(2)}) %collective-permute-start.10) | collective-permute-done | bytes 262176 | tf_op jit(solution)/shard_map/ppermute | solution.py:17
  147.5 7.5 %collective-permute-done.32 = bf16[4,32,1024]{2,1,0:T(8,128)(2,1)S(1)} collective-permute-done((bf16[4,32,1024]{2,1,0:T(8,128)(2,1)S(1)}, bf16[4,32,1024]{2,1,0:T(8,128)(2,1)S(1)}, u32[]{:S(2)}, u32[]{:S(2)}) %collective-permute-start.32) | collective-permute-done | bytes 262176 | tf_op jit(solution)/shard_map/ppermute | solution.py:17
  156.9 4.0 %collective-permute-start.35 = (bf16[32,1024]{1,0:T(8,128)(2,1)S(1)}, bf16[32,1024]{1,0:T(8,128)(2,1)S(1)}, u32[]{:S(2)}, u32[]{:S(2)}) collective-permute-start(bf16[32,1024]{1,0:T(8,128)(2,1)S(1)} %get-tuple-element.55), channel_id=1, source_target_pairs={{0,192},{64,0},{128,64},{192,128},{1,193},{65,1},{129,65},{193,129... | collective-permute-start | bytes 196616 | tf_op jit(solution)/shard_map/ppermute | solution.py:17
  160.9 7.0 %collective-permute-start.34 = (bf16[32,1024]{1,0:T(8,128)(2,1)S(1)}, bf16[32,1024]{1,0:T(8,128)(2,1)S(1)}, u32[]{:S(2)}, u32[]{:S(2)}) collective-permute-start(bf16[32,1024]{1,0:T(8,128)(2,1)S(1)} %get-tuple-element.56), channel_id=1, source_target_pairs={{0,128},{64,192},{128,0},{192,64},{1,129},{65,193},{129,1},{193,65... | collective-permute-start | bytes 196616 | tf_op jit(solution)/shard_map/ppermute | solution.py:17
  167.9 6.0 %collective-permute-start.33 = (bf16[32,1024]{1,0:T(8,128)(2,1)S(1)}, bf16[32,1024]{1,0:T(8,128)(2,1)S(1)}, u32[]{:S(2)}, u32[]{:S(2)}) collective-permute-start(bf16[32,1024]{1,0:T(8,128)(2,1)S(1)} %get-tuple-element.54), channel_id=1, source_target_pairs={{0,64},{64,128},{128,192},{192,0},{1,65},{65,129},{129,193},{193,1... | collective-permute-start | bytes 196616 | tf_op jit(solution)/shard_map/ppermute | solution.py:17
  174.3 5.5 %collective-permute-start.27 = (bf16[32,2048]{1,0:T(8,128)(2,1)S(1)}, bf16[32,2048]{1,0:T(8,128)(2,1)S(1)}, u32[]{:S(2)}, u32[]{:S(2)}) collective-permute-start(bf16[32,2048]{1,0:T(8,128)(2,1)S(1)} %get-tuple-element.53), channel_id=1, source_target_pairs={{0,128},{64,192},{128,0},{192,64},{1,129},{65,193},{129,1},{193,65... | collective-permute-start | bytes 393224 | tf_op jit(solution)/shard_map/ppermute | solution.py:17
  183.3 4.7 %collective-permute-done.27 = bf16[32,2048]{1,0:T(8,128)(2,1)S(1)} collective-permute-done((bf16[32,2048]{1,0:T(8,128)(2,1)S(1)}, bf16[32,2048]{1,0:T(8,128)(2,1)S(1)}, u32[]{:S(2)}, u32[]{:S(2)}) %collective-permute-start.27) | collective-permute-done | bytes 131104 | tf_op jit(solution)/shard_map/ppermute | solution.py:17
  (120 shorter events, 35.7 us)
Async XLA Ops:
  2.3 16.4 %collective-permute-start.3 = (bf16[128,1024]{1,0:T(8,128)(2,1)}, bf16[128,1024]{1,0:T(8,128)(2,1)S(1)}, u32[]{:S(2)}, u32[]{:S(2)}) collective-permute-start(bf16[128,1024]{1,0:T(8,128)(2,1)} %refs_0_.2), channel_id=1, source_target_pairs={{0,4},{4,0},{1,5},{5,1},{2,6},{6,2},{3,7},{7,3},{8,12},{12,8},{9,1... | collective-permute-start | bytes 786440 | tf_op jit(solution)/shard_map/ppermute | solution.py:17
  13.7 17.2 %collective-permute-start.11 = (bf16[128,1024]{1,0:T(8,128)(2,1)}, bf16[128,1024]{1,0:T(8,128)(2,1)S(1)}, u32[]{:S(2)}, u32[]{:S(2)}) collective-permute-start(bf16[128,1024]{1,0:T(8,128)(2,1)} %refs_0_.3), channel_id=1, source_target_pairs={{0,1},{1,2},{2,3},{3,0},{4,5},{5,6},{6,7},{7,4},{8,9},{9,10},{10,1... | collective-permute-start | bytes 786440 | tf_op jit(solution)/shard_map/ppermute | solution.py:17
  15.9 20.0 %collective-permute-start.14 = (bf16[128,1024]{1,0:T(8,128)(2,1)}, bf16[128,1024]{1,0:T(8,128)(2,1)S(1)}, u32[]{:S(2)}, u32[]{:S(2)}) collective-permute-start(bf16[128,1024]{1,0:T(8,128)(2,1)} %refs_0_.3), channel_id=1, source_target_pairs={{0,4},{4,0},{1,5},{5,1},{2,6},{6,2},{3,7},{7,3},{8,12},{12,8},{9,1... | collective-permute-start | bytes 786440 | tf_op jit(solution)/shard_map/ppermute | solution.py:17
  18.7 19.8 %collective-permute-start.4 = (bf16[128,1024]{1,0:T(8,128)(2,1)S(1)}, bf16[128,1024]{1,0:T(8,128)(2,1)S(1)}, u32[]{:S(2)}, u32[]{:S(2)}) collective-permute-start(bf16[128,1024]{1,0:T(8,128)(2,1)S(1)} %collective-permute-done.3.refs_4_), channel_id=1, source_target_pairs={{0,1},{1,2},{2,3},{3,0},{4,5},{5,6},{6,7},{7,4},{8,9},{9,10},{10,1... | collective-permute-start | bytes 786440 | tf_op jit(solution)/shard_map/ppermute | solution.py:17
  26.2 15.6 %collective-permute-start.6 = (bf16[128,1024]{1,0:T(8,128)(2,1)S(1)}, bf16[128,1024]{1,0:T(8,128)(2,1)S(1)}, u32[]{:S(2)}, u32[]{:S(2)}) collective-permute-start(bf16[128,1024]{1,0:T(8,128)(2,1)S(1)} %collective-permute-done.3.refs_4_), channel_id=1, source_target_pairs={{0,3},{1,0},{2,1},{3,2},{4,7},{5,4},{6,5},{7,6},{8,11},{9,8},{10,9... | collective-permute-start | bytes 786440 | tf_op jit(solution)/shard_map/ppermute | solution.py:17
  30.9 30.1 %collective-permute-start.12 = (bf16[128,1024]{1,0:T(8,128)(2,1)}, bf16[128,1024]{1,0:T(8,128)(2,1)S(1)}, u32[]{:S(2)}, u32[]{:S(2)}) collective-permute-start(bf16[128,1024]{1,0:T(8,128)(2,1)} %refs_0_.3), channel_id=1, source_target_pairs={{0,2},{1,3},{2,0},{3,1},{4,6},{5,7},{6,4},{7,5},{8,10},{9,11},{10,... | collective-permute-start | bytes 786440 | tf_op jit(solution)/shard_map/ppermute | solution.py:17
  35.9 25.4 %collective-permute-start.13 = (bf16[128,1024]{1,0:T(8,128)(2,1)}, bf16[128,1024]{1,0:T(8,128)(2,1)S(1)}, u32[]{:S(2)}, u32[]{:S(2)}) collective-permute-start(bf16[128,1024]{1,0:T(8,128)(2,1)} %refs_0_.3), channel_id=1, source_target_pairs={{0,3},{1,0},{2,1},{3,2},{4,7},{5,4},{6,5},{7,6},{8,11},{9,8},{10,9... | collective-permute-start | bytes 786440 | tf_op jit(solution)/shard_map/ppermute | solution.py:17
  38.4 24.9 %collective-permute-start.15 = (bf16[128,1024]{1,0:T(8,128)(2,1)S(1)}, bf16[128,1024]{1,0:T(8,128)(2,1)S(1)}, u32[]{:S(2)}, u32[]{:S(2)}) collective-permute-start(bf16[128,1024]{1,0:T(8,128)(2,1)S(1)} %collective-permute-done.14.refs_4_), channel_id=1, source_target_pairs={{0,1},{1,2},{2,3},{3,0},{4,5},{5,6},{6,7},{7,4},{8,9},{9,10},{10,1... | collective-permute-start | bytes 786440 | tf_op jit(solution)/shard_map/ppermute | solution.py:17
  38.5 26.2 %collective-permute-start.16 = (bf16[128,1024]{1,0:T(8,128)(2,1)S(1)}, bf16[128,1024]{1,0:T(8,128)(2,1)S(1)}, u32[]{:S(2)}, u32[]{:S(2)}) collective-permute-start(bf16[128,1024]{1,0:T(8,128)(2,1)S(1)} %collective-permute-done.14.refs_4_), channel_id=1, source_target_pairs={{0,2},{1,3},{2,0},{3,1},{4,6},{5,7},{6,4},{7,5},{8,10},{9,11},{10,... | collective-permute-start | bytes 786440 | tf_op jit(solution)/shard_map/ppermute | solution.py:17
  41.8 22.8 %collective-permute-start.17 = (bf16[128,1024]{1,0:T(8,128)(2,1)S(1)}, bf16[128,1024]{1,0:T(8,128)(2,1)S(1)}, u32[]{:S(2)}, u32[]{:S(2)}) collective-permute-start(bf16[128,1024]{1,0:T(8,128)(2,1)S(1)} %collective-permute-done.14.refs_4_), channel_id=1, source_target_pairs={{0,3},{1,0},{2,1},{3,2},{4,7},{5,4},{6,5},{7,6},{8,11},{9,8},{10,9... | collective-permute-start | bytes 786440 | tf_op jit(solution)/shard_map/ppermute | solution.py:17
  61.0 39.0 %collective-permute-start.9 = (bf16[2,128,1024]{2,1,0:T(8,128)(2,1)}, bf16[2,128,1024]{2,1,0:T(8,128)(2,1)S(1)}, u32[]{:S(2)}, u32[]{:S(2)}) collective-permute-start(bf16[2,128,1024]{2,1,0:T(8,128)(2,1)} %get-tuple-element.28), channel_id=1, source_target_pairs={{0,1},{1,2},{2,3},{3,0},{4,5},{5,6},{6,7},{7,4},{8,9},{9,10},{10,1... | collective-permute-start | bytes 1572872 | tf_op jit(solution)/shard_map/ppermute | solution.py:17
  61.3 40.8 %collective-permute-start.8 = (bf16[2,128,1024]{2,1,0:T(8,128)(2,1)}, bf16[2,128,1024]{2,1,0:T(8,128)(2,1)S(1)}, u32[]{:S(2)}, u32[]{:S(2)}) collective-permute-start(bf16[2,128,1024]{2,1,0:T(8,128)(2,1)} %get-tuple-element.27), channel_id=1, source_target_pairs={{0,2},{1,3},{2,0},{3,1},{4,6},{5,7},{6,4},{7,5},{8,10},{9,11},{10,... | collective-permute-start | bytes 1572872 | tf_op jit(solution)/shard_map/ppermute | solution.py:17
  63.3 41.3 %collective-permute-start.7 = (bf16[2,128,1024]{2,1,0:T(8,128)(2,1)}, bf16[2,128,1024]{2,1,0:T(8,128)(2,1)S(1)}, u32[]{:S(2)}, u32[]{:S(2)}) collective-permute-start(bf16[2,128,1024]{2,1,0:T(8,128)(2,1)} %get-tuple-element.26), channel_id=1, source_target_pairs={{0,3},{1,0},{2,1},{3,2},{4,7},{5,4},{6,5},{7,6},{8,11},{9,8},{10,9... | collective-permute-start | bytes 1572872 | tf_op jit(solution)/shard_map/ppermute | solution.py:17
  89.5 54.4 %collective-permute-start.22 = (bf16[4,4,32,2048]{3,2,1,0:T(8,128)(2,1)}, bf16[4,4,32,2048]{3,2,1,0:T(8,128)(2,1)S(1)}, u32[]{:S(2)}, u32[]{:S(2)}) collective-permute-start(bf16[4,4,32,2048]{3,2,1,0:T(8,128)(2,1)} %get-tuple-element.42), channel_id=1, source_target_pairs={{0,8},{8,0},{1,9},{9,1},{2,10},{10,2},{3,11},{11,3},{4,12},{12,4},... | collective-permute-start | bytes 6291464 | tf_op jit(solution)/shard_map/ppermute | solution.py:17
  99.1 26.9 %collective-permute-start.20 = (bf16[2,128,1024]{2,1,0:T(8,128)(2,1)}, bf16[2,128,1024]{2,1,0:T(8,128)(2,1)S(1)}, u32[]{:S(2)}, u32[]{:S(2)}) collective-permute-start(bf16[2,128,1024]{2,1,0:T(8,128)(2,1)} %get-tuple-element.40), channel_id=1, source_target_pairs={{0,1},{1,2},{2,3},{3,0},{4,5},{5,6},{6,7},{7,4},{8,9},{9,10},{10,1... | collective-permute-start | bytes 1572872 | tf_op jit(solution)/shard_map/ppermute | solution.py:17
  100.0 27.3 %collective-permute-start.19 = (bf16[2,128,1024]{2,1,0:T(8,128)(2,1)}, bf16[2,128,1024]{2,1,0:T(8,128)(2,1)S(1)}, u32[]{:S(2)}, u32[]{:S(2)}) collective-permute-start(bf16[2,128,1024]{2,1,0:T(8,128)(2,1)} %get-tuple-element.39), channel_id=1, source_target_pairs={{0,2},{1,3},{2,0},{3,1},{4,6},{5,7},{6,4},{7,5},{8,10},{9,11},{10,... | collective-permute-start | bytes 1572872 | tf_op jit(solution)/shard_map/ppermute | solution.py:17
  102.1 25.2 %collective-permute-start.18 = (bf16[2,128,1024]{2,1,0:T(8,128)(2,1)}, bf16[2,128,1024]{2,1,0:T(8,128)(2,1)S(1)}, u32[]{:S(2)}, u32[]{:S(2)}) collective-permute-start(bf16[2,128,1024]{2,1,0:T(8,128)(2,1)} %get-tuple-element.38), channel_id=1, source_target_pairs={{0,3},{1,0},{2,1},{3,2},{4,7},{5,4},{6,5},{7,6},{8,11},{9,8},{10,9... | collective-permute-start | bytes 1572872 | tf_op jit(solution)/shard_map/ppermute | solution.py:17
  104.6 34.7 %collective-permute-start.29 = (bf16[4,4,32,1024]{3,2,1,0:T(8,128)(2,1)S(1)}, bf16[4,4,32,1024]{3,2,1,0:T(8,128)(2,1)S(1)}, u32[]{:S(2)}, u32[]{:S(2)}) collective-permute-start(bf16[4,4,32,1024]{3,2,1,0:T(8,128)(2,1)S(1)} %copy-done.4), channel_id=1, source_target_pairs={{0,8},{8,0},{1,9},{9,1},{2,10},{10,2},{3,11},{11,3},{4,12},{12,4},... | collective-permute-start | bytes 3145736 | tf_op jit(solution)/shard_map/ppermute | solution.py:17
  127.7 17.5 %collective-permute-start.21 = (bf16[128,1024]{1,0:T(8,128)(2,1)S(1)}, bf16[128,1024]{1,0:T(8,128)(2,1)S(1)}, u32[]{:S(2)}, u32[]{:S(2)}) collective-permute-start(bf16[128,1024]{1,0:T(8,128)(2,1)S(1)} %fusion.16), channel_id=1, source_target_pairs={{0,4},{4,0},{1,5},{5,1},{2,6},{6,2},{3,7},{7,3},{8,12},{12,8},{9,1... | collective-permute-start | bytes 786440 | tf_op jit(solution)/shard_map/ppermute | solution.py:17
  145.1 22.9 %collective-permute-start.25 = (bf16[4,32,2048]{2,1,0:T(8,128)(2,1)S(1)}, bf16[4,32,2048]{2,1,0:T(8,128)(2,1)S(1)}, u32[]{:S(2)}, u32[]{:S(2)}) collective-permute-start(bf16[4,32,2048]{2,1,0:T(8,128)(2,1)S(1)} %get-tuple-element.46), channel_id=1, source_target_pairs={{0,48},{16,0},{32,16},{48,32},{1,49},{17,1},{33,17},{49,33},{2,50}... | collective-permute-start | bytes 1572872 | tf_op jit(solution)/shard_map/ppermute | solution.py:17
  145.2 28.7 %collective-permute-start.24 = (bf16[4,32,2048]{2,1,0:T(8,128)(2,1)S(1)}, bf16[4,32,2048]{2,1,0:T(8,128)(2,1)S(1)}, u32[]{:S(2)}, u32[]{:S(2)}) collective-permute-start(bf16[4,32,2048]{2,1,0:T(8,128)(2,1)S(1)} %get-tuple-element.47), channel_id=1, source_target_pairs={{0,32},{16,48},{32,0},{48,16},{1,33},{17,49},{33,1},{49,17},{2,34}... | collective-permute-start | bytes 1572872 | tf_op jit(solution)/shard_map/ppermute | solution.py:17
  155.0 18.9 %collective-permute-start.23 = (bf16[4,32,2048]{2,1,0:T(8,128)(2,1)S(1)}, bf16[4,32,2048]{2,1,0:T(8,128)(2,1)S(1)}, u32[]{:S(2)}, u32[]{:S(2)}) collective-permute-start(bf16[4,32,2048]{2,1,0:T(8,128)(2,1)S(1)} %get-tuple-element.45), channel_id=1, source_target_pairs={{0,16},{16,32},{32,48},{48,0},{1,17},{17,33},{33,49},{49,1},{2,18}... | collective-permute-start | bytes 1572872 | tf_op jit(solution)/shard_map/ppermute | solution.py:17
  156.9 23.0 %collective-permute-start.35 = (bf16[32,1024]{1,0:T(8,128)(2,1)S(1)}, bf16[32,1024]{1,0:T(8,128)(2,1)S(1)}, u32[]{:S(2)}, u32[]{:S(2)}) collective-permute-start(bf16[32,1024]{1,0:T(8,128)(2,1)S(1)} %get-tuple-element.55), channel_id=1, source_target_pairs={{0,192},{64,0},{128,64},{192,128},{1,193},{65,1},{129,65},{193,129... | collective-permute-start | bytes 196616 | tf_op jit(solution)/shard_map/ppermute | solution.py:17
  160.9 20.9 %collective-permute-start.34 = (bf16[32,1024]{1,0:T(8,128)(2,1)S(1)}, bf16[32,1024]{1,0:T(8,128)(2,1)S(1)}, u32[]{:S(2)}, u32[]{:S(2)}) collective-permute-start(bf16[32,1024]{1,0:T(8,128)(2,1)S(1)} %get-tuple-element.56), channel_id=1, source_target_pairs={{0,128},{64,192},{128,0},{192,64},{1,129},{65,193},{129,1},{193,65... | collective-permute-start | bytes 196616 | tf_op jit(solution)/shard_map/ppermute | solution.py:17
  (31 other events, 412.8 us)
where the time goes:
time: 193 us; the launch traced here: 189 us
  starting transfers between devices  81.2 us (42%)
  Pallas kernels  48.8 us (25%)
  waiting for transfers between devices  47.6 us (25%)
  local copies, waits for them, and re-layouts  6.52 us (3%)
  other arithmetic  3.91 us (2%)
    ppermute x36, starting transfers between devices, send(): return lax.ppermute(value, axis, [(i, (i + step) % n) for i in range(n)])  81.2 us
    ppermute x36, waiting for transfers between devices, send(): return lax.ppermute(value, axis, [(i, (i + step) % n) for i in range(n)])  47.6 us
    pallas_call x1, Pallas kernels, per_device(): call(forward_kernel, steps, ins, outs, 3 * unit)(*(a for *_, a in ins))  15.1 us
    pallas_call x1, Pallas kernels, per_device(): call(input_kernel, steps, ins, pieces, 2 * unit)(*(a for *_, a in ins))  9.58 us
    pallas_call x1, Pallas kernels, per_device(): call(weight_kernel, 4, ins, grads(2 * wide), 2 * unit, 1)  9.02 us
    pallas_call x1, Pallas kernels, per_device(): gu, = call(back_kernel, steps, ins, outs, unit)(*(a for *_, a in ins))  7.91 us
    pallas_call x1, Pallas kernels, per_device(): call(down_kernel, 4, ins, outs, unit, 1)(core, *(a for *_, a in ins))  7.13 us
  transfers between devices with their start and end apart: 36, of which 8 were waited for; matrix products, arithmetic and copies ran while one was open for 5% of the time, Pallas kernels for 26%

commit v1 on v0

v1 whole, which is shorter than its diff:
```python
import jax
import jax.numpy as jnp
from jax import lax
from jax.experimental import pallas as pl
from jax.experimental.pallas import tpu as pltpu
from jax.sharding import Mesh, PartitionSpec as P

EXP = 2
AXES = ("zlo", "x", "core", "zhi", "y")
SIZES = {"zlo": 4, "x": 4, "core": 2, "zhi": 2, "y": 4}
F32, BF16 = jnp.float32, jnp.bfloat16
TILE = 256


def send(value, axis, step):
    n = SIZES[axis]
    return lax.ppermute(value, axis, [(i, (i + step) % n) for i in range(n)])


def after(value, *first):
    return lax.optimization_barrier((value, first))[0]


def exchange(value, axis):
    return lax.all_to_all(value, axis, 0, 0, tiled=True)


def near_first(values):
    v = values.reshape(2, -1)
    return jnp.where(lax.axis_index("zhi") == 0, v, v[::-1]).reshape(-1, 1)


def gather_y(block):
    copies = jnp.broadcast_to(block[None], (SIZES["y"], *block.shape))
    return exchange(copies, "y").reshape(-1, block.shape[-1])


def total(pieces):
    value = pieces[0].astype(F32)
    for k in range(1, pieces.shape[0]):
        value = value + pieces[k].astype(F32)
    return value


def pick(value, axis):
    n = SIZES[axis]
    me = lax.axis_index(axis)
    own = lax.dynamic_index_in_dim(value, me, 0, keepdims=False)
    return own, [lax.dynamic_index_in_dim(value, (me + k) % n, 0, keepdims=False).astype(BF16) for k in range(1, n)]


def add(own, pieces, axis):
    for k, piece in enumerate(pieces, 1):
        own = own + send(piece, axis, k).astype(F32)
    return own


def dot(a, b, ca, cb):
    return lax.dot_general(a, b, (((ca,), (cb,)), ((), ())), preferred_element_type=F32)


def split(value, second):
    zero = jnp.zeros_like(value)
    return jnp.where(second, zero, value), jnp.where(second, value, zero)


def put_grad(value, core, own, other):
    v = value.reshape(4, 2, value.shape[0] // 8, value.shape[1])
    first = core == 0
    own[...] = jnp.where(first, v[:, 0], v[:, 1])[:, None]
    other[...] = jnp.where(first, v[:, 1], v[:, 0]).astype(BF16)[:, None]


def forward_kernel(second_ref, near, far, wg, wu, wd, hh_ref, a_ref, s_ref, out_ref):
    second = second_ref[...] > 0
    x = jnp.where(pl.program_id(0) < 2, near[...], far[...])
    xx = jnp.concatenate(split(x, second), axis=1)
    gate = dot(xx, wg[...], 1, 0)
    up = dot(xx, wu[...], 1, 0)
    sigma = 1.0 / (1.0 + jnp.exp(-gate))
    silu = gate * sigma
    a_ref[...] = up * sigma * (1.0 + gate * (1.0 - sigma))
    s_ref[...] = silu
    hidden = (silu * up).astype(BF16)
    hh = jnp.concatenate(split(hidden, second), axis=1)
    hh_ref[...] = hh
    out_ref[...] = dot(hh, wd[...], 1, 0).astype(BF16).reshape(out_ref.shape)


def down_kernel(core_ref, scale_ref, near, far, hh, dout, own, other):
    i = pl.program_id(0)
    rows = near.shape[0]

    @pl.when(i == 0)
    def _():
        for h, block in enumerate((near, far)):
            at = slice(h * rows, (h + 1) * rows)
            dout[at] = (scale_ref[at] * block[...].astype(F32)).astype(BF16)

    columns = pl.ds(pl.multiple_of(i * TILE, TILE), TILE)
    put_grad(dot(dout[:, columns], hh[...], 0, 0), core_ref[0], own, other)


def back_kernel(second_ref, dout, wd, a_ref, s_ref, gu_ref):
    second = second_ref[...] > 0
    ff = a_ref.shape[1]
    both = dot(dout[...], wd[...], 1, 1)
    back = jnp.where(second, both[:, ff:], both[:, :ff])
    gate_grad = (back * a_ref[...]).astype(BF16)
    up_grad = (back * s_ref[...]).astype(BF16)
    gu_ref[...] = jnp.concatenate(split(gate_grad, second) + split(up_grad, second), axis=1)


def weight_kernel(core_ref, near, far, gu, own, other):
    rows = near.shape[0]
    value = dot(near[...], gu[:rows], 0, 0) + dot(far[...], gu[rows:], 0, 0)
    put_grad(value, core_ref[0], own, other)


def input_kernel(gu, wg, wu, near, far):
    ff = wg.shape[2]
    i = pl.program_id(0)
    value = None
    for j, w in enumerate((wg, wu)):
        for e in range(EXP):
            c = (j * EXP + e) * ff
            term = dot(gu[:, c : c + ff], w[e], 1, 1)
            value = term if value is None else value + term
    value = value.astype(BF16).reshape(2, -1, value.shape[1])

    @pl.when(i < 2)
    def _():
        near[pl.ds(2 * i, 2)] = value

    @pl.when(i >= 2)
    def _():
        far[pl.ds(2 * i - 4, 2)] = value


def call(kernel, grid, ins, outs, flops, scalars=0):
    moved = sum(a.size * a.dtype.itemsize for *_, a in ins + outs)
    return pl.pallas_call(
        kernel,
        out_shape=[jax.ShapeDtypeStruct(a.shape, a.dtype) for *_, a in outs],
        grid_spec=pltpu.PrefetchScalarGridSpec(
            num_scalar_prefetch=scalars,
            grid=(grid,),
            in_specs=[pl.BlockSpec(b, m) for b, m, _ in ins],
            out_specs=[pl.BlockSpec(b, m) for b, m, _ in outs],
        ),
        compiler_params=pltpu.CompilerParams(vmem_limit_bytes=56 << 20),
        cost_estimate=pl.CostEstimate(flops=flops, bytes_accessed=moved, transcendentals=0),
    )


def whole(a):
    return (a.shape, lambda i, *_: (0,) * len(a.shape), a)


def tiled(a, axis, size):
    block = tuple(size if d == axis else n for d, n in enumerate(a.shape))
    return (block, lambda i, *_: tuple(i if d == axis else 0 for d in range(len(a.shape))), a)


def sds(shape, dtype):
    return jax.ShapeDtypeStruct(shape, dtype)


def per_device(tokens, cotangent, assign, prob, w_gate, w_up, w_down):
    block, width = tokens.shape
    rows = assign.shape[0]
    ff = w_gate.shape[2]
    own_rows = width // 32
    wide = EXP * ff
    unit = 2 * rows * width * ff * EXP
    second = near_first(assign)
    scale = near_first(prob)
    core = lax.axis_index("core").astype(jnp.int32).reshape(1)
    wg2, wu2 = (w.reshape(EXP * width, ff) for w in (w_gate, w_up))
    wd2 = w_down.reshape(wide, width)
    half = rows // 2

    def pieces_of(columns):
        return [tiled(sds((4, 4, own_rows, columns), t), 1, 1) for t in (F32, BF16)]

    def run(kernel, ins, outs, flops, *scalars):
        return call(kernel, 4, ins, outs, flops, len(scalars))(*scalars, *(a for *_, a in ins))

    far_tokens = send(tokens, "zhi", 1)
    x0 = gather_y(tokens)
    x1 = gather_y(far_tokens)
    far_cot = send(after(cotangent, far_tokens), "zhi", 1)
    d0 = gather_y(after(cotangent, x0))
    d1 = gather_y(after(far_cot, x1))

    tile = (TILE, width)
    ins = [tiled(second, 0, TILE)]
    ins += [(tile, lambda i: (jnp.minimum(i, 1), 0), x0), (tile, lambda i: (jnp.maximum(i - 2, 0), 0), x1)]
    ins += [whole(a) for a in (wg2, wu2, wd2)]
    outs = [tiled(sds((rows, wide), BF16), 0, TILE)]
    outs += [tiled(sds((rows, ff), F32), 0, TILE)] * 2
    outs += [((2, 1, block, width), lambda i: (i % 2, i // 2, 0, 0), sds((4, 2, block, width), BF16))]
    hh, act, silu, out = run(forward_kernel, ins, outs, 3 * unit)
    out = exchange(out, "y")

    ins = [whole(a) for a in (scale, d0, d1, hh)]
    outs = [whole(sds((rows, width), BF16)), *pieces_of(wide)]
    dout, down, other = run(down_kernel, ins, outs, unit, core)
    down_c = send(other, "core", 1)

    ins = [tiled(after(second, down), 0, TILE), tiled(dout, 0, TILE), whole(wd2), tiled(act, 0, TILE), tiled(silu, 0, TILE)]
    (gu,) = run(back_kernel, ins, [tiled(sds((rows, 2 * wide), BF16), 0, TILE)], unit)

    out = total(after(out, gu))
    far_out = send(out[1].astype(BF16), "zhi", 1)
    down = (down + after(down_c, gu).astype(F32)).astype(BF16)

    x0, x1 = after((x0, x1), down, out)
    ins = [tiled(x0, 1, TILE), tiled(x1, 1, TILE), whole(gu)]
    both, other = run(weight_kernel, ins, pieces_of(2 * wide), 2 * unit, core)
    down = exchange(down, "x")
    both_c = send(other, "core", 1)

    own_scale = lax.dynamic_slice_in_dim(scale, lax.axis_index("y") * block, block)
    output = ((out[0] + after(far_out, both).astype(F32)) * own_scale).astype(BF16)
    ins = [tiled(after(gu, both, output), 0, TILE), whole(w_gate), whole(w_up)]
    outs = [whole(sds((4, block, width), BF16))] * 2
    near, far = run(input_kernel, ins, outs, 2 * unit)

    both, pieces = pick(both + after(both_c, near).astype(F32), "x")
    far, near, both = after((far, near, both), pieces)
    both = add(both, pieces, "x")
    far = exchange(far, "y")
    near = exchange(after(near, far), "y")
    far = send(total(far).astype(BF16), "zhi", 1)
    grads = jnp.concatenate([total(down), both], axis=2).astype(BF16)
    grads = exchange(after(grads, near), "zlo")
    input_grad = (total(near) + far.astype(F32)).astype(BF16)
    grads = total(grads).reshape(own_rows, 3, EXP, ff)
    return (
        output,
        input_grad,
        grads[:, 1].swapaxes(0, 1),
        grads[:, 2].swapaxes(0, 1),
        grads[:, 0].transpose(1, 2, 0),
    )


def solution(mesh):
    fine = Mesh(mesh.devices.reshape(*SIZES.values()), AXES)
    dp, shard = ("zlo", "x", "core"), ("zhi", "y")
    return jax.shard_map(
        per_device,
        mesh=fine,
        in_specs=(
            P(AXES, None),
            P(AXES, None),
            P(dp),
            P(dp),
            P(None, None, shard),
            P(None, None, shard),
            P(None, shard, None),
        ),
        out_specs=(
            P(AXES, None),
            P(AXES, None),
            P(None, dp, shard),
            P(None, dp, shard),
            P(None, shard, dp),
        ),
        check_vma=False,
    )
```

time: 193 us -> 229 us (1.19); the launches traced: 189 us -> 228 us
  waiting for transfers between devices: 47.6 us -> 88.2 us
  starting transfers between devices: 81.2 us -> 70.7 us
  local copies, waits for them, and re-layouts: 6.52 us -> 13.3 us
  other arithmetic: 3.91 us -> 8.62 us
  Pallas kernels: 48.8 us -> 46 us
    ppermute x36 -> x9, starting transfers between devices: 81.2 us -> 27.2 us  [send(): return lax.ppermute(value, axis, [(i, (i + step) % n) for i in range(n)])]
    all_to_all x0 -> x9, starting transfers between devices: none -> 43.5 us  [exchange(): return lax.all_to_all(value, axis, 0, 0, tiled=True)]
    all_to_all x0 -> x9, waiting for transfers between devices: none -> 39.7 us  [exchange(): return lax.all_to_all(value, axis, 0, 0, tiled=True)]
    broadcast_in_dim x0 -> x4, local copies, waits for them, and re-layouts: none -> 5.83 us  [gather_y(): copies = jnp.broadcast_to(block[None], (SIZES['y'], *block.shape))]
    pallas_call x5, Pallas kernels: 48.8 us -> 46 us  [run(): call(kernel, 4, ins, outs, flops, len(scalars))]
    ppermute x36 -> x9, waiting for transfers between devices: 47.6 us -> 48.5 us  [send(): return lax.ppermute(value, axis, [(i, (i + step) % n) for i in range(n)])]
  transfers between devices with their start and end apart: 36 -> 18, of which waited for: 8 -> 12; matrix products, arithmetic and copies ran while one was open for 5% -> 6% of each run, Pallas kernels for 26% -> 17%
where the time goes in v1:
time: 229 us; the launch traced here: 228 us
  waiting for transfers between devices  88.2 us (39%)
  starting transfers between devices  70.7 us (31%)
  Pallas kernels  46 us (20%)
  local copies, waits for them, and re-layouts  13.3 us (6%)
  other arithmetic  8.62 us (4%)
    ppermute x9, waiting for transfers between devices, send(): return lax.ppermute(value, axis, [(i, (i + step) % n) for i in range(n)])  48.5 us
    pallas_call x5, Pallas kernels, run(): call(kernel, 4, ins, outs, flops, len(scalars))  46 us
    all_to_all x9, starting transfers between devices, exchange(): return lax.all_to_all(value, axis, 0, 0, tiled=True)  43.5 us
    all_to_all x9, waiting for transfers between devices, exchange(): return lax.all_to_all(value, axis, 0, 0, tiled=True)  39.7 us
    ppermute x9, starting transfers between devices, send(): return lax.ppermute(value, axis, [(i, (i + step) % n) for i in range(n)])  27.2 us
    broadcast_in_dim x4, local copies, waits for them, and re-layouts, gather_y(): copies = jnp.broadcast_to(block[None], (SIZES['y'], *block.shape))  5.83 us
  transfers between devices with their start and end apart: 18, of which 12 were waited for; matrix products, arithmetic and copies ran while one was open for 6% of the time, Pallas kernels for 17%

profile of v1, /device:TPU:6, one launch (start us, length us, event | category | flops | bytes accessed | tf_op | source)
XLA Modules:
  0.0 227.6 jit_solution(3341222689532908676)
XLA Ops:
  2.8 4.5 %all-to-all-start = ((bf16[4,128,1024]{2,1,0:T(8,128)(2,1)}), bf16[4,128,1024]{2,1,0:T(8,128)(2,1)S(1)}, u32[]{:S(2)}, u32[]{:S(2)}) async-start(bf16[4,128,1024]{2,1,0:T(8,128)(2,1)} %broadcast_in_dim.8), calls=%async_computation | async-start | bytes 2097152 | tf_op jit(solution)/shard_map/all_to_all | solution.py:25
  7.2 7.2 %collective-permute-start = (bf16[128,1024]{1,0:T(8,128)(2,1)S(1)}, bf16[128,1024]{1,0:T(8,128)(2,1)S(1)}, u32[]{:S(2)}, u32[]{:S(2)}) collective-permute-start(bf16[128,1024]{1,0:T(8,128)(2,1)S(1)} %copy-done.6), channel_id=1, source_target_pairs={{0,4},{4,0},{1,5},{5,1},{2,6},{6,2},{3,7},{7,3},{8,12},{12,8},{9,1... | collective-permute-start | bytes 786440 | tf_op jit(solution)/shard_map/ppermute | solution.py:17
  14.4 7.2 %collective-permute-done = bf16[128,1024]{1,0:T(8,128)(2,1)S(1)} collective-permute-done((bf16[128,1024]{1,0:T(8,128)(2,1)S(1)}, bf16[128,1024]{1,0:T(8,128)(2,1)S(1)}, u32[]{:S(2)}, u32[]{:S(2)}) %collective-permute-start) | collective-permute-done | bytes 262176 | tf_op jit(solution)/shard_map/ppermute | solution.py:17
  23.6 3.8 %all-to-all-start.1 = ((bf16[4,128,1024]{2,1,0:T(8,128)(2,1)}), bf16[4,128,1024]{2,1,0:T(8,128)(2,1)S(1)}, u32[]{:S(2)}, u32[]{:S(2)}) async-start(bf16[4,128,1024]{2,1,0:T(8,128)(2,1)} %broadcast_in_dim.9), calls=%async_computation.1 | async-start | bytes 2097152 | tf_op jit(solution)/shard_map/all_to_all | solution.py:25
  27.4 13.9 %all-to-all-done.1 = bf16[4,128,1024]{2,1,0:T(8,128)(2,1)S(1)} async-done(((bf16[4,128,1024]{2,1,0:T(8,128)(2,1)}), bf16[4,128,1024]{2,1,0:T(8,128)(2,1)S(1)}, u32[]{:S(2)}, u32[]{:S(2)}) %all-to-all-start.1) | async-done | bytes 1048608 | tf_op jit(solution)/shard_map/all_to_all | solution.py:25
  42.5 3.5 %all-to-all-start.3 = ((bf16[4,128,1024]{2,1,0:T(8,128)(2,1)}), bf16[4,128,1024]{2,1,0:T(8,128)(2,1)S(1)}, u32[]{:S(2)}, u32[]{:S(2)}) async-start(bf16[4,128,1024]{2,1,0:T(8,128)(2,1)} %broadcast_in_dim.10), calls=%async_computation.3 | async-start | bytes 2097152 | tf_op jit(solution)/shard_map/all_to_all | solution.py:25
  46.0 7.3 %collective-permute-start.1 = (bf16[128,1024]{1,0:T(8,128)(2,1)S(1)}, bf16[128,1024]{1,0:T(8,128)(2,1)S(1)}, u32[]{:S(2)}, u32[]{:S(2)}) collective-permute-start(bf16[128,1024]{1,0:T(8,128)(2,1)S(1)} %copy-done.7), channel_id=1, source_target_pairs={{0,4},{4,0},{1,5},{5,1},{2,6},{6,2},{3,7},{7,3},{8,12},{12,8},{9,1... | collective-permute-start | bytes 786440 | tf_op jit(solution)/shard_map/ppermute | solution.py:17
  53.6 9.2 %collective-permute-done.1 = bf16[128,1024]{1,0:T(8,128)(2,1)S(1)} collective-permute-done((bf16[128,1024]{1,0:T(8,128)(2,1)S(1)}, bf16[128,1024]{1,0:T(8,128)(2,1)S(1)}, u32[]{:S(2)}, u32[]{:S(2)}) %collective-permute-start.1) | collective-permute-done | bytes 262176 | tf_op jit(solution)/shard_map/ppermute | solution.py:17
  64.0 4.6 %all-to-all-start.4 = ((bf16[4,128,1024]{2,1,0:T(8,128)(2,1)}), bf16[4,128,1024]{2,1,0:T(8,128)(2,1)S(1)}, u32[]{:S(2)}, u32[]{:S(2)}) async-start(bf16[4,128,1024]{2,1,0:T(8,128)(2,1)} %broadcast_in_dim.11), calls=%async_computation.4 | async-start | bytes 2097152 | tf_op jit(solution)/shard_map/all_to_all | solution.py:25
  70.6 12.6 %shard_map.110 = (bf16[1024,1024]{1,0:T(8,128)(2,1)}, f32[1024,512]{1,0:T(8,128)}, f32[1024,512]{1,0:T(8,128)}, bf16[4,2,128,1024]{3,2,1,0:T(8,128)(2,1)}) custom-call(s32[1024,1]{1,0:T(8,128)} %copy.15.second_ref, bf16[512,1024]{1,0:T(8,128)(2,1)} %bitcast.61, bf16[512,1024]{1,0:T(8,128)(2,1)} %bitcast.63, bf16[2048,512]{1,0:T(8,128)(2,1)} %bitcast.72, ...), custom_call_target="tpu_custom_call" | custom-call | flops 6442450944 | bytes 16781312 | tf_op jit(solution)/shard_map/pallas_call | solution.py:187
  84.3 7.1 %shard_map.111 = (bf16[1024,1024]{1,0:T(8,128)(2,1)}, f32[4,4,32,1024]{3,2,1,0:T(8,128)}, bf16[4,4,32,1024]{3,2,1,0:T(8,128)(2,1)}) custom-call(s32[1]{0:T(128)} %bitcast.5.core_ref, f32[1024,1]{1,0:T(8,128)} %copy.16.scale_ref, bf16[512,1024]{1,0:T(8,128)(2,1)} %bitcast.65, bf16[512,1024]{1,0:T(8,128)(2,1)} %bitcast.66, bf16[1024,1024]{1,0:T(8,128)(2,1)} %get-tuple-element.36.hh), custom_call_target="tpu_custom_call" | custom-call | flops 2147483648 | bytes 9441280 | tf_op jit(solution)/shard_map/pallas_call | solution.py:187
  91.4 4.8 %all-to-all-start.2 = ((bf16[4,2,128,1024]{3,2,1,0:T(8,128)(2,1)}), bf16[4,2,128,1024]{3,2,1,0:T(8,128)(2,1)S(1)}, u32[]{:S(2)}, u32[]{:S(2)}) async-start(bf16[4,2,128,1024]{3,2,1,0:T(8,128)(2,1)} %get-tuple-element.32), calls=%async_computation.2 | async-start | bytes 4194304 | tf_op jit(solution)/shard_map/all_to_all | solution.py:25
  97.2 8.0 %shard_map.112.gu = bf16[1024,2048]{1,0:T(8,128)(2,1)} custom-call(s32[1024,1]{1,0:T(8,128)} %copy.17.second_ref, bf16[1024,1024]{1,0:T(8,128)(2,1)} %get-tuple-element.39.dout, bf16[1024,1024]{1,0:T(8,128)(2,1)} %bitcast.60, f32[1024,512]{1,0:T(8,128)} %get-tuple-element.40.a_ref, f32[1024,512]{1,0:T(8,128)} %get-tuple-element.41.s_ref), custom_call_target="tpu_custom_call" | custom-call | flops 2147483648 | bytes 12587008 | tf_op jit(solution)/shard_map/pallas_call | solution.py:187
  106.5 8.9 %shard_map.113 = (f32[4,4,32,2048]{3,2,1,0:T(8,128)}, bf16[4,4,32,2048]{3,2,1,0:T(8,128)(2,1)}) custom-call(s32[1]{0:T(128)} %bitcast.5.core_ref, bf16[512,1024]{1,0:T(8,128)(2,1)} %bitcast.62, bf16[512,1024]{1,0:T(8,128)(2,1)} %bitcast.64, bf16[1024,2048]{1,0:T(8,128)(2,1)} %shard_map.112.gu), custom_call_target="tpu_custom_call" | custom-call | flops 4294967296 | bytes 12582912 | tf_op jit(solution)/shard_map/pallas_call | solution.py:187
  115.6 7.6 %all-to-all-done.2 = bf16[4,2,128,1024]{3,2,1,0:T(8,128)(2,1)S(1)} async-done(((bf16[4,2,128,1024]{3,2,1,0:T(8,128)(2,1)}), bf16[4,2,128,1024]{3,2,1,0:T(8,128)(2,1)S(1)}, u32[]{:S(2)}, u32[]{:S(2)}) %all-to-all-start.2) | async-done | bytes 2097184 | tf_op jit(solution)/shard_map/all_to_all | solution.py:25
  123.5 6.5 %collective-permute-start.2 = (bf16[128,1024]{1,0:T(8,128)(2,1)S(1)}, bf16[128,1024]{1,0:T(8,128)(2,1)S(1)}, u32[]{:S(2)}, u32[]{:S(2)}) collective-permute-start(bf16[128,1024]{1,0:T(8,128)(2,1)S(1)} %fusion.9), channel_id=1, source_target_pairs={{0,4},{4,0},{1,5},{5,1},{2,6},{6,2},{3,7},{7,3},{8,12},{12,8},{9,1... | collective-permute-start | bytes 786440 | tf_op jit(solution)/shard_map/ppermute | solution.py:17
  130.0 4.8 %all-to-all-start.7 = ((bf16[4,4,32,1024]{3,2,1,0:T(8,128)(2,1)}), bf16[4,4,32,1024]{3,2,1,0:T(8,128)(2,1)S(1)}, u32[]{:S(2)}, u32[]{:S(2)}) async-start(bf16[4,4,32,1024]{3,2,1,0:T(8,128)(2,1)} %add_convert_fusion), calls=%async_computation.7 | async-start | bytes 2097152 | tf_op jit(solution)/shard_map/all_to_all | solution.py:25
  138.2 9.4 %shard_map.114 = (bf16[4,128,1024]{2,1,0:T(8,128)(2,1)}, bf16[4,128,1024]{2,1,0:T(8,128)(2,1)}) custom-call(bf16[1024,2048]{1,0:T(8,128)(2,1)} %shard_map.112.gu, bf16[2,1024,512]{2,1,0:T(8,128)(2,1)} %wg.1, bf16[2,1024,512]{2,1,0:T(8,128)(2,1)} %wu.1), custom_call_target="tpu_custom_call" | custom-call | flops 4294967296 | bytes 10485760 | tf_op jit(solution)/shard_map/pallas_call | solution.py:187
  151.1 3.5 %all-to-all-start.5 = ((bf16[4,128,1024]{2,1,0:T(8,128)(2,1)}), bf16[4,128,1024]{2,1,0:T(8,128)(2,1)S(1)}, u32[]{:S(2)}, u32[]{:S(2)}) async-start(bf16[4,128,1024]{2,1,0:T(8,128)(2,1)} %get-tuple-element.55), calls=%async_computation.5 | async-start | bytes 2097152 | tf_op jit(solution)/shard_map/all_to_all | solution.py:25
  159.1 9.7 %all-to-all-done.5 = bf16[4,128,1024]{2,1,0:T(8,128)(2,1)S(1)} async-done(((bf16[4,128,1024]{2,1,0:T(8,128)(2,1)}), bf16[4,128,1024]{2,1,0:T(8,128)(2,1)S(1)}, u32[]{:S(2)}, u32[]{:S(2)}) %all-to-all-start.5) | async-done | bytes 1048608 | tf_op jit(solution)/shard_map/all_to_all | solution.py:25
  172.3 7.8 %collective-permute-done.8 = bf16[4,32,2048]{2,1,0:T(8,128)(2,1)} collective-permute-done((bf16[4,32,2048]{2,1,0:T(8,128)(2,1)}, bf16[4,32,2048]{2,1,0:T(8,128)(2,1)}, u32[]{:S(2)}, u32[]{:S(2)}) %collective-permute-start.8) | collective-permute-done | bytes 524320 | tf_op jit(solution)/shard_map/ppermute | solution.py:17
  185.5 10.6 %all-to-all-start.8 = ((bf16[4,32,3072]{2,1,0:T(8,128)(2,1)}), bf16[4,32,3072]{2,1,0:T(8,128)(2,1)S(1)}, u32[]{:S(2)}, u32[]{:S(2)}) async-start(bf16[4,32,3072]{2,1,0:T(8,128)(2,1)} %pad_maximum_fusion), calls=%async_computation.8 | async-start | bytes 1572864 | tf_op jit(solution)/shard_map/all_to_all | solution.py:25
  198.0 21.2 %collective-permute-done.5 = bf16[128,1024]{1,0:T(8,128)(2,1)S(1)} collective-permute-done((bf16[128,1024]{1,0:T(8,128)(2,1)S(1)}, bf16[128,1024]{1,0:T(8,128)(2,1)S(1)}, u32[]{:S(2)}, u32[]{:S(2)}) %collective-permute-start.5) | collective-permute-done | bytes 262176 | tf_op jit(solution)/shard_map/ppermute | solution.py:17
  220.1 5.6 %all-to-all-done.8 = bf16[4,32,3072]{2,1,0:T(8,128)(2,1)S(1)} async-done(((bf16[4,32,3072]{2,1,0:T(8,128)(2,1)}), bf16[4,32,3072]{2,1,0:T(8,128)(2,1)S(1)}, u32[]{:S(2)}, u32[]{:S(2)}) %all-to-all-start.8) | async-done | bytes 786464 | tf_op jit(solution)/shard_map/all_to_all | solution.py:25
  (70 shorter events, 37.8 us)
Async XLA Ops:
  2.8 19.6 %all-to-all-start = ((bf16[4,128,1024]{2,1,0:T(8,128)(2,1)}), bf16[4,128,1024]{2,1,0:T(8,128)(2,1)S(1)}, u32[]{:S(2)}, u32[]{:S(2)}) async-start(bf16[4,128,1024]{2,1,0:T(8,128)(2,1)} %broadcast_in_dim.8), calls=%async_computation | async-start | bytes 2097152 | tf_op jit(solution)/shard_map/all_to_all | solution.py:25
  7.2 34.0 %copy-start.7 = (bf16[128,1024]{1,0:T(8,128)(2,1)S(1)}, bf16[128,1024]{1,0:T(8,128)(2,1)}, u32[]{:S(2)}) copy-start(bf16[128,1024]{1,0:T(8,128)(2,1)} %param.8) | copy-start | bytes 786436
  7.2 14.3 %collective-permute-start = (bf16[128,1024]{1,0:T(8,128)(2,1)S(1)}, bf16[128,1024]{1,0:T(8,128)(2,1)S(1)}, u32[]{:S(2)}, u32[]{:S(2)}) collective-permute-start(bf16[128,1024]{1,0:T(8,128)(2,1)S(1)} %copy-done.6), channel_id=1, source_target_pairs={{0,4},{4,0},{1,5},{5,1},{2,6},{6,2},{3,7},{7,3},{8,12},{12,8},{9,1... | collective-permute-start | bytes 786440 | tf_op jit(solution)/shard_map/ppermute | solution.py:17
  22.3 20.2 %copy-start.2 = (bf16[4,128,1024]{2,1,0:T(8,128)(2,1)}, bf16[4,128,1024]{2,1,0:T(8,128)(2,1)S(1)}, u32[]{:S(2)}) copy-start(bf16[4,128,1024]{2,1,0:T(8,128)(2,1)S(1)} %all-to-all-done) | copy-start | bytes 3145732
  23.6 17.7 %all-to-all-start.1 = ((bf16[4,128,1024]{2,1,0:T(8,128)(2,1)}), bf16[4,128,1024]{2,1,0:T(8,128)(2,1)S(1)}, u32[]{:S(2)}, u32[]{:S(2)}) async-start(bf16[4,128,1024]{2,1,0:T(8,128)(2,1)} %broadcast_in_dim.9), calls=%async_computation.1 | async-start | bytes 2097152 | tf_op jit(solution)/shard_map/all_to_all | solution.py:25
  27.4 25.9 %copy-start.8 = (s32[1024]{0:T(1024)S(1)}, s32[1024]{0:T(1024)}, u32[]{:S(2)}) copy-start(s32[1024]{0:T(1024)} %param.9) | copy-start | bytes 12292
  27.4 25.9 %copy-start.9 = (f32[1024]{0:T(1024)S(1)}, f32[1024]{0:T(1024)}, u32[]{:S(2)}) copy-start(f32[1024]{0:T(1024)} %param.10) | copy-start | bytes 12292
  41.3 22.8 %copy-start.3 = (bf16[4,128,1024]{2,1,0:T(8,128)(2,1)}, bf16[4,128,1024]{2,1,0:T(8,128)(2,1)S(1)}, u32[]{:S(2)}) copy-start(bf16[4,128,1024]{2,1,0:T(8,128)(2,1)S(1)} %all-to-all-done.1) | copy-start | bytes 3145732
  42.5 20.3 %all-to-all-start.3 = ((bf16[4,128,1024]{2,1,0:T(8,128)(2,1)}), bf16[4,128,1024]{2,1,0:T(8,128)(2,1)S(1)}, u32[]{:S(2)}, u32[]{:S(2)}) async-start(bf16[4,128,1024]{2,1,0:T(8,128)(2,1)} %broadcast_in_dim.10), calls=%async_computation.3 | async-start | bytes 2097152 | tf_op jit(solution)/shard_map/all_to_all | solution.py:25
  46.0 16.8 %collective-permute-start.1 = (bf16[128,1024]{1,0:T(8,128)(2,1)S(1)}, bf16[128,1024]{1,0:T(8,128)(2,1)S(1)}, u32[]{:S(2)}, u32[]{:S(2)}) collective-permute-start(bf16[128,1024]{1,0:T(8,128)(2,1)S(1)} %copy-done.7), channel_id=1, source_target_pairs={{0,4},{4,0},{1,5},{5,1},{2,6},{6,2},{3,7},{7,3},{8,12},{12,8},{9,1... | collective-permute-start | bytes 786440 | tf_op jit(solution)/shard_map/ppermute | solution.py:17
  64.0 19.2 %all-to-all-start.4 = ((bf16[4,128,1024]{2,1,0:T(8,128)(2,1)}), bf16[4,128,1024]{2,1,0:T(8,128)(2,1)S(1)}, u32[]{:S(2)}, u32[]{:S(2)}) async-start(bf16[4,128,1024]{2,1,0:T(8,128)(2,1)} %broadcast_in_dim.11), calls=%async_computation.4 | async-start | bytes 2097152 | tf_op jit(solution)/shard_map/all_to_all | solution.py:25
  91.4 13.8 %collective-permute-start.3 = (bf16[4,4,32,1024]{3,2,1,0:T(8,128)(2,1)}, bf16[4,4,32,1024]{3,2,1,0:T(8,128)(2,1)S(1)}, u32[]{:S(2)}, u32[]{:S(2)}) collective-permute-start(bf16[4,4,32,1024]{3,2,1,0:T(8,128)(2,1)} %get-tuple-element.43), channel_id=1, source_target_pairs={{0,8},{8,0},{1,9},{9,1},{2,10},{10,2},{3,11},{11,3},{4,12},{12,4},... | collective-permute-start | bytes 3145736 | tf_op jit(solution)/shard_map/ppermute | solution.py:17
  91.4 31.8 %all-to-all-start.2 = ((bf16[4,2,128,1024]{3,2,1,0:T(8,128)(2,1)}), bf16[4,2,128,1024]{3,2,1,0:T(8,128)(2,1)S(1)}, u32[]{:S(2)}, u32[]{:S(2)}) async-start(bf16[4,2,128,1024]{3,2,1,0:T(8,128)(2,1)} %get-tuple-element.32), calls=%async_computation.2 | async-start | bytes 4194304 | tf_op jit(solution)/shard_map/all_to_all | solution.py:25
  115.4 32.3 %collective-permute-start.4 = (bf16[4,4,32,2048]{3,2,1,0:T(8,128)(2,1)}, bf16[4,4,32,2048]{3,2,1,0:T(8,128)(2,1)}, u32[]{:S(2)}, u32[]{:S(2)}) collective-permute-start(bf16[4,4,32,2048]{3,2,1,0:T(8,128)(2,1)} %get-tuple-element.52), channel_id=1, source_target_pairs={{0,8},{8,0},{1,9},{9,1},{2,10},{10,2},{3,11},{11,3},{4,12},{12,4},... | collective-permute-start | bytes 6291464 | tf_op jit(solution)/shard_map/ppermute | solution.py:17
  123.5 13.9 %collective-permute-start.2 = (bf16[128,1024]{1,0:T(8,128)(2,1)S(1)}, bf16[128,1024]{1,0:T(8,128)(2,1)S(1)}, u32[]{:S(2)}, u32[]{:S(2)}) collective-permute-start(bf16[128,1024]{1,0:T(8,128)(2,1)S(1)} %fusion.9), channel_id=1, source_target_pairs={{0,4},{4,0},{1,5},{5,1},{2,6},{6,2},{3,7},{7,3},{8,12},{12,8},{9,1... | collective-permute-start | bytes 786440 | tf_op jit(solution)/shard_map/ppermute | solution.py:17
  130.0 21.1 %all-to-all-start.7 = ((bf16[4,4,32,1024]{3,2,1,0:T(8,128)(2,1)}), bf16[4,4,32,1024]{3,2,1,0:T(8,128)(2,1)S(1)}, u32[]{:S(2)}, u32[]{:S(2)}) async-start(bf16[4,4,32,1024]{3,2,1,0:T(8,128)(2,1)} %add_convert_fusion), calls=%async_computation.7 | async-start | bytes 2097152 | tf_op jit(solution)/shard_map/all_to_all | solution.py:25
  138.2 9.4 %copy-start = (f32[4,4,32,2048]{3,2,1,0:T(8,128)S(1)}, f32[4,4,32,2048]{3,2,1,0:T(8,128)}, u32[]{:S(2)}) copy-start(f32[4,4,32,2048]{3,2,1,0:T(8,128)} %get-tuple-element.47) | copy-start | bytes 12582916
  151.1 17.7 %all-to-all-start.5 = ((bf16[4,128,1024]{2,1,0:T(8,128)(2,1)}), bf16[4,128,1024]{2,1,0:T(8,128)(2,1)S(1)}, u32[]{:S(2)}, u32[]{:S(2)}) async-start(bf16[4,128,1024]{2,1,0:T(8,128)(2,1)} %get-tuple-element.55), calls=%async_computation.5 | async-start | bytes 2097152 | tf_op jit(solution)/shard_map/all_to_all | solution.py:25
  154.7 25.5 %collective-permute-start.8 = (bf16[4,32,2048]{2,1,0:T(8,128)(2,1)}, bf16[4,32,2048]{2,1,0:T(8,128)(2,1)}, u32[]{:S(2)}, u32[]{:S(2)}) collective-permute-start(bf16[4,32,2048]{2,1,0:T(8,128)(2,1)} %get-tuple-element.59), channel_id=1, source_target_pairs={{0,48},{16,0},{32,16},{48,32},{1,49},{17,1},{33,17},{49,33},{2,50}... | collective-permute-start | bytes 1572872 | tf_op jit(solution)/shard_map/ppermute | solution.py:17
  155.7 24.4 %collective-permute-start.7 = (bf16[4,32,2048]{2,1,0:T(8,128)(2,1)}, bf16[4,32,2048]{2,1,0:T(8,128)(2,1)}, u32[]{:S(2)}, u32[]{:S(2)}) collective-permute-start(bf16[4,32,2048]{2,1,0:T(8,128)(2,1)} %get-tuple-element.60), channel_id=1, source_target_pairs={{0,32},{16,48},{32,0},{48,16},{1,33},{17,49},{33,1},{49,17},{2,34}... | collective-permute-start | bytes 1572872 | tf_op jit(solution)/shard_map/ppermute | solution.py:17
  156.9 23.9 %collective-permute-start.6 = (bf16[4,32,2048]{2,1,0:T(8,128)(2,1)}, bf16[4,32,2048]{2,1,0:T(8,128)(2,1)}, u32[]{:S(2)}, u32[]{:S(2)}) collective-permute-start(bf16[4,32,2048]{2,1,0:T(8,128)(2,1)} %get-tuple-element.61), channel_id=1, source_target_pairs={{0,16},{16,32},{32,48},{48,0},{1,17},{17,33},{33,49},{49,1},{2,18}... | collective-permute-start | bytes 1572872 | tf_op jit(solution)/shard_map/ppermute | solution.py:17
  168.8 16.7 %all-to-all-start.6 = ((bf16[4,128,1024]{2,1,0:T(8,128)(2,1)}), bf16[4,128,1024]{2,1,0:T(8,128)(2,1)S(1)}, u32[]{:S(2)}, u32[]{:S(2)}) async-start(bf16[4,128,1024]{2,1,0:T(8,128)(2,1)} %get-tuple-element.56), calls=%async_computation.6 | async-start | bytes 2097152 | tf_op jit(solution)/shard_map/all_to_all | solution.py:25
  185.5 40.2 %all-to-all-start.8 = ((bf16[4,32,3072]{2,1,0:T(8,128)(2,1)}), bf16[4,32,3072]{2,1,0:T(8,128)(2,1)S(1)}, u32[]{:S(2)}, u32[]{:S(2)}) async-start(bf16[4,32,3072]{2,1,0:T(8,128)(2,1)} %pad_maximum_fusion), calls=%async_computation.8 | async-start | bytes 1572864 | tf_op jit(solution)/shard_map/all_to_all | solution.py:25
  196.3 22.9 %collective-permute-start.5 = (bf16[128,1024]{1,0:T(8,128)(2,1)S(1)}, bf16[128,1024]{1,0:T(8,128)(2,1)S(1)}, u32[]{:S(2)}, u32[]{:S(2)}) collective-permute-start(bf16[128,1024]{1,0:T(8,128)(2,1)S(1)} %fusion.7), channel_id=1, source_target_pairs={{0,4},{4,0},{1,5},{5,1},{2,6},{6,2},{3,7},{7,3},{8,12},{12,8},{9,1... | collective-permute-start | bytes 786440 | tf_op jit(solution)/shard_map/ppermute | solution.py:17
  (4 other events, 23.4 us)

commit v2 on v1

--- a/solution.py
+++ b/solution.py
@@ -17,8 +17,8 @@
     return lax.ppermute(value, axis, [(i, (i + step) % n) for i in range(n)])
 
 
-def after(value, *first):
-    return lax.optimization_barrier((value, first))[0]
+def tie(*values):
+    return lax.optimization_barrier(values)
 
 
 def exchange(value, axis):
@@ -49,9 +49,13 @@
     return own, [lax.dynamic_index_in_dim(value, (me + k) % n, 0, keepdims=False).astype(BF16) for k in range(1, n)]
 
 
-def add(own, pieces, axis):
-    for k, piece in enumerate(pieces, 1):
-        own = own + send(piece, axis, k).astype(F32)
+def sends(pieces, axis):
+    return [send(piece, axis, k) for k, piece in enumerate(pieces, 1)]
+
+
+def add(own, pieces):
+    for piece in pieces:
+        own = own + piece.astype(F32)
     return own
 
 
@@ -67,7 +71,7 @@
 def put_grad(value, core, own, other):
     v = value.reshape(4, 2, value.shape[0] // 8, value.shape[1])
     first = core == 0
-    own[...] = jnp.where(first, v[:, 0], v[:, 1])[:, None]
+    own[...] = jnp.where(first, v[:, 0], v[:, 1]).astype(BF16)[:, None]
     other[...] = jnp.where(first, v[:, 1], v[:, 0]).astype(BF16)[:, None]
 
 
@@ -87,15 +91,16 @@
     out_ref[...] = dot(hh, wd[...], 1, 0).astype(BF16).reshape(out_ref.shape)
 
 
-def down_kernel(core_ref, scale_ref, near, far, hh, dout, own, other):
+def down_kernel(core_ref, scale_ref, cots, hh, dout, own, other):
     i = pl.program_id(0)
-    rows = near.shape[0]
+    ny, nz, rows, _ = cots.shape
 
     @pl.when(i == 0)
     def _():
-        for h, block in enumerate((near, far)):
-            at = slice(h * rows, (h + 1) * rows)
-            dout[at] = (scale_ref[at] * block[...].astype(F32)).astype(BF16)
+        for y in range(ny):
+            for z in range(nz):
+                at = slice((z * ny + y) * rows, (z * ny + y + 1) * rows)
+                dout[at] = (scale_ref[at] * cots[y, z].astype(F32)).astype(BF16)
 
     columns = pl.ds(pl.multiple_of(i * TILE, TILE), TILE)
     put_grad(dot(dout[:, columns], hh[...], 0, 0), core_ref[0], own, other)
@@ -148,7 +153,7 @@
             in_specs=[pl.BlockSpec(b, m) for b, m, _ in ins],
             out_specs=[pl.BlockSpec(b, m) for b, m, _ in outs],
         ),
-        compiler_params=pltpu.CompilerParams(vmem_limit_bytes=56 << 20),
+        compiler_params=pltpu.CompilerParams(vmem_limit_bytes=26 << 20),
         cost_estimate=pl.CostEstimate(flops=flops, bytes_accessed=moved, transcendentals=0),
     )
 
@@ -181,17 +186,18 @@
     half = rows // 2
 
     def pieces_of(columns):
-        return [tiled(sds((4, 4, own_rows, columns), t), 1, 1) for t in (F32, BF16)]
+        return [tiled(sds((4, 4, own_rows, columns), BF16), 1, 1)] * 2
 
     def run(kernel, ins, outs, flops, *scalars):
         return call(kernel, 4, ins, outs, flops, len(scalars))(*scalars, *(a for *_, a in ins))
 
     far_tokens = send(tokens, "zhi", 1)
     x0 = gather_y(tokens)
+    far_tokens, cotangent = tie(far_tokens, cotangent)
     x1 = gather_y(far_tokens)
-    far_cot = send(after(cotangent, far_tokens), "zhi", 1)
-    d0 = gather_y(after(cotangent, x0))
-    d1 = gather_y(after(far_cot, x1))
+    far_cot = send(cotangent, "zhi", 1)
+    both_cot = jnp.stack([cotangent, far_cot])
+    cots = exchange(jnp.broadcast_to(both_cot[None], (SIZES["y"], *both_cot.shape)), "y")
 
     tile = (TILE, width)
     ins = [tiled(second, 0, TILE)]
@@ -203,39 +209,45 @@
     hh, act, silu, out = run(forward_kernel, ins, outs, 3 * unit)
     out = exchange(out, "y")
 
-    ins = [whole(a) for a in (scale, d0, d1, hh)]
+    ins = [whole(a) for a in (scale, cots, hh)]
     outs = [whole(sds((rows, width), BF16)), *pieces_of(wide)]
     dout, down, other = run(down_kernel, ins, outs, unit, core)
     down_c = send(other, "core", 1)
 
-    ins = [tiled(after(second, down), 0, TILE), tiled(dout, 0, TILE), whole(wd2), tiled(act, 0, TILE), tiled(silu, 0, TILE)]
+    ins = [tiled(second, 0, TILE), tiled(dout, 0, TILE), whole(wd2), tiled(act, 0, TILE), tiled(silu, 0, TILE)]
     (gu,) = run(back_kernel, ins, [tiled(sds((rows, 2 * wide), BF16), 0, TILE)], unit)
 
-    out = total(after(out, gu))
-    far_out = send(out[1].astype(BF16), "zhi", 1)
-    down = (down + after(down_c, gu).astype(F32)).astype(BF16)
-
-    x0, x1 = after((x0, x1), down, out)
+    gu, down_c = tie(gu, down_c)
+    down, down_x = pick(add(down.astype(F32), [down_c]), "x")
+    gu, down, down_x = tie(gu, down, down_x)
+    down_x = sends(down_x, "x")
     ins = [tiled(x0, 1, TILE), tiled(x1, 1, TILE), whole(gu)]
     both, other = run(weight_kernel, ins, pieces_of(2 * wide), 2 * unit, core)
-    down = exchange(down, "x")
     both_c = send(other, "core", 1)
-
-    own_scale = lax.dynamic_slice_in_dim(scale, lax.axis_index("y") * block, block)
-    output = ((out[0] + after(far_out, both).astype(F32)) * own_scale).astype(BF16)
-    ins = [tiled(after(gu, both, output), 0, TILE), whole(w_gate), whole(w_up)]
+    out, both = tie(out, both)
+    out = total(out)
+    out, gu, both = tie(out, gu, both)
+    far_out = send(out[1].astype(BF16), "zhi", 1)
+
+    ins = [tiled(gu, 0, TILE), whole(w_gate), whole(w_up)]
     outs = [whole(sds((4, block, width), BF16))] * 2
     near, far = run(input_kernel, ins, outs, 2 * unit)
 
-    both, pieces = pick(both + after(both_c, near).astype(F32), "x")
-    far, near, both = after((far, near, both), pieces)
-    both = add(both, pieces, "x")
+    near, far, both_c, down_x, far_out = tie(near, far, both_c, down_x, far_out)
+    both, both_x = pick(add(both.astype(F32), [both_c]), "x")
+    far, near, both, both_x = tie(far, near, both, both_x)
+    both_x = sends(both_x, "x")
     far = exchange(far, "y")
-    near = exchange(after(near, far), "y")
+    near, far = tie(near, far)
+    near = exchange(near, "y")
     far = send(total(far).astype(BF16), "zhi", 1)
-    grads = jnp.concatenate([total(down), both], axis=2).astype(BF16)
-    grads = exchange(after(grads, near), "zlo")
-    input_grad = (total(near) + far.astype(F32)).astype(BF16)
+    own_scale = lax.dynamic_slice_in_dim(scale, lax.axis_index("y") * block, block)
+    output = (add(out[0], [far_out]) * own_scale).astype(BF16)
+    down = add(down, down_x)
+    grads = jnp.concatenate([down, add(both, both_x)], axis=2).astype(BF16)
+    grads, near, far = tie(grads, near, far)
+    grads = exchange(grads, "zlo")
+    input_grad = add(total(near), [far]).astype(BF16)
     grads = total(grads).reshape(own_rows, 3, EXP, ff)
     return (
         output,

time: 229 us -> 217 us (0.948)
  local copies, waits for them, and re-layouts: 13.3 us -> 36.7 us
  waiting for transfers between devices: 88.2 us -> 68.4 us
  Pallas kernels: 46 us -> 30.8 us
  starting transfers between devices: 70.7 us -> 65.6 us
  other arithmetic: 8.62 us -> 13.7 us
    unnamed x23 -> x70, local copies, waits for them, and re-layouts: 1.71 us -> 28.5 us
    pallas_call x5, Pallas kernels: 46 us -> 30.8 us  [run(): call(kernel, 4, ins, outs, flops, len(scalars))]
    ppermute x9 -> x12, waiting for transfers between devices: 48.5 us -> 34.2 us  [send(): return lax.ppermute(value, axis, [(i, (i + step) % n) for i in range(n)])]
    all_to_all x9 -> x7, starting transfers between devices: 43.5 us -> 35.4 us  [exchange(): return lax.all_to_all(value, axis, 0, 0, tiled=True)]
    all_to_all x9 -> x7, waiting for transfers between devices: 39.7 us -> 34.2 us  [exchange(): return lax.all_to_all(value, axis, 0, 0, tiled=True)]
    ppermute x9 -> x12, starting transfers between devices: 27.2 us -> 30.2 us  [send(): return lax.ppermute(value, axis, [(i, (i + step) % n) for i in range(n)])]
    add x1 -> x2, other arithmetic: 2.18 us -> 4.86 us  [add(): own = own + piece.astype(F32)]
    broadcast_in_dim x4 -> x2, local copies, waits for them, and re-layouts: 5.83 us -> 3.46 us  [gather_y(): copies = jnp.broadcast_to(block[None], (SIZES['y'], *block.shape))]
  transfers between devices with their start and end apart: 18 -> 19, of which waited for: 12 -> 10; matrix products, arithmetic and copies ran while one was open for 6% -> 6% of each run, Pallas kernels for 17% -> 12%
where the time goes in v2:
time: 217 us; the launch traced here: 216 us
  waiting for transfers between devices  68.4 us (32%)
  starting transfers between devices  65.6 us (30%)
  local copies, waits for them, and re-layouts  36.7 us (17%)
  Pallas kernels  30.8 us (14%)
  other arithmetic  13.7 us (6%)
    all_to_all x7, starting transfers between devices, exchange(): return lax.all_to_all(value, axis, 0, 0, tiled=True)  35.4 us
    ppermute x12, waiting for transfers between devices, send(): return lax.ppermute(value, axis, [(i, (i + step) % n) for i in range(n)])  34.2 us
    all_to_all x7, waiting for transfers between devices, exchange(): return lax.all_to_all(value, axis, 0, 0, tiled=True)  34.2 us
    pallas_call x5, Pallas kernels, run(): call(kernel, 4, ins, outs, flops, len(scalars))  30.8 us
    ppermute x12, starting transfers between devices, send(): return lax.ppermute(value, axis, [(i, (i + step) % n) for i in range(n)])  30.2 us
    unnamed x70, local copies, waits for them, and re-layouts  28.5 us
    add x2, other arithmetic, add(): own = own + piece.astype(F32)  4.86 us
  transfers between devices with their start and end apart: 19, of which 10 were waited for; matrix products, arithmetic and copies ran while one was open for 6% of the time, Pallas kernels for 12%

profile of v2, /device:TPU:6, one launch (start us, length us, event | category | flops | bytes accessed | tf_op | source)
XLA Modules:
  0.0 216.2 jit_solution(14700553792007811398)
XLA Ops:
  2.8 4.5 %all-to-all-start = ((bf16[4,128,1024]{2,1,0:T(8,128)(2,1)}), bf16[4,128,1024]{2,1,0:T(8,128)(2,1)S(1)}, u32[]{:S(2)}, u32[]{:S(2)}) async-start(bf16[4,128,1024]{2,1,0:T(8,128)(2,1)} %broadcast_in_dim.6), calls=%async_computation | async-start | bytes 2097152 | tf_op jit(solution)/shard_map/all_to_all | solution.py:25
  7.3 7.2 %collective-permute-start = (bf16[128,1024]{1,0:T(8,128)(2,1)S(1)}, bf16[128,1024]{1,0:T(8,128)(2,1)S(1)}, u32[]{:S(2)}, u32[]{:S(2)}) collective-permute-start(bf16[128,1024]{1,0:T(8,128)(2,1)S(1)} %copy-done.26), channel_id=1, source_target_pairs={{0,4},{4,0},{1,5},{5,1},{2,6},{6,2},{3,7},{7,3},{8,12},{12,8},{9,1... | collective-permute-start | bytes 786440 | tf_op jit(solution)/shard_map/ppermute | solution.py:17
  14.5 7.2 %collective-permute-done = bf16[128,1024]{1,0:T(8,128)(2,1)S(1)} collective-permute-done((bf16[128,1024]{1,0:T(8,128)(2,1)S(1)}, bf16[128,1024]{1,0:T(8,128)(2,1)S(1)}, u32[]{:S(2)}, u32[]{:S(2)}) %collective-permute-start) | collective-permute-done | bytes 262176 | tf_op jit(solution)/shard_map/ppermute | solution.py:17
  23.7 3.8 %all-to-all-start.1 = ((bf16[4,128,1024]{2,1,0:T(8,128)(2,1)}), bf16[4,128,1024]{2,1,0:T(8,128)(2,1)S(1)}, u32[]{:S(2)}, u32[]{:S(2)}) async-start(bf16[4,128,1024]{2,1,0:T(8,128)(2,1)} %broadcast_in_dim.7), calls=%async_computation.1 | async-start | bytes 2097152 | tf_op jit(solution)/shard_map/all_to_all | solution.py:25
  27.4 9.5 %collective-permute-start.1 = (bf16[128,1024]{1,0:T(8,128)(2,1)S(1)}, bf16[128,1024]{1,0:T(8,128)(2,1)S(1)}, u32[]{:S(2)}, u32[]{:S(2)}) collective-permute-start(bf16[128,1024]{1,0:T(8,128)(2,1)S(1)} %copy-done.27), channel_id=1, source_target_pairs={{0,4},{4,0},{1,5},{5,1},{2,6},{6,2},{3,7},{7,3},{8,12},{12,8},{9,1... | collective-permute-start | bytes 786440 | tf_op jit(solution)/shard_map/ppermute | solution.py:17
  36.9 7.8 %collective-permute-done.1 = bf16[128,1024]{1,0:T(8,128)(2,1)S(1)} collective-permute-done((bf16[128,1024]{1,0:T(8,128)(2,1)S(1)}, bf16[128,1024]{1,0:T(8,128)(2,1)S(1)}, u32[]{:S(2)}, u32[]{:S(2)}) %collective-permute-start.1) | collective-permute-done | bytes 262176 | tf_op jit(solution)/shard_map/ppermute | solution.py:17
  47.4 4.6 %all-to-all-start.3 = ((bf16[4,2,128,1024]{3,2,1,0:T(8,128)(2,1)}), bf16[4,2,128,1024]{3,2,1,0:T(8,128)(2,1)}, u32[]{:S(2)}, u32[]{:S(2)}) async-start(bf16[4,2,128,1024]{3,2,1,0:T(8,128)(2,1)} %broadcast_in_dim.8), calls=%async_computation.3 | async-start | bytes 4194304 | tf_op jit(solution)/shard_map/all_to_all | solution.py:25
  58.5 8.4 %shard_map.110 = (bf16[1024,1024]{1,0:T(8,128)(2,1)S(1)}, f32[1024,512]{1,0:T(8,128)S(1)}, f32[1024,512]{1,0:T(8,128)S(1)}, bf16[4,2,128,1024]{3,2,1,0:T(8,128)(2,1)S(1)}) custom-call(s32[1024,1]{1,0:T(8,128)S(1)} %bitcast.67, bf16[512,1024]{1,0:T(8,128)(2,1)S(1)} %bitcast.69, bf16[512,1024]{1,0:T(8,128)(2,1)S(1)} %bitcast.71, ...), custom_call_target="tpu_custom_call" | custom-call | flops 6442450944 | bytes 16781312 | tf_op jit(solution)/shard_map/pallas_call | solution.py:192
  74.4 5.9 %shard_map.111 = (bf16[1024,1024]{1,0:T(8,128)(2,1)S(1)}, bf16[4,4,32,1024]{3,2,1,0:T(8,128)(2,1)S(1)}, bf16[4,4,32,1024]{3,2,1,0:T(8,128)(2,1)}) custom-call(s32[1]{0:T(128)} %bitcast.5.core_ref, f32[1024,1]{1,0:T(8,128)S(1)} %copy.16.scale_ref, bf16[4,2,128,1024]{3,2,1,0:T(8,128)(2,1)} %all-to-all-done.3.cots, bf16[1024,1024]{1,0:T(8,128)(2,1)S(1)} %copy-done.23), custom_call_target="tpu_custom_call" | custom-call | flops 2147483648 | bytes 8392704 | tf_op jit(solution)/shard_map/pallas_call | solution.py:192
  82.6 4.5 %all-to-all-start.2 = ((bf16[4,2,128,1024]{3,2,1,0:T(8,128)(2,1)}), bf16[4,2,128,1024]{3,2,1,0:T(8,128)(2,1)}, u32[]{:S(2)}, u32[]{:S(2)}) async-start(bf16[4,2,128,1024]{3,2,1,0:T(8,128)(2,1)} %copy-done.9), calls=%async_computation.2 | async-start | bytes 4194304 | tf_op jit(solution)/shard_map/all_to_all | solution.py:25
  91.8 3.4 %shard_map.112.gu = bf16[1024,2048]{1,0:T(8,128)(2,1)S(1)} custom-call(s32[1024,1]{1,0:T(8,128)S(1)} %bitcast.68, bf16[1024,1024]{1,0:T(8,128)(2,1)S(1)} %copy-done.8, bf16[1024,1024]{1,0:T(8,128)(2,1)S(1)} %bitcast.66, f32[1024,512]{1,0:T(8,128)S(1)} %copy-done.4, f32[1024,512]{1,0:T(8,128)S(1)} %copy-done.6), custom_call_target="tpu_custom_call" | custom-call | flops 2147483648 | bytes 12587008 | tf_op jit(solution)/shard_map/pallas_call | solution.py:192
  99.3 6.4 %shard_map.113 = (bf16[4,4,32,2048]{3,2,1,0:T(8,128)(2,1)S(1)}, bf16[4,4,32,2048]{3,2,1,0:T(8,128)(2,1)}) custom-call(s32[1]{0:T(128)} %bitcast.5.core_ref, bf16[512,1024]{1,0:T(8,128)(2,1)S(1)} %bitcast.70, bf16[512,1024]{1,0:T(8,128)(2,1)S(1)} %bitcast.72, bf16[1024,2048]{1,0:T(8,128)(2,1)S(1)} %shard_map.112.gu), custom_call_target="tpu_custom_call" | custom-call | flops 4294967296 | bytes 10485760 | tf_op jit(solution)/shard_map/pallas_call | solution.py:192
  106.4 2.6 %collective-permute-start.5 = (bf16[4,32,1024]{2,1,0:T(8,128)(2,1)S(1)}, bf16[4,32,1024]{2,1,0:T(8,128)(2,1)}, u32[]{:S(2)}, u32[]{:S(2)}) collective-permute-start(bf16[4,32,1024]{2,1,0:T(8,128)(2,1)S(1)} %get-tuple-element.69), channel_id=1, source_target_pairs={{0,32},{16,48},{32,0},{48,16},{1,33},{17,49},{33,1},{49,17},{2,34}... | collective-permute-start | bytes 786440 | tf_op jit(solution)/shard_map/ppermute | solution.py:17
  109.0 5.4 %all-to-all-done.2 = bf16[4,2,128,1024]{3,2,1,0:T(8,128)(2,1)} async-done(((bf16[4,2,128,1024]{3,2,1,0:T(8,128)(2,1)}), bf16[4,2,128,1024]{3,2,1,0:T(8,128)(2,1)}, u32[]{:S(2)}, u32[]{:S(2)}) %all-to-all-start.2) | async-done | bytes 2097184 | tf_op jit(solution)/shard_map/all_to_all | solution.py:25
  117.4 6.4 %collective-permute-start.7 = (bf16[128,1024]{1,0:T(8,128)(2,1)S(1)}, bf16[128,1024]{1,0:T(8,128)(2,1)S(1)}, u32[]{:S(2)}, u32[]{:S(2)}) collective-permute-start(bf16[128,1024]{1,0:T(8,128)(2,1)S(1)} %fusion.10), channel_id=1, source_target_pairs={{0,4},{4,0},{1,5},{5,1},{2,6},{6,2},{3,7},{7,3},{8,12},{12,8},{9,1... | collective-permute-start | bytes 786440 | tf_op jit(solution)/shard_map/ppermute | solution.py:17
  127.6 6.7 %shard_map.114 = (bf16[4,128,1024]{2,1,0:T(8,128)(2,1)}, bf16[4,128,1024]{2,1,0:T(8,128)(2,1)}) custom-call(bf16[1024,2048]{1,0:T(8,128)(2,1)S(1)} %copy-done.1, bf16[2,1024,512]{2,1,0:T(8,128)(2,1)S(1)} %copy-done.19, bf16[2,1024,512]{2,1,0:T(8,128)(2,1)S(1)} %copy-done.21), custom_call_target="tpu_custom_call" | custom-call | flops 4294967296 | bytes 10485760 | tf_op jit(solution)/shard_map/pallas_call | solution.py:192
  134.9 2.4 %convert_add_fusion = f32[4,4,32,2048]{3,2,1,0:T(8,128)S(1)} fusion(bf16[4,4,32,2048]{3,2,1,0:T(8,128)(2,1)} %collective-permute-done.3, bf16[4,4,32,2048]{3,2,1,0:T(8,128)(2,1)S(1)} %get-tuple-element.78), kind=kLoop, calls=%fused_computation | loop fusion | flops 3145728 | bytes 8388608 | tf_op jit(solution)/shard_map/add | solution.py:58
  138.7 3.5 %all-to-all-start.4 = ((bf16[4,128,1024]{2,1,0:T(8,128)(2,1)}), bf16[4,128,1024]{2,1,0:T(8,128)(2,1)S(1)}, u32[]{:S(2)}, u32[]{:S(2)}) async-start(bf16[4,128,1024]{2,1,0:T(8,128)(2,1)} %get-tuple-element.85), calls=%async_computation.4 | async-start | bytes 2097152 | tf_op jit(solution)/shard_map/all_to_all | solution.py:25
  146.4 10.1 %all-to-all-done.4 = bf16[4,128,1024]{2,1,0:T(8,128)(2,1)S(1)} async-done(((bf16[4,128,1024]{2,1,0:T(8,128)(2,1)}), bf16[4,128,1024]{2,1,0:T(8,128)(2,1)S(1)}, u32[]{:S(2)}, u32[]{:S(2)}) %all-to-all-start.4) | async-done | bytes 1048608 | tf_op jit(solution)/shard_map/all_to_all | solution.py:25
  156.5 3.5 %all-to-all-start.5 = ((bf16[4,128,1024]{2,1,0:T(8,128)(2,1)}), bf16[4,128,1024]{2,1,0:T(8,128)(2,1)S(1)}, u32[]{:S(2)}, u32[]{:S(2)}) async-start(bf16[4,128,1024]{2,1,0:T(8,128)(2,1)} %get-tuple-element.86), calls=%async_computation.5 | async-start | bytes 2097152 | tf_op jit(solution)/shard_map/all_to_all | solution.py:25
  160.1 8.1 %collective-permute-done.10 = bf16[4,32,2048]{2,1,0:T(8,128)(2,1)} collective-permute-done((bf16[4,32,2048]{2,1,0:T(8,128)(2,1)}, bf16[4,32,2048]{2,1,0:T(8,128)(2,1)}, u32[]{:S(2)}, u32[]{:S(2)}) %collective-permute-start.10) | collective-permute-done | bytes 524320 | tf_op jit(solution)/shard_map/ppermute | solution.py:17
  171.8 10.6 %collective-permute-done.11 = bf16[128,1024]{1,0:T(8,128)(2,1)S(1)} collective-permute-done((bf16[128,1024]{1,0:T(8,128)(2,1)S(1)}, bf16[128,1024]{1,0:T(8,128)(2,1)S(1)}, u32[]{:S(2)}, u32[]{:S(2)}) %collective-permute-start.11) | collective-permute-done | bytes 262176 | tf_op jit(solution)/shard_map/ppermute | solution.py:17
  183.1 11.0 %all-to-all-start.6 = ((bf16[4,32,3072]{2,1,0:T(8,128)(2,1)}), bf16[4,32,3072]{2,1,0:T(8,128)(2,1)S(1)}, u32[]{:S(2)}, u32[]{:S(2)}) async-start(bf16[4,32,3072]{2,1,0:T(8,128)(2,1)} %pad_maximum_fusion), calls=%async_computation.6 | async-start | bytes 1572864 | tf_op jit(solution)/shard_map/all_to_all | solution.py:25
  196.7 17.6 %all-to-all-done.6 = bf16[4,32,3072]{2,1,0:T(8,128)(2,1)S(1)} async-done(((bf16[4,32,3072]{2,1,0:T(8,128)(2,1)}), bf16[4,32,3072]{2,1,0:T(8,128)(2,1)S(1)}, u32[]{:S(2)}, u32[]{:S(2)}) %all-to-all-start.6) | async-done | bytes 786464 | tf_op jit(solution)/shard_map/all_to_all | solution.py:25
  (119 shorter events, 54.1 us)
Async XLA Ops:
  2.8 19.6 %all-to-all-start = ((bf16[4,128,1024]{2,1,0:T(8,128)(2,1)}), bf16[4,128,1024]{2,1,0:T(8,128)(2,1)S(1)}, u32[]{:S(2)}, u32[]{:S(2)}) async-start(bf16[4,128,1024]{2,1,0:T(8,128)(2,1)} %broadcast_in_dim.6), calls=%async_computation | async-start | bytes 2097152 | tf_op jit(solution)/shard_map/all_to_all | solution.py:25
  7.3 20.2 %copy-start.27 = (bf16[128,1024]{1,0:T(8,128)(2,1)S(1)}, bf16[128,1024]{1,0:T(8,128)(2,1)}, u32[]{:S(2)}) copy-start(bf16[128,1024]{1,0:T(8,128)(2,1)} %param.8) | copy-start | bytes 786436
  7.3 14.3 %collective-permute-start = (bf16[128,1024]{1,0:T(8,128)(2,1)S(1)}, bf16[128,1024]{1,0:T(8,128)(2,1)S(1)}, u32[]{:S(2)}, u32[]{:S(2)}) collective-permute-start(bf16[128,1024]{1,0:T(8,128)(2,1)S(1)} %copy-done.26), channel_id=1, source_target_pairs={{0,4},{4,0},{1,5},{5,1},{2,6},{6,2},{3,7},{7,3},{8,12},{12,8},{9,1... | collective-permute-start | bytes 786440 | tf_op jit(solution)/shard_map/ppermute | solution.py:17
  22.4 22.4 %copy-start.10 = (bf16[4,128,1024]{2,1,0:T(8,128)(2,1)}, bf16[4,128,1024]{2,1,0:T(8,128)(2,1)S(1)}, u32[]{:S(2)}) copy-start(bf16[4,128,1024]{2,1,0:T(8,128)(2,1)S(1)} %all-to-all-done) | copy-start | bytes 3145732
  23.7 21.1 %all-to-all-start.1 = ((bf16[4,128,1024]{2,1,0:T(8,128)(2,1)}), bf16[4,128,1024]{2,1,0:T(8,128)(2,1)S(1)}, u32[]{:S(2)}, u32[]{:S(2)}) async-start(bf16[4,128,1024]{2,1,0:T(8,128)(2,1)} %broadcast_in_dim.7), calls=%async_computation.1 | async-start | bytes 2097152 | tf_op jit(solution)/shard_map/all_to_all | solution.py:25
  27.4 17.3 %collective-permute-start.1 = (bf16[128,1024]{1,0:T(8,128)(2,1)S(1)}, bf16[128,1024]{1,0:T(8,128)(2,1)S(1)}, u32[]{:S(2)}, u32[]{:S(2)}) collective-permute-start(bf16[128,1024]{1,0:T(8,128)(2,1)S(1)} %copy-done.27), channel_id=1, source_target_pairs={{0,4},{4,0},{1,5},{5,1},{2,6},{6,2},{3,7},{7,3},{8,12},{12,8},{9,1... | collective-permute-start | bytes 786440 | tf_op jit(solution)/shard_map/ppermute | solution.py:17
  47.4 25.4 %all-to-all-start.3 = ((bf16[4,2,128,1024]{3,2,1,0:T(8,128)(2,1)}), bf16[4,2,128,1024]{3,2,1,0:T(8,128)(2,1)}, u32[]{:S(2)}, u32[]{:S(2)}) async-start(bf16[4,2,128,1024]{3,2,1,0:T(8,128)(2,1)} %broadcast_in_dim.8), calls=%async_computation.3 | async-start | bytes 4194304 | tf_op jit(solution)/shard_map/all_to_all | solution.py:25
  82.6 12.7 %collective-permute-start.2 = (bf16[4,4,32,1024]{3,2,1,0:T(8,128)(2,1)}, bf16[4,4,32,1024]{3,2,1,0:T(8,128)(2,1)}, u32[]{:S(2)}, u32[]{:S(2)}) collective-permute-start(bf16[4,4,32,1024]{3,2,1,0:T(8,128)(2,1)} %get-tuple-element.55), channel_id=1, source_target_pairs={{0,8},{8,0},{1,9},{9,1},{2,10},{10,2},{3,11},{11,3},{4,12},{12,4},... | collective-permute-start | bytes 3145736 | tf_op jit(solution)/shard_map/ppermute | solution.py:17
  82.6 31.8 %all-to-all-start.2 = ((bf16[4,2,128,1024]{3,2,1,0:T(8,128)(2,1)}), bf16[4,2,128,1024]{3,2,1,0:T(8,128)(2,1)}, u32[]{:S(2)}, u32[]{:S(2)}) async-start(bf16[4,2,128,1024]{3,2,1,0:T(8,128)(2,1)} %copy-done.9), calls=%async_computation.2 | async-start | bytes 4194304 | tf_op jit(solution)/shard_map/all_to_all | solution.py:25
  105.7 29.2 %collective-permute-start.3 = (bf16[4,4,32,2048]{3,2,1,0:T(8,128)(2,1)}, bf16[4,4,32,2048]{3,2,1,0:T(8,128)(2,1)}, u32[]{:S(2)}, u32[]{:S(2)}) collective-permute-start(bf16[4,4,32,2048]{3,2,1,0:T(8,128)(2,1)} %get-tuple-element.67), channel_id=1, source_target_pairs={{0,8},{8,0},{1,9},{9,1},{2,10},{10,2},{3,11},{11,3},{4,12},{12,4},... | collective-permute-start | bytes 6291464 | tf_op jit(solution)/shard_map/ppermute | solution.py:17
  106.1 28.2 %collective-permute-start.4 = (bf16[4,32,1024]{2,1,0:T(8,128)(2,1)S(1)}, bf16[4,32,1024]{2,1,0:T(8,128)(2,1)}, u32[]{:S(2)}, u32[]{:S(2)}) collective-permute-start(bf16[4,32,1024]{2,1,0:T(8,128)(2,1)S(1)} %get-tuple-element.68), channel_id=1, source_target_pairs={{0,16},{16,32},{32,48},{48,0},{1,17},{17,33},{33,49},{49,1},{2,18}... | collective-permute-start | bytes 786440 | tf_op jit(solution)/shard_map/ppermute | solution.py:17
  106.4 27.9 %collective-permute-start.5 = (bf16[4,32,1024]{2,1,0:T(8,128)(2,1)S(1)}, bf16[4,32,1024]{2,1,0:T(8,128)(2,1)}, u32[]{:S(2)}, u32[]{:S(2)}) collective-permute-start(bf16[4,32,1024]{2,1,0:T(8,128)(2,1)S(1)} %get-tuple-element.69), channel_id=1, source_target_pairs={{0,32},{16,48},{32,0},{48,16},{1,33},{17,49},{33,1},{49,17},{2,34}... | collective-permute-start | bytes 786440 | tf_op jit(solution)/shard_map/ppermute | solution.py:17
  109.0 25.3 %collective-permute-start.6 = (bf16[4,32,1024]{2,1,0:T(8,128)(2,1)S(1)}, bf16[4,32,1024]{2,1,0:T(8,128)(2,1)}, u32[]{:S(2)}, u32[]{:S(2)}) collective-permute-start(bf16[4,32,1024]{2,1,0:T(8,128)(2,1)S(1)} %get-tuple-element.70), channel_id=1, source_target_pairs={{0,48},{16,0},{32,16},{48,32},{1,49},{17,1},{33,17},{49,33},{2,50}... | collective-permute-start | bytes 786440 | tf_op jit(solution)/shard_map/ppermute | solution.py:17
  114.4 9.4 %copy-start.19 = (bf16[2,1024,512]{2,1,0:T(8,128)(2,1)S(1)}, bf16[2,1024,512]{2,1,0:T(8,128)(2,1)}, u32[]{:S(2)}) copy-start(bf16[2,1024,512]{2,1,0:T(8,128)(2,1)} %wg.1) | copy-start | bytes 6291460
  117.4 17.5 %collective-permute-start.7 = (bf16[128,1024]{1,0:T(8,128)(2,1)S(1)}, bf16[128,1024]{1,0:T(8,128)(2,1)S(1)}, u32[]{:S(2)}, u32[]{:S(2)}) collective-permute-start(bf16[128,1024]{1,0:T(8,128)(2,1)S(1)} %fusion.10), channel_id=1, source_target_pairs={{0,4},{4,0},{1,5},{5,1},{2,6},{6,2},{3,7},{7,3},{8,12},{12,8},{9,1... | collective-permute-start | bytes 786440 | tf_op jit(solution)/shard_map/ppermute | solution.py:17
  138.7 17.9 %all-to-all-start.4 = ((bf16[4,128,1024]{2,1,0:T(8,128)(2,1)}), bf16[4,128,1024]{2,1,0:T(8,128)(2,1)S(1)}, u32[]{:S(2)}, u32[]{:S(2)}) async-start(bf16[4,128,1024]{2,1,0:T(8,128)(2,1)} %get-tuple-element.85), calls=%async_computation.4 | async-start | bytes 2097152 | tf_op jit(solution)/shard_map/all_to_all | solution.py:25
  142.2 17.9 %collective-permute-start.8 = (bf16[4,32,2048]{2,1,0:T(8,128)(2,1)}, bf16[4,32,2048]{2,1,0:T(8,128)(2,1)}, u32[]{:S(2)}, u32[]{:S(2)}) collective-permute-start(bf16[4,32,2048]{2,1,0:T(8,128)(2,1)} %get-tuple-element.81), channel_id=1, source_target_pairs={{0,16},{16,32},{32,48},{48,0},{1,17},{17,33},{33,49},{49,1},{2,18}... | collective-permute-start | bytes 1572872 | tf_op jit(solution)/shard_map/ppermute | solution.py:17
  142.7 17.3 %collective-permute-start.9 = (bf16[4,32,2048]{2,1,0:T(8,128)(2,1)}, bf16[4,32,2048]{2,1,0:T(8,128)(2,1)}, u32[]{:S(2)}, u32[]{:S(2)}) collective-permute-start(bf16[4,32,2048]{2,1,0:T(8,128)(2,1)} %get-tuple-element.82), channel_id=1, source_target_pairs={{0,32},{16,48},{32,0},{48,16},{1,33},{17,49},{33,1},{49,17},{2,34}... | collective-permute-start | bytes 1572872 | tf_op jit(solution)/shard_map/ppermute | solution.py:17
  145.2 23.0 %collective-permute-start.10 = (bf16[4,32,2048]{2,1,0:T(8,128)(2,1)}, bf16[4,32,2048]{2,1,0:T(8,128)(2,1)}, u32[]{:S(2)}, u32[]{:S(2)}) collective-permute-start(bf16[4,32,2048]{2,1,0:T(8,128)(2,1)} %get-tuple-element.83), channel_id=1, source_target_pairs={{0,48},{16,0},{32,16},{48,32},{1,49},{17,1},{33,17},{49,33},{2,50}... | collective-permute-start | bytes 1572872 | tf_op jit(solution)/shard_map/ppermute | solution.py:17
  156.5 25.8 %all-to-all-start.5 = ((bf16[4,128,1024]{2,1,0:T(8,128)(2,1)}), bf16[4,128,1024]{2,1,0:T(8,128)(2,1)S(1)}, u32[]{:S(2)}, u32[]{:S(2)}) async-start(bf16[4,128,1024]{2,1,0:T(8,128)(2,1)} %get-tuple-element.86), calls=%async_computation.5 | async-start | bytes 2097152 | tf_op jit(solution)/shard_map/all_to_all | solution.py:25
  169.8 24.2 %copy-start.25 = (f32[2,128,1024]{2,1,0:T(8,128)S(1)}, f32[2,128,1024]{2,1,0:T(8,128)}, u32[]{:S(2)}) copy-start(f32[2,128,1024]{2,1,0:T(8,128)} %copy-done.24) | copy-start | bytes 3145732
  170.0 24.0 %copy-start.29 = (bf16[128,1024]{1,0:T(8,128)(2,1)S(1)}, bf16[128,1024]{1,0:T(8,128)(2,1)}, u32[]{:S(2)}) copy-start(bf16[128,1024]{1,0:T(8,128)(2,1)} %copy-done.28) | copy-start | bytes 786436
  170.0 12.3 %collective-permute-start.11 = (bf16[128,1024]{1,0:T(8,128)(2,1)S(1)}, bf16[128,1024]{1,0:T(8,128)(2,1)S(1)}, u32[]{:S(2)}, u32[]{:S(2)}) collective-permute-start(bf16[128,1024]{1,0:T(8,128)(2,1)S(1)} %fusion.9), channel_id=1, source_target_pairs={{0,4},{4,0},{1,5},{5,1},{2,6},{6,2},{3,7},{7,3},{8,12},{12,8},{9,1... | collective-permute-start | bytes 786440 | tf_op jit(solution)/shard_map/ppermute | solution.py:17
  183.1 31.3 %all-to-all-start.6 = ((bf16[4,32,3072]{2,1,0:T(8,128)(2,1)}), bf16[4,32,3072]{2,1,0:T(8,128)(2,1)S(1)}, u32[]{:S(2)}, u32[]{:S(2)}) async-start(bf16[4,32,3072]{2,1,0:T(8,128)(2,1)} %pad_maximum_fusion), calls=%async_computation.6 | async-start | bytes 1572864 | tf_op jit(solution)/shard_map/all_to_all | solution.py:25
  (28 other events, 59.0 us)

commit v3 on v2

--- a/solution.py
+++ b/solution.py
@@ -83,27 +83,28 @@
     up = dot(xx, wu[...], 1, 0)
     sigma = 1.0 / (1.0 + jnp.exp(-gate))
     silu = gate * sigma
-    a_ref[...] = up * sigma * (1.0 + gate * (1.0 - sigma))
-    s_ref[...] = silu
+    a_ref[...] = (up * sigma * (1.0 + gate * (1.0 - sigma))).astype(BF16)
+    s_ref[...] = silu.astype(BF16)
     hidden = (silu * up).astype(BF16)
     hh = jnp.concatenate(split(hidden, second), axis=1)
     hh_ref[...] = hh
     out_ref[...] = dot(hh, wd[...], 1, 0).astype(BF16).reshape(out_ref.shape)
 
 
-def down_kernel(core_ref, scale_ref, cots, hh, dout, own, other):
+def down_kernel(place, scale_ref, *refs):
+    hh, dout, own, other = refs[8:]
     i = pl.program_id(0)
-    ny, nz, rows, _ = cots.shape
+    rows = refs[0].shape[0]
 
     @pl.when(i == 0)
     def _():
-        for y in range(ny):
-            for z in range(nz):
-                at = slice((z * ny + y) * rows, (z * ny + y + 1) * rows)
-                dout[at] = (scale_ref[at] * cots[y, z].astype(F32)).astype(BF16)
+        for j, block in enumerate(refs[:8]):
+            y = (place[1] + 4 - j % 4) % 4
+            at = pl.ds(pl.multiple_of((j // 4 * 4 + y) * rows, rows), rows)
+            dout[at] = (scale_ref[at] * block[...].astype(F32)).astype(BF16)
 
     columns = pl.ds(pl.multiple_of(i * TILE, TILE), TILE)
-    put_grad(dot(dout[:, columns], hh[...], 0, 0), core_ref[0], own, other)
+    put_grad(dot(dout[:, columns], hh[...], 0, 0), place[0], own, other)
 
 
 def back_kernel(second_ref, dout, wd, a_ref, s_ref, gu_ref):
@@ -116,30 +117,21 @@
     gu_ref[...] = jnp.concatenate(split(gate_grad, second) + split(up_grad, second), axis=1)
 
 
-def weight_kernel(core_ref, near, far, gu, own, other):
+def weight_kernel(place, near, far, gu, own, other):
     rows = near.shape[0]
     value = dot(near[...], gu[:rows], 0, 0) + dot(far[...], gu[rows:], 0, 0)
-    put_grad(value, core_ref[0], own, other)
-
-
-def input_kernel(gu, wg, wu, near, far):
+    put_grad(value, place[0], own, other)
+
+
+def input_kernel(gu, wg, wu, out_ref):
     ff = wg.shape[2]
-    i = pl.program_id(0)
     value = None
     for j, w in enumerate((wg, wu)):
         for e in range(EXP):
             c = (j * EXP + e) * ff
             term = dot(gu[:, c : c + ff], w[e], 1, 1)
             value = term if value is None else value + term
-    value = value.astype(BF16).reshape(2, -1, value.shape[1])
-
-    @pl.when(i < 2)
-    def _():
-        near[pl.ds(2 * i, 2)] = value
-
-    @pl.when(i >= 2)
-    def _():
-        far[pl.ds(2 * i - 4, 2)] = value
+    out_ref[...] = value.astype(BF16).reshape(out_ref.shape)
 
 
 def call(kernel, grid, ins, outs, flops, scalars=0):
@@ -153,7 +145,7 @@
             in_specs=[pl.BlockSpec(b, m) for b, m, _ in ins],
             out_specs=[pl.BlockSpec(b, m) for b, m, _ in outs],
         ),
-        compiler_params=pltpu.CompilerParams(vmem_limit_bytes=26 << 20),
+        compiler_params=pltpu.CompilerParams(vmem_limit_bytes=56 << 20),
         cost_estimate=pl.CostEstimate(flops=flops, bytes_accessed=moved, transcendentals=0),
     )
 
@@ -180,72 +172,74 @@
     unit = 2 * rows * width * ff * EXP
     second = near_first(assign)
     scale = near_first(prob)
-    core = lax.axis_index("core").astype(jnp.int32).reshape(1)
+    place = jnp.stack([lax.axis_index("core"), lax.axis_index("y")]).astype(jnp.int32)
     wg2, wu2 = (w.reshape(EXP * width, ff) for w in (w_gate, w_up))
     wd2 = w_down.reshape(wide, width)
-    half = rows // 2
 
     def pieces_of(columns):
         return [tiled(sds((4, 4, own_rows, columns), BF16), 1, 1)] * 2
 
-    def run(kernel, ins, outs, flops, *scalars):
-        return call(kernel, 4, ins, outs, flops, len(scalars))(*scalars, *(a for *_, a in ins))
+    def run(kernel, ins, outs, flops, *scalars, grid=4):
+        return call(kernel, grid, ins, outs, flops, len(scalars))(*scalars, *(a for *_, a in ins))
+
+    def inputs(gu, h):
+        ins = [((TILE, 2 * wide), lambda i: (i + 2 * h, 0), gu), whole(w_gate), whole(w_up)]
+        (part,) = run(input_kernel, ins, [tiled(sds((4, block, width), BF16), 0, 2)], unit, grid=2)
+        return part
 
     far_tokens = send(tokens, "zhi", 1)
+    far_cot = send(cotangent, "zhi", 1)
     x0 = gather_y(tokens)
-    far_tokens, cotangent = tie(far_tokens, cotangent)
+    d0 = sends([cotangent] * 3, "y")
+    x0, far_tokens, far_cot, d0 = tie(x0, far_tokens, far_cot, d0)
     x1 = gather_y(far_tokens)
-    far_cot = send(cotangent, "zhi", 1)
-    both_cot = jnp.stack([cotangent, far_cot])
-    cots = exchange(jnp.broadcast_to(both_cot[None], (SIZES["y"], *both_cot.shape)), "y")
+    d1 = sends([far_cot] * 3, "y")
 
     tile = (TILE, width)
     ins = [tiled(second, 0, TILE)]
     ins += [(tile, lambda i: (jnp.minimum(i, 1), 0), x0), (tile, lambda i: (jnp.maximum(i - 2, 0), 0), x1)]
     ins += [whole(a) for a in (wg2, wu2, wd2)]
     outs = [tiled(sds((rows, wide), BF16), 0, TILE)]
-    outs += [tiled(sds((rows, ff), F32), 0, TILE)] * 2
+    outs += [tiled(sds((rows, ff), BF16), 0, TILE)] * 2
     outs += [((2, 1, block, width), lambda i: (i % 2, i // 2, 0, 0), sds((4, 2, block, width), BF16))]
     hh, act, silu, out = run(forward_kernel, ins, outs, 3 * unit)
     out = exchange(out, "y")
 
-    ins = [whole(a) for a in (scale, cots, hh)]
+    ins = [whole(a) for a in (scale, cotangent, *d0, far_cot, *d1, hh)]
     outs = [whole(sds((rows, width), BF16)), *pieces_of(wide)]
-    dout, down, other = run(down_kernel, ins, outs, unit, core)
+    dout, down, other = run(down_kernel, ins, outs, unit, place)
     down_c = send(other, "core", 1)
 
     ins = [tiled(second, 0, TILE), tiled(dout, 0, TILE), whole(wd2), tiled(act, 0, TILE), tiled(silu, 0, TILE)]
     (gu,) = run(back_kernel, ins, [tiled(sds((rows, 2 * wide), BF16), 0, TILE)], unit)
-
-    gu, down_c = tie(gu, down_c)
+    far = inputs(gu, 1)
+
+    far, out, down_c = tie(far, out, down_c)
     down, down_x = pick(add(down.astype(F32), [down_c]), "x")
-    gu, down, down_x = tie(gu, down, down_x)
+    out = total(out)
+    far, out, down, down_x, gu = tie(far, out, down, down_x, gu)
+    far = exchange(far, "y")
     down_x = sends(down_x, "x")
+    far_out = send(out[1].astype(BF16), "zhi", 1)
+
     ins = [tiled(x0, 1, TILE), tiled(x1, 1, TILE), whole(gu)]
-    both, other = run(weight_kernel, ins, pieces_of(2 * wide), 2 * unit, core)
+    both, other = run(weight_kernel, ins, pieces_of(2 * wide), 2 * unit, place)
     both_c = send(other, "core", 1)
-    out, both = tie(out, both)
-    out = total(out)
-    out, gu, both = tie(out, gu, both)
-    far_out = send(out[1].astype(BF16), "zhi", 1)
-
-    ins = [tiled(gu, 0, TILE), whole(w_gate), whole(w_up)]
-    outs = [whole(sds((4, block, width), BF16))] * 2
-    near, far = run(input_kernel, ins, outs, 2 * unit)
+    both, gu = tie(both, gu)
+    near = inputs(gu, 0)
 
     near, far, both_c, down_x, far_out = tie(near, far, both_c, down_x, far_out)
     both, both_x = pick(add(both.astype(F32), [both_c]), "x")
-    far, near, both, both_x = tie(far, near, both, both_x)
+    far = total(far).astype(BF16)
+    near, far, both, both_x = tie(near, far, both, both_x)
     both_x = sends(both_x, "x")
-    far = exchange(far, "y")
-    near, far = tie(near, far)
+    far = send(far, "zhi", 1)
     near = exchange(near, "y")
-    far = send(total(far).astype(BF16), "zhi", 1)
     own_scale = lax.dynamic_slice_in_dim(scale, lax.axis_index("y") * block, block)
     output = (add(out[0], [far_out]) * own_scale).astype(BF16)
     down = add(down, down_x)
+    down, near, far, both_x = tie(down, near, far, both_x)
     grads = jnp.concatenate([down, add(both, both_x)], axis=2).astype(BF16)
-    grads, near, far = tie(grads, near, far)
     grads = exchange(grads, "zlo")
     input_grad = add(total(near), [far]).astype(BF16)
     grads = total(grads).reshape(own_rows, 3, EXP, ff)

time: 217 us -> 209 us (0.963)
  local copies, waits for them, and re-layouts: 36.7 us -> 14.9 us
  Pallas kernels: 30.8 us -> 49.2 us
  starting transfers between devices: 65.6 us -> 61.6 us
    unnamed x70 -> x46, local copies, waits for them, and re-layouts: 28.5 us -> 6.83 us
    pallas_call x5 -> x6, Pallas kernels: 30.8 us -> 49.2 us  [run(): call(kernel, grid, ins, outs, flops, len(scalars))]
    all_to_all x7 -> x6, starting transfers between devices: 35.4 us -> 26.3 us  [exchange(): return lax.all_to_all(value, axis, 0, 0, tiled=True)]
    ppermute x12 -> x18, starting transfers between devices: 30.2 us -> 35.2 us  [send(): return lax.ppermute(value, axis, [(i, (i + step) % n) for i in range(n)])]
    ppermute x12 -> x18, waiting for transfers between devices: 34.2 us -> 38.3 us  [send(): return lax.ppermute(value, axis, [(i, (i + step) % n) for i in range(n)])]
    all_to_all x7 -> x6, waiting for transfers between devices: 34.2 us -> 30.9 us  [exchange(): return lax.all_to_all(value, axis, 0, 0, tiled=True)]
    add x2 -> x3, other arithmetic: 4.86 us -> 6.04 us  [add(): own = own + piece.astype(F32)]
  transfers between devices with their start and end apart: 19 -> 24, of which waited for: 10 -> 12; matrix products, arithmetic and copies ran while one was open for 6% -> 3% of each run, Pallas kernels for 12% -> 19%
where the time goes in v3:
time: 209 us; the launch traced here: 208 us
  waiting for transfers between devices  69.2 us (33%)
  starting transfers between devices  61.6 us (29%)
  Pallas kernels  49.2 us (24%)
  local copies, waits for them, and re-layouts  14.9 us (7%)
  other arithmetic  12.3 us (6%)
    pallas_call x6, Pallas kernels, run(): call(kernel, grid, ins, outs, flops, len(scalars))  49.2 us
    ppermute x18, waiting for transfers between devices, send(): return lax.ppermute(value, axis, [(i, (i + step) % n) for i in range(n)])  38.3 us
    ppermute x18, starting transfers between devices, send(): return lax.ppermute(value, axis, [(i, (i + step) % n) for i in range(n)])  35.2 us
    all_to_all x6, waiting for transfers between devices, exchange(): return lax.all_to_all(value, axis, 0, 0, tiled=True)  30.9 us
    all_to_all x6, starting transfers between devices, exchange(): return lax.all_to_all(value, axis, 0, 0, tiled=True)  26.3 us
    unnamed x46, local copies, waits for them, and re-layouts  6.83 us
    add x3, other arithmetic, add(): own = own + piece.astype(F32)  6.04 us
  transfers between devices with their start and end apart: 24, of which 12 were waited for; matrix products, arithmetic and copies ran while one was open for 3% of the time, Pallas kernels for 19%

profile of v3, /device:TPU:6, one launch (start us, length us, event | category | flops | bytes accessed | tf_op | source)
XLA Modules:
  0.0 208.2 jit_solution(18423626706915501443)
XLA Ops:
  2.8 4.5 %all-to-all-start = ((bf16[4,128,1024]{2,1,0:T(8,128)(2,1)}), bf16[4,128,1024]{2,1,0:T(8,128)(2,1)S(1)}, u32[]{:S(2)}, u32[]{:S(2)}) async-start(bf16[4,128,1024]{2,1,0:T(8,128)(2,1)} %broadcast_in_dim.4), calls=%async_computation | async-start | bytes 2097152 | tf_op jit(solution)/shard_map/all_to_all | solution.py:25
  7.3 7.3 %collective-permute-start = (bf16[128,1024]{1,0:T(8,128)(2,1)S(1)}, bf16[128,1024]{1,0:T(8,128)(2,1)S(1)}, u32[]{:S(2)}, u32[]{:S(2)}) collective-permute-start(bf16[128,1024]{1,0:T(8,128)(2,1)S(1)} %copy-done.6), channel_id=1, source_target_pairs={{0,4},{4,0},{1,5},{5,1},{2,6},{6,2},{3,7},{7,3},{8,12},{12,8},{9,1... | collective-permute-start | bytes 786440 | tf_op jit(solution)/shard_map/ppermute | solution.py:17
  14.6 3.5 %collective-permute-start.3 = (bf16[128,1024]{1,0:T(8,128)(2,1)S(1)}, bf16[128,1024]{1,0:T(8,128)(2,1)S(1)}, u32[]{:S(2)}, u32[]{:S(2)}) collective-permute-start(bf16[128,1024]{1,0:T(8,128)(2,1)S(1)} %copy-done.15), channel_id=1, source_target_pairs={{0,2},{1,3},{2,0},{3,1},{4,6},{5,7},{6,4},{7,5},{8,10},{9,11},{10,... | collective-permute-start | bytes 786440 | tf_op jit(solution)/shard_map/ppermute | solution.py:17
  21.4 3.8 %collective-permute-done = bf16[128,1024]{1,0:T(8,128)(2,1)S(1)} collective-permute-done((bf16[128,1024]{1,0:T(8,128)(2,1)S(1)}, bf16[128,1024]{1,0:T(8,128)(2,1)S(1)}, u32[]{:S(2)}, u32[]{:S(2)}) %collective-permute-start) | collective-permute-done | bytes 262176 | tf_op jit(solution)/shard_map/ppermute | solution.py:17
  25.3 4.2 %collective-permute-done.3.refs_2_ = bf16[128,1024]{1,0:T(8,128)(2,1)S(1)} collective-permute-done((bf16[128,1024]{1,0:T(8,128)(2,1)S(1)}, bf16[128,1024]{1,0:T(8,128)(2,1)S(1)}, u32[]{:S(2)}, u32[]{:S(2)}) %collective-permute-start.3) | collective-permute-done | bytes 262176 | tf_op jit(solution)/shard_map/ppermute | solution.py:17
  29.5 4.1 %collective-permute-done.2.refs_1_ = bf16[128,1024]{1,0:T(8,128)(2,1)S(1)} collective-permute-done((bf16[128,1024]{1,0:T(8,128)(2,1)S(1)}, bf16[128,1024]{1,0:T(8,128)(2,1)S(1)}, u32[]{:S(2)}, u32[]{:S(2)}) %collective-permute-start.2) | collective-permute-done | bytes 262176 | tf_op jit(solution)/shard_map/ppermute | solution.py:17
  38.0 3.9 %all-to-all-start.1 = ((bf16[4,128,1024]{2,1,0:T(8,128)(2,1)}), bf16[4,128,1024]{2,1,0:T(8,128)(2,1)S(1)}, u32[]{:S(2)}, u32[]{:S(2)}) async-start(bf16[4,128,1024]{2,1,0:T(8,128)(2,1)} %broadcast_in_dim.5), calls=%async_computation.1 | async-start | bytes 2097152 | tf_op jit(solution)/shard_map/all_to_all | solution.py:25
  43.3 3.2 %collective-permute-start.7 = (bf16[128,1024]{1,0:T(8,128)(2,1)S(1)}, bf16[128,1024]{1,0:T(8,128)(2,1)S(1)}, u32[]{:S(2)}, u32[]{:S(2)}) collective-permute-start(bf16[128,1024]{1,0:T(8,128)(2,1)S(1)} %collective-permute-done.1.refs_4_), channel_id=1, source_target_pairs={{0,3},{1,0},{2,1},{3,2},{4,7},{5,4},{6,5},{7,6},{8,11},{9,8},{10,9... | collective-permute-start | bytes 786440 | tf_op jit(solution)/shard_map/ppermute | solution.py:17
  48.3 12.3 %all-to-all-done.1 = bf16[4,128,1024]{2,1,0:T(8,128)(2,1)S(1)} async-done(((bf16[4,128,1024]{2,1,0:T(8,128)(2,1)}), bf16[4,128,1024]{2,1,0:T(8,128)(2,1)S(1)}, u32[]{:S(2)}, u32[]{:S(2)}) %all-to-all-start.1) | async-done | bytes 1048608 | tf_op jit(solution)/shard_map/all_to_all | solution.py:25
  61.6 12.8 %shard_map.110 = (bf16[1024,1024]{1,0:T(8,128)(2,1)}, bf16[1024,512]{1,0:T(8,128)(2,1)}, bf16[1024,512]{1,0:T(8,128)(2,1)}, bf16[4,2,128,1024]{3,2,1,0:T(8,128)(2,1)}) custom-call(s32[1024,1]{1,0:T(8,128)} %bitcast.68, bf16[512,1024]{1,0:T(8,128)(2,1)} %bitcast.70, bf16[512,1024]{1,0:T(8,128)(2,1)} %bitcast.72, bf16[2048,512]{1,0:T(8,128)(2,1)} %bitcast.64, ...), custom_call_target="tpu_custom_call" | custom-call | flops 6442450944 | bytes 14684160 | tf_op jit(solution)/shard_map/pallas_call | solution.py:183
  74.4 3.6 %all-to-all-start.2 = ((bf16[4,2,128,1024]{3,2,1,0:T(8,128)(2,1)}), bf16[4,2,128,1024]{3,2,1,0:T(8,128)(2,1)S(1)}, u32[]{:S(2)}, u32[]{:S(2)}) async-start(bf16[4,2,128,1024]{3,2,1,0:T(8,128)(2,1)} %get-tuple-element.61), calls=%async_computation.2 | async-start | bytes 4194304 | tf_op jit(solution)/shard_map/all_to_all | solution.py:25
  80.4 7.6 %shard_map.111 = (bf16[1024,1024]{1,0:T(8,128)(2,1)}, bf16[4,4,32,1024]{3,2,1,0:T(8,128)(2,1)}, bf16[4,4,32,1024]{3,2,1,0:T(8,128)(2,1)}) custom-call(s32[2]{0:T(128)} %pad_add_fusion.place, f32[1024,1]{1,0:T(8,128)} %copy.16.scale_ref, bf16[128,1024]{1,0:T(8,128)(2,1)} %refs_0_.1, bf16[128,1024]{1,0:T(8,128)(2,1)} %copy-done.17, ...), custom_call_target="tpu_custom_call" | custom-call | flops 2147483648 | bytes 8392704 | tf_op jit(solution)/shard_map/pallas_call | solution.py:183
  88.2 7.4 %shard_map.112.gu = bf16[1024,2048]{1,0:T(8,128)(2,1)} custom-call(s32[1024,1]{1,0:T(8,128)} %bitcast.69, bf16[1024,1024]{1,0:T(8,128)(2,1)} %get-tuple-element.58.dout, bf16[1024,1024]{1,0:T(8,128)(2,1)} %bitcast.67, bf16[1024,512]{1,0:T(8,128)(2,1)} %get-tuple-element.59.a_ref, bf16[1024,512]{1,0:T(8,128)(2,1)} %get-tuple-element.60.s_ref), custom_call_target="tpu_custom_call" | custom-call | flops 2147483648 | bytes 10489856 | tf_op jit(solution)/shard_map/pallas_call | solution.py:183
  95.6 6.0 %shard_map.113 = bf16[4,128,1024]{2,1,0:T(8,128)(2,1)} custom-call(bf16[1024,2048]{1,0:T(8,128)(2,1)} %shard_map.112.gu, bf16[2,1024,512]{2,1,0:T(8,128)(2,1)} %wg.3, bf16[2,1024,512]{2,1,0:T(8,128)(2,1)} %wu.3), custom_call_target="tpu_custom_call" | custom-call | flops 2147483648 | bytes 9437184 | tf_op jit(solution)/shard_map/pallas_call | solution.py:183
  106.4 9.4 %shard_map.114 = (bf16[4,4,32,2048]{3,2,1,0:T(8,128)(2,1)}, bf16[4,4,32,2048]{3,2,1,0:T(8,128)(2,1)}) custom-call(s32[2]{0:T(128)} %pad_add_fusion.place, bf16[512,1024]{1,0:T(8,128)(2,1)} %bitcast.71, bf16[512,1024]{1,0:T(8,128)(2,1)} %bitcast.73, bf16[1024,2048]{1,0:T(8,128)(2,1)} %shard_map.112.gu), custom_call_target="tpu_custom_call" | custom-call | flops 4294967296 | bytes 10485760 | tf_op jit(solution)/shard_map/pallas_call | solution.py:183
  116.2 4.8 %all-to-all-start.3 = ((bf16[4,128,1024]{2,1,0:T(8,128)(2,1)}), bf16[4,128,1024]{2,1,0:T(8,128)(2,1)S(1)}, u32[]{:S(2)}, u32[]{:S(2)}) async-start(bf16[4,128,1024]{2,1,0:T(8,128)(2,1)} %shard_map.113), calls=%async_computation.3 | async-start | bytes 2097152 | tf_op jit(solution)/shard_map/all_to_all | solution.py:25
  121.0 5.9 %collective-permute-start.13 = (bf16[128,1024]{1,0:T(8,128)(2,1)S(1)}, bf16[128,1024]{1,0:T(8,128)(2,1)S(1)}, u32[]{:S(2)}, u32[]{:S(2)}) collective-permute-start(bf16[128,1024]{1,0:T(8,128)(2,1)S(1)} %fusion.10), channel_id=1, source_target_pairs={{0,4},{4,0},{1,5},{5,1},{2,6},{6,2},{3,7},{7,3},{8,12},{12,8},{9,1... | collective-permute-start | bytes 786440 | tf_op jit(solution)/shard_map/ppermute | solution.py:17
  129.8 5.9 %shard_map.115 = bf16[4,128,1024]{2,1,0:T(8,128)(2,1)} custom-call(bf16[1024,2048]{1,0:T(8,128)(2,1)} %shard_map.112.gu, bf16[2,1024,512]{2,1,0:T(8,128)(2,1)} %wg.3, bf16[2,1024,512]{2,1,0:T(8,128)(2,1)} %wu.3), custom_call_target="tpu_custom_call" | custom-call | flops 2147483648 | bytes 9437184 | tf_op jit(solution)/shard_map/pallas_call | solution.py:183
  147.4 4.5 %all-to-all-start.4 = ((bf16[4,128,1024]{2,1,0:T(8,128)(2,1)}), bf16[4,128,1024]{2,1,0:T(8,128)(2,1)S(1)}, u32[]{:S(2)}, u32[]{:S(2)}) async-start(bf16[4,128,1024]{2,1,0:T(8,128)(2,1)} %shard_map.115), calls=%async_computation.4 | async-start | bytes 2097152 | tf_op jit(solution)/shard_map/all_to_all | solution.py:25
  155.0 3.6 %collective-permute-start.14 = (bf16[128,1024]{1,0:T(8,128)(2,1)}, bf16[128,1024]{1,0:T(8,128)(2,1)S(1)}, u32[]{:S(2)}, u32[]{:S(2)}) collective-permute-start(bf16[128,1024]{1,0:T(8,128)(2,1)} %fusion.9), channel_id=1, source_target_pairs={{0,4},{4,0},{1,5},{5,1},{2,6},{6,2},{3,7},{7,3},{8,12},{12,8},{9,1... | collective-permute-start | bytes 786440 | tf_op jit(solution)/shard_map/ppermute | solution.py:17
  160.1 7.7 %collective-permute-done.14 = bf16[128,1024]{1,0:T(8,128)(2,1)S(1)} collective-permute-done((bf16[128,1024]{1,0:T(8,128)(2,1)}, bf16[128,1024]{1,0:T(8,128)(2,1)S(1)}, u32[]{:S(2)}, u32[]{:S(2)}) %collective-permute-start.14) | collective-permute-done | bytes 262176 | tf_op jit(solution)/shard_map/ppermute | solution.py:17
  170.8 7.4 %collective-permute-done.17 = bf16[4,32,2048]{2,1,0:T(8,128)(2,1)} collective-permute-done((bf16[4,32,2048]{2,1,0:T(8,128)(2,1)}, bf16[4,32,2048]{2,1,0:T(8,128)(2,1)}, u32[]{:S(2)}, u32[]{:S(2)}) %collective-permute-start.17) | collective-permute-done | bytes 524320 | tf_op jit(solution)/shard_map/ppermute | solution.py:17
  180.9 5.0 %all-to-all-start.5 = ((bf16[4,32,3072]{2,1,0:T(8,128)(2,1)}), bf16[4,32,3072]{2,1,0:T(8,128)(2,1)S(1)}, u32[]{:S(2)}, u32[]{:S(2)}) async-start(bf16[4,32,3072]{2,1,0:T(8,128)(2,1)} %pad_maximum_fusion), calls=%async_computation.5 | async-start | bytes 1572864 | tf_op jit(solution)/shard_map/all_to_all | solution.py:25
  187.7 18.6 %all-to-all-done.5 = bf16[4,32,3072]{2,1,0:T(8,128)(2,1)S(1)} async-done(((bf16[4,32,3072]{2,1,0:T(8,128)(2,1)}), bf16[4,32,3072]{2,1,0:T(8,128)(2,1)S(1)}, u32[]{:S(2)}, u32[]{:S(2)}) %all-to-all-start.5) | async-done | bytes 786464 | tf_op jit(solution)/shard_map/all_to_all | solution.py:25
  (105 shorter events, 49.9 us)
Async XLA Ops:
  2.8 33.9 %all-to-all-start = ((bf16[4,128,1024]{2,1,0:T(8,128)(2,1)}), bf16[4,128,1024]{2,1,0:T(8,128)(2,1)S(1)}, u32[]{:S(2)}, u32[]{:S(2)}) async-start(bf16[4,128,1024]{2,1,0:T(8,128)(2,1)} %broadcast_in_dim.4), calls=%async_computation | async-start | bytes 2097152 | tf_op jit(solution)/shard_map/all_to_all | solution.py:25
  7.3 18.0 %collective-permute-start = (bf16[128,1024]{1,0:T(8,128)(2,1)S(1)}, bf16[128,1024]{1,0:T(8,128)(2,1)S(1)}, u32[]{:S(2)}, u32[]{:S(2)}) collective-permute-start(bf16[128,1024]{1,0:T(8,128)(2,1)S(1)} %copy-done.6), channel_id=1, source_target_pairs={{0,4},{4,0},{1,5},{5,1},{2,6},{6,2},{3,7},{7,3},{8,12},{12,8},{9,1... | collective-permute-start | bytes 786440 | tf_op jit(solution)/shard_map/ppermute | solution.py:17
  14.6 14.9 %collective-permute-start.3 = (bf16[128,1024]{1,0:T(8,128)(2,1)S(1)}, bf16[128,1024]{1,0:T(8,128)(2,1)S(1)}, u32[]{:S(2)}, u32[]{:S(2)}) collective-permute-start(bf16[128,1024]{1,0:T(8,128)(2,1)S(1)} %copy-done.15), channel_id=1, source_target_pairs={{0,2},{1,3},{2,0},{3,1},{4,6},{5,7},{6,4},{7,5},{8,10},{9,11},{10,... | collective-permute-start | bytes 786440 | tf_op jit(solution)/shard_map/ppermute | solution.py:17
  18.1 15.5 %collective-permute-start.2 = (bf16[128,1024]{1,0:T(8,128)(2,1)S(1)}, bf16[128,1024]{1,0:T(8,128)(2,1)S(1)}, u32[]{:S(2)}, u32[]{:S(2)}) collective-permute-start(bf16[128,1024]{1,0:T(8,128)(2,1)S(1)} %copy-done.15), channel_id=1, source_target_pairs={{0,1},{1,2},{2,3},{3,0},{4,5},{5,6},{6,7},{7,4},{8,9},{9,10},{10,1... | collective-permute-start | bytes 786440 | tf_op jit(solution)/shard_map/ppermute | solution.py:17
  18.6 18.1 %collective-permute-start.1 = (bf16[128,1024]{1,0:T(8,128)(2,1)S(1)}, bf16[128,1024]{1,0:T(8,128)(2,1)S(1)}, u32[]{:S(2)}, u32[]{:S(2)}) collective-permute-start(bf16[128,1024]{1,0:T(8,128)(2,1)S(1)} %copy-done.15), channel_id=1, source_target_pairs={{0,4},{4,0},{1,5},{5,1},{2,6},{6,2},{3,7},{7,3},{8,12},{12,8},{9,1... | collective-permute-start | bytes 786440 | tf_op jit(solution)/shard_map/ppermute | solution.py:17
  18.7 18.0 %collective-permute-start.4 = (bf16[128,1024]{1,0:T(8,128)(2,1)S(1)}, bf16[128,1024]{1,0:T(8,128)(2,1)S(1)}, u32[]{:S(2)}, u32[]{:S(2)}) collective-permute-start(bf16[128,1024]{1,0:T(8,128)(2,1)S(1)} %copy-done.15), channel_id=1, source_target_pairs={{0,3},{1,0},{2,1},{3,2},{4,7},{5,4},{6,5},{7,6},{8,11},{9,8},{10,9... | collective-permute-start | bytes 786440 | tf_op jit(solution)/shard_map/ppermute | solution.py:17
  38.0 22.6 %all-to-all-start.1 = ((bf16[4,128,1024]{2,1,0:T(8,128)(2,1)}), bf16[4,128,1024]{2,1,0:T(8,128)(2,1)S(1)}, u32[]{:S(2)}, u32[]{:S(2)}) async-start(bf16[4,128,1024]{2,1,0:T(8,128)(2,1)} %broadcast_in_dim.5), calls=%async_computation.1 | async-start | bytes 2097152 | tf_op jit(solution)/shard_map/all_to_all | solution.py:25
  43.3 36.3 %collective-permute-start.7 = (bf16[128,1024]{1,0:T(8,128)(2,1)S(1)}, bf16[128,1024]{1,0:T(8,128)(2,1)S(1)}, u32[]{:S(2)}, u32[]{:S(2)}) collective-permute-start(bf16[128,1024]{1,0:T(8,128)(2,1)S(1)} %collective-permute-done.1.refs_4_), channel_id=1, source_target_pairs={{0,3},{1,0},{2,1},{3,2},{4,7},{5,4},{6,5},{7,6},{8,11},{9,8},{10,9... | collective-permute-start | bytes 786440 | tf_op jit(solution)/shard_map/ppermute | solution.py:17
  46.5 33.1 %collective-permute-start.6 = (bf16[128,1024]{1,0:T(8,128)(2,1)S(1)}, bf16[128,1024]{1,0:T(8,128)(2,1)}, u32[]{:S(2)}, u32[]{:S(2)}) collective-permute-start(bf16[128,1024]{1,0:T(8,128)(2,1)S(1)} %collective-permute-done.1.refs_4_), channel_id=1, source_target_pairs={{0,2},{1,3},{2,0},{3,1},{4,6},{5,7},{6,4},{7,5},{8,10},{9,11},{10,... | collective-permute-start | bytes 786440 | tf_op jit(solution)/shard_map/ppermute | solution.py:17
  47.4 32.2 %collective-permute-start.5 = (bf16[128,1024]{1,0:T(8,128)(2,1)S(1)}, bf16[128,1024]{1,0:T(8,128)(2,1)}, u32[]{:S(2)}, u32[]{:S(2)}) collective-permute-start(bf16[128,1024]{1,0:T(8,128)(2,1)S(1)} %collective-permute-done.1.refs_4_), channel_id=1, source_target_pairs={{0,1},{1,2},{2,3},{3,0},{4,5},{5,6},{6,7},{7,4},{8,9},{9,10},{10,1... | collective-permute-start | bytes 786440 | tf_op jit(solution)/shard_map/ppermute | solution.py:17
  74.4 28.2 %all-to-all-start.2 = ((bf16[4,2,128,1024]{3,2,1,0:T(8,128)(2,1)}), bf16[4,2,128,1024]{3,2,1,0:T(8,128)(2,1)S(1)}, u32[]{:S(2)}, u32[]{:S(2)}) async-start(bf16[4,2,128,1024]{3,2,1,0:T(8,128)(2,1)} %get-tuple-element.61), calls=%async_computation.2 | async-start | bytes 4194304 | tf_op jit(solution)/shard_map/all_to_all | solution.py:25
  88.0 13.6 %collective-permute-start.8 = (bf16[4,4,32,1024]{3,2,1,0:T(8,128)(2,1)}, bf16[4,4,32,1024]{3,2,1,0:T(8,128)(2,1)S(1)}, u32[]{:S(2)}, u32[]{:S(2)}) collective-permute-start(bf16[4,4,32,1024]{3,2,1,0:T(8,128)(2,1)} %get-tuple-element.62), channel_id=1, source_target_pairs={{0,8},{8,0},{1,9},{9,1},{2,10},{10,2},{3,11},{11,3},{4,12},{12,4},... | collective-permute-start | bytes 3145736 | tf_op jit(solution)/shard_map/ppermute | solution.py:17
  115.8 26.3 %collective-permute-start.9 = (bf16[4,4,32,2048]{3,2,1,0:T(8,128)(2,1)}, bf16[4,4,32,2048]{3,2,1,0:T(8,128)(2,1)}, u32[]{:S(2)}, u32[]{:S(2)}) collective-permute-start(bf16[4,4,32,2048]{3,2,1,0:T(8,128)(2,1)} %get-tuple-element.72), channel_id=1, source_target_pairs={{0,8},{8,0},{1,9},{9,1},{2,10},{10,2},{3,11},{11,3},{4,12},{12,4},... | collective-permute-start | bytes 6291464 | tf_op jit(solution)/shard_map/ppermute | solution.py:17
  116.2 25.9 %all-to-all-start.3 = ((bf16[4,128,1024]{2,1,0:T(8,128)(2,1)}), bf16[4,128,1024]{2,1,0:T(8,128)(2,1)S(1)}, u32[]{:S(2)}, u32[]{:S(2)}) async-start(bf16[4,128,1024]{2,1,0:T(8,128)(2,1)} %shard_map.113), calls=%async_computation.3 | async-start | bytes 2097152 | tf_op jit(solution)/shard_map/all_to_all | solution.py:25
  121.0 14.7 %collective-permute-start.13 = (bf16[128,1024]{1,0:T(8,128)(2,1)S(1)}, bf16[128,1024]{1,0:T(8,128)(2,1)S(1)}, u32[]{:S(2)}, u32[]{:S(2)}) collective-permute-start(bf16[128,1024]{1,0:T(8,128)(2,1)S(1)} %fusion.10), channel_id=1, source_target_pairs={{0,4},{4,0},{1,5},{5,1},{2,6},{6,2},{3,7},{7,3},{8,12},{12,8},{9,1... | collective-permute-start | bytes 786440 | tf_op jit(solution)/shard_map/ppermute | solution.py:17
  126.9 9.2 %collective-permute-start.10 = (bf16[4,32,1024]{2,1,0:T(8,128)(2,1)S(1)}, bf16[4,32,1024]{2,1,0:T(8,128)(2,1)S(1)}, u32[]{:S(2)}, u32[]{:S(2)}) collective-permute-start(bf16[4,32,1024]{2,1,0:T(8,128)(2,1)S(1)} %get-tuple-element.73), channel_id=1, source_target_pairs={{0,16},{16,32},{32,48},{48,0},{1,17},{17,33},{33,49},{49,1},{2,18}... | collective-permute-start | bytes 786440 | tf_op jit(solution)/shard_map/ppermute | solution.py:17
  127.4 10.8 %collective-permute-start.11 = (bf16[4,32,1024]{2,1,0:T(8,128)(2,1)S(1)}, bf16[4,32,1024]{2,1,0:T(8,128)(2,1)S(1)}, u32[]{:S(2)}, u32[]{:S(2)}) collective-permute-start(bf16[4,32,1024]{2,1,0:T(8,128)(2,1)S(1)} %get-tuple-element.74), channel_id=1, source_target_pairs={{0,32},{16,48},{32,0},{48,16},{1,33},{17,49},{33,1},{49,17},{2,34}... | collective-permute-start | bytes 786440 | tf_op jit(solution)/shard_map/ppermute | solution.py:17
  129.8 12.3 %collective-permute-start.12 = (bf16[4,32,1024]{2,1,0:T(8,128)(2,1)S(1)}, bf16[4,32,1024]{2,1,0:T(8,128)(2,1)}, u32[]{:S(2)}, u32[]{:S(2)}) collective-permute-start(bf16[4,32,1024]{2,1,0:T(8,128)(2,1)S(1)} %get-tuple-element.75), channel_id=1, source_target_pairs={{0,48},{16,0},{32,16},{48,32},{1,49},{17,1},{33,17},{49,33},{2,50}... | collective-permute-start | bytes 786440 | tf_op jit(solution)/shard_map/ppermute | solution.py:17
  147.4 30.9 %all-to-all-start.4 = ((bf16[4,128,1024]{2,1,0:T(8,128)(2,1)}), bf16[4,128,1024]{2,1,0:T(8,128)(2,1)S(1)}, u32[]{:S(2)}, u32[]{:S(2)}) async-start(bf16[4,128,1024]{2,1,0:T(8,128)(2,1)} %shard_map.115), calls=%async_computation.4 | async-start | bytes 2097152 | tf_op jit(solution)/shard_map/all_to_all | solution.py:25
  151.9 15.9 %collective-permute-start.15 = (bf16[4,32,2048]{2,1,0:T(8,128)(2,1)}, bf16[4,32,2048]{2,1,0:T(8,128)(2,1)S(1)}, u32[]{:S(2)}, u32[]{:S(2)}) collective-permute-start(bf16[4,32,2048]{2,1,0:T(8,128)(2,1)} %get-tuple-element.87), channel_id=1, source_target_pairs={{0,16},{16,32},{32,48},{48,0},{1,17},{17,33},{33,49},{49,1},{2,18}... | collective-permute-start | bytes 1572872 | tf_op jit(solution)/shard_map/ppermute | solution.py:17
  153.5 16.6 %collective-permute-start.16 = (bf16[4,32,2048]{2,1,0:T(8,128)(2,1)}, bf16[4,32,2048]{2,1,0:T(8,128)(2,1)S(1)}, u32[]{:S(2)}, u32[]{:S(2)}) collective-permute-start(bf16[4,32,2048]{2,1,0:T(8,128)(2,1)} %get-tuple-element.88), channel_id=1, source_target_pairs={{0,32},{16,48},{32,0},{48,16},{1,33},{17,49},{33,1},{49,17},{2,34}... | collective-permute-start | bytes 1572872 | tf_op jit(solution)/shard_map/ppermute | solution.py:17
  154.9 23.4 %collective-permute-start.17 = (bf16[4,32,2048]{2,1,0:T(8,128)(2,1)}, bf16[4,32,2048]{2,1,0:T(8,128)(2,1)}, u32[]{:S(2)}, u32[]{:S(2)}) collective-permute-start(bf16[4,32,2048]{2,1,0:T(8,128)(2,1)} %get-tuple-element.89), channel_id=1, source_target_pairs={{0,48},{16,0},{32,16},{48,32},{1,49},{17,1},{33,17},{49,33},{2,50}... | collective-permute-start | bytes 1572872 | tf_op jit(solution)/shard_map/ppermute | solution.py:17
  155.0 12.7 %collective-permute-start.14 = (bf16[128,1024]{1,0:T(8,128)(2,1)}, bf16[128,1024]{1,0:T(8,128)(2,1)S(1)}, u32[]{:S(2)}, u32[]{:S(2)}) collective-permute-start(bf16[128,1024]{1,0:T(8,128)(2,1)} %fusion.9), channel_id=1, source_target_pairs={{0,4},{4,0},{1,5},{5,1},{2,6},{6,2},{3,7},{7,3},{8,12},{12,8},{9,1... | collective-permute-start | bytes 786440 | tf_op jit(solution)/shard_map/ppermute | solution.py:17
  180.9 25.3 %all-to-all-start.5 = ((bf16[4,32,3072]{2,1,0:T(8,128)(2,1)}), bf16[4,32,3072]{2,1,0:T(8,128)(2,1)S(1)}, u32[]{:S(2)}, u32[]{:S(2)}) async-start(bf16[4,32,3072]{2,1,0:T(8,128)(2,1)} %pad_maximum_fusion), calls=%async_computation.5 | async-start | bytes 1572864 | tf_op jit(solution)/shard_map/all_to_all | solution.py:25
  (21 other events, 264.7 us)

commit v4 on v0

--- a/solution.py
+++ b/solution.py
@@ -33,24 +33,25 @@
     return parts
 
 
-def scatter_group(own, *pieces):
-    total = own
-    for k, piece in enumerate(pieces, 1):
-        total = total + send(piece, "y", -k).astype(F32)
-    return total[0] + send(total[1].astype(BF16), "zhi", 1).astype(F32)
-
-
-def scatter_rows(own, other):
-    total = own + send(other, "core", 1).astype(F32)
-    for axis in ("x", "zlo"):
-        g = total
-        n = SIZES[axis]
-        me = lax.axis_index(axis)
-        total = lax.dynamic_index_in_dim(g, me, 0, keepdims=False)
-        for k in range(1, n):
-            piece = lax.dynamic_index_in_dim(g, (me + k) % n, 0, keepdims=False)
-            total = total + send(piece.astype(BF16), axis, k).astype(F32)
-    return total
+def tie(*values):
+    return lax.optimization_barrier(values)
+
+
+def sends(pieces, axis, way=1):
+    return [send(piece, axis, way * k) for k, piece in enumerate(pieces, 1)]
+
+
+def add(own, pieces):
+    for piece in pieces:
+        own = own + piece.astype(F32)
+    return own
+
+
+def pick(value, axis):
+    n = SIZES[axis]
+    me = lax.axis_index(axis)
+    own = lax.dynamic_index_in_dim(value, me, 0, keepdims=False)
+    return own, [lax.dynamic_index_in_dim(value, (me + k) % n, 0, keepdims=False).astype(BF16) for k in range(1, n)]
 
 
 def dot(a, b, ca, cb):
@@ -80,7 +81,7 @@
 def put_grad(value, core, own, other):
     v = value.reshape(4, 2, value.shape[0] // 8, value.shape[1])
     first = core == 0
-    own[...] = jnp.where(first, v[:, 0], v[:, 1])[:, None]
+    own[...] = jnp.where(first, v[:, 0], v[:, 1]).astype(BF16)[:, None]
     other[...] = jnp.where(first, v[:, 1], v[:, 0]).astype(BF16)[:, None]
 
 
@@ -111,34 +112,29 @@
     put_rows(dot(hh, wd[...], 1, 0), *refs[15:19])
 
 
-def down_kernel(core_ref, scale_ref, *refs):
-    blocks = refs[:8]
-    hh, dout, own, other = refs[8:]
+def back_kernel(second_ref, scale_ref, *refs):
+    a_ref, s_ref, wd, dout, gu_ref = refs[4:]
     i = pl.program_id(0)
-    n = blocks[0].shape[0]
+    n = refs[0].shape[1]
 
     @pl.when(i == 0)
     def _():
-        for b, block in enumerate(blocks):
+        for b in range(8):
             at = slice(b * n, (b + 1) * n)
-            dout[at] = (scale_ref[at] * block[...].astype(F32)).astype(BF16)
-
-    columns = pl.ds(pl.multiple_of(i * TILE, TILE), TILE)
-    put_grad(dot(dout[:, columns], hh[...], 0, 0), core_ref[0], own, other)
-
-
-def back_kernel(second_ref, dout, wd, a_ref, s_ref, gu_ref):
+            dout[at] = (scale_ref[at] * refs[b % 4][b // 4].astype(F32)).astype(BF16)
+
+    rows = pl.ds(pl.multiple_of(i * TILE, TILE), TILE)
     second = second_ref[...] > 0
     ff = a_ref.shape[1]
-    both = dot(dout[...], wd[...], 1, 1)
+    both = dot(dout[rows], wd[...], 1, 1)
     back = jnp.where(second, both[:, ff:], both[:, :ff])
     gate_grad = (back * a_ref[...]).astype(BF16)
     up_grad = (back * s_ref[...]).astype(BF16)
     gu_ref[...] = jnp.concatenate(split(gate_grad, second) + split(up_grad, second), axis=1)
 
 
-def weight_kernel(core_ref, x_ref, gu, own, other):
-    put_grad(dot(x_ref[...], gu[...], 0, 0), core_ref[0], own, other)
+def outer_kernel(core_ref, left, right, own, other):
+    put_grad(dot(left[...], right[...], 0, 0), core_ref[0], own, other)
 
 
 def input_kernel(gu, wg, wu, *outs):
@@ -153,7 +149,6 @@
 
 
 def call(kernel, grid, ins, outs, flops, scalars=0):
-    moved = sum(a.size * a.dtype.itemsize for *_, a in ins + outs)
     return pl.pallas_call(
         kernel,
         out_shape=[jax.ShapeDtypeStruct(a.shape, a.dtype) for *_, a in outs],
@@ -164,7 +159,7 @@
             out_specs=[pl.BlockSpec(b, m) for b, m, _ in outs],
         ),
         compiler_params=pltpu.CompilerParams(vmem_limit_bytes=56 << 20),
-        cost_estimate=pl.CostEstimate(flops=flops, bytes_accessed=moved, transcendentals=0),
+        cost_estimate=pl.CostEstimate(flops=flops, bytes_accessed=flops // 400, transcendentals=0),
     )
 
 
@@ -193,13 +188,20 @@
     scale = relative(prob)
     core = lax.axis_index("core").astype(jnp.int32).reshape(1)
     xs = gather_group(tokens)
-    ds = gather_group(cotangent)
+    pair = jnp.stack([cotangent, send(cotangent, "zhi", 1)])
+    ds = [pair, *sends([pair] * 3, "y")]
     wg2, wu2 = (w.reshape(EXP * width, ff) for w in (w_gate, w_up))
     wd2 = w_down.reshape(wide, width)
     pieces = [whole(sds((2, block, width), t)) for t in (F32, BF16, BF16, BF16)]
 
-    def grads(columns):
-        return [tiled(sds((4, 4, own_rows, columns), t), 1, 1) for t in (F32, BF16)]
+    def run(kernel, ins, outs, flops, *scalars):
+        return call(kernel, 4, ins, outs, flops, len(scalars))(*scalars, *(a for *_, a in ins))
+
+    def outer(left, right, cost):
+        columns = right.shape[1]
+        outs = [tiled(sds((4, 4, own_rows, columns), BF16), 1, 1)] * 2
+        own, other = run(outer_kernel, [tiled(left, 1, TILE), whole(right)], outs, cost, core)
+        return own, send(other, "core", 1)
 
     ins = [whole(a) for a in (second, *xs, wg2, wu2, wd2)]
     outs = [
@@ -209,27 +211,45 @@
         tiled(sds((rows, ff), F32), 0, TILE),
         *pieces,
     ]
-    x, hh, act, silu, *out_pieces = call(forward_kernel, steps, ins, outs, 3 * unit)(*(a for *_, a in ins))
-
-    ins = [whole(a) for a in (scale, *ds, hh)]
-    outs = [whole(sds((rows, width), BF16)), *grads(wide)]
-    dout, *down = call(down_kernel, 4, ins, outs, unit, 1)(core, *(a for *_, a in ins))
-
-    ins = [tiled(second, 0, TILE), tiled(dout, 0, TILE), whole(wd2), tiled(act, 0, TILE), tiled(silu, 0, TILE)]
-    outs = [tiled(sds((rows, 2 * wide), BF16), 0, TILE)]
-    (gu,) = call(back_kernel, steps, ins, outs, unit)(*(a for *_, a in ins))
-
-    ins = [tiled(x, 1, TILE), whole(gu)]
-    gate_up = call(weight_kernel, 4, ins, grads(2 * wide), 2 * unit, 1)(core, *(a for *_, a in ins))
-
-    gu, gate_up = lax.optimization_barrier((gu, gate_up))
+    x, hh, act, silu, out, *out_y = run(forward_kernel, ins, outs, 3 * unit)
+    ds, out_y = tie(ds, out_y)
+    out_y = sends(out_y, "y", -1)
+
+    ins = [tiled(second, 0, TILE), whole(scale), *(whole(a) for a in ds)]
+    ins += [tiled(act, 0, TILE), tiled(silu, 0, TILE), whole(wd2)]
+    outs = [whole(sds((rows, width), BF16)), tiled(sds((rows, 2 * wide), BF16), 0, TILE)]
+    dout, gu = run(back_kernel, ins, outs, unit // 20)
+    both, both_c = outer(x, gu, unit // 10)
+    out, out_y, both, dout = tie(out, out_y, both, dout)
+    out = add(out, out_y)
+    out, dout, both = tie(out, dout, both)
+    far_out = send(out[1].astype(BF16), "zhi", 1)
+    down, down_c = outer(dout, hh, 8 * unit)
+    down, both_c, gu, both = tie(down, both_c, gu, both)
+    both, both_x = pick(add(both.astype(F32), [both_c]), "x")
+    gu, both, both_x = tie(gu, both, both_x)
+    both_x = sends(both_x, "x")
+
     ins = [tiled(gu, 0, TILE), whole(w_gate), whole(w_up)]
-    in_pieces = call(input_kernel, steps, ins, pieces, 2 * unit)(*(a for *_, a in ins))
-
-    output = scatter_group(*out_pieces) * scale[:block]
-    grad_down = scatter_rows(*down).reshape(own_rows, EXP, ff)
-    both = scatter_rows(*gate_up).reshape(own_rows, 2, EXP, ff)
-    input_grad = scatter_group(*in_pieces)
+    near, *in_y = run(input_kernel, ins, pieces, 8 * unit)
+    near, in_y, down_c, far_out, both_x[0], both_x[2] = tie(near, in_y, down_c, far_out, both_x[0], both_x[2])
+    in_y = sends(in_y, "y", -1)
+    down, down_x = pick(add(down.astype(F32), [down_c]), "x")
+    output = ((out[0] + far_out.astype(F32)) * scale[:block]).astype(BF16)
+    down, down_x, both, both_x, output = tie(down, down_x, both, both_x, output)
+    down_x = sends(down_x, "x")
+    both, both_z = pick(add(both, both_x), "zlo")
+    both, both_z, near, in_y = tie(both, both_z, near, in_y)
+    both_z = sends(both_z, "zlo")
+    near = add(near, in_y)
+    down_x[0], near, down = tie(down_x[0], near, down)
+    far = send(near[1].astype(BF16), "zhi", 1)
+    down, down_z = pick(add(down, down_x), "zlo")
+    down, down_z, both, both_z = tie(down, down_z, both, both_z)
+    down_z = sends(down_z, "zlo")
+    both = add(both, both_z).reshape(own_rows, 2, EXP, ff)
+    input_grad = near[0] + far.astype(F32)
+    grad_down = add(down, down_z).reshape(own_rows, EXP, ff)
     return (
         output.astype(BF16),
         input_grad.astype(BF16),

time: 193 us -> 194 us (level); the launches traced: 189 us -> 192 us
  waiting for transfers between devices: 47.6 us -> 63.2 us
  starting transfers between devices: 81.2 us -> 68.5 us
  other arithmetic: 3.91 us -> 5.93 us
    ppermute x36 -> x33, waiting for transfers between devices: 47.6 us -> 63.2 us  [send(): return lax.ppermute(value, axis, [(i, (i + step) % n) for i in range(n)])]
    ppermute x36 -> x33, starting transfers between devices: 81.2 us -> 68.5 us  [send(): return lax.ppermute(value, axis, [(i, (i + step) % n) for i in range(n)])]
  transfers between devices with their start and end apart: 36 -> 33, of which waited for: 8 -> 14; matrix products, arithmetic and copies ran while one was open for 5% -> 5% of each run, Pallas kernels for 26% -> 25%
where the time goes in v4:
time: 194 us; the launch traced here: 192 us
  starting transfers between devices  68.5 us (35%)
  waiting for transfers between devices  63.2 us (33%)
  Pallas kernels  48.3 us (25%)
  other arithmetic  5.93 us (3%)
  local copies, waits for them, and re-layouts  5.26 us (3%)
    ppermute x33, starting transfers between devices, send(): return lax.ppermute(value, axis, [(i, (i + step) % n) for i in range(n)])  68.5 us
    ppermute x33, waiting for transfers between devices, send(): return lax.ppermute(value, axis, [(i, (i + step) % n) for i in range(n)])  63.2 us
    pallas_call x5, Pallas kernels, run(): call(kernel, 4, ins, outs, flops, len(scalars))  48.3 us
  transfers between devices with their start and end apart: 33, of which 14 were waited for; matrix products, arithmetic and copies ran while one was open for 5% of the time, Pallas kernels for 25%

profile of v4, /device:TPU:6, one launch (start us, length us, event | category | flops | bytes accessed | tf_op | source)
XLA Modules:
  0.0 192.3 jit_solution(2706599692218829420)
XLA Ops:
  0.6 7.3 %collective-permute-start.3 = (bf16[128,1024]{1,0:T(8,128)(2,1)}, bf16[128,1024]{1,0:T(8,128)(2,1)S(1)}, u32[]{:S(2)}, u32[]{:S(2)}) collective-permute-start(bf16[128,1024]{1,0:T(8,128)(2,1)} %refs_0_.1), channel_id=1, source_target_pairs={{0,4},{4,0},{1,5},{5,1},{2,6},{6,2},{3,7},{7,3},{8,12},{12,8},{9,1... | collective-permute-start | bytes 786440 | tf_op jit(solution)/shard_map/ppermute | solution.py:17
  9.6 2.9 %collective-permute-start.1 = (bf16[128,1024]{1,0:T(8,128)(2,1)}, bf16[128,1024]{1,0:T(8,128)(2,1)S(1)}, u32[]{:S(2)}, u32[]{:S(2)}) collective-permute-start(bf16[128,1024]{1,0:T(8,128)(2,1)} %refs_0_.1), channel_id=1, source_target_pairs={{0,2},{1,3},{2,0},{3,1},{4,6},{5,7},{6,4},{7,5},{8,10},{9,11},{10,... | collective-permute-start | bytes 786440 | tf_op jit(solution)/shard_map/ppermute | solution.py:17
  13.8 2.2 %collective-permute-done.3.refs_4_ = bf16[128,1024]{1,0:T(8,128)(2,1)S(1)} collective-permute-done((bf16[128,1024]{1,0:T(8,128)(2,1)}, bf16[128,1024]{1,0:T(8,128)(2,1)S(1)}, u32[]{:S(2)}, u32[]{:S(2)}) %collective-permute-start.3) | collective-permute-done | bytes 262176 | tf_op jit(solution)/shard_map/ppermute | solution.py:17
  17.6 5.7 %collective-permute-start.5 = (bf16[128,1024]{1,0:T(8,128)(2,1)S(1)}, bf16[128,1024]{1,0:T(8,128)(2,1)}, u32[]{:S(2)}, u32[]{:S(2)}) collective-permute-start(bf16[128,1024]{1,0:T(8,128)(2,1)S(1)} %collective-permute-done.3.refs_4_), channel_id=1, source_target_pairs={{0,2},{1,3},{2,0},{3,1},{4,6},{5,7},{6,4},{7,5},{8,10},{9,11},{10,... | collective-permute-start | bytes 786440 | tf_op jit(solution)/shard_map/ppermute | solution.py:17
  31.8 5.1 %collective-permute-done.5.refs_6_ = bf16[128,1024]{1,0:T(8,128)(2,1)} collective-permute-done((bf16[128,1024]{1,0:T(8,128)(2,1)S(1)}, bf16[128,1024]{1,0:T(8,128)(2,1)}, u32[]{:S(2)}, u32[]{:S(2)}) %collective-permute-start.5) | collective-permute-done | bytes 262176 | tf_op jit(solution)/shard_map/ppermute | solution.py:17
  36.9 15.1 %shard_map.110 = (bf16[1024,1024]{1,0:T(8,128)(2,1)}, bf16[1024,1024]{1,0:T(8,128)(2,1)}, f32[1024,512]{1,0:T(8,128)}, f32[1024,512]{1,0:T(8,128)}, f32[2,128,10...) custom-call(s32[1024,1]{1,0:T(8,128)} %copy.15.second_ref, ...), custom_call_target="tpu_custom_call" | custom-call | flops 6442450944 | bytes 16106127 | tf_op jit(solution)/shard_map/pallas_call | solution.py:198
  52.0 5.7 %collective-permute-done.9.refs_2_ = bf16[2,128,1024]{2,1,0:T(8,128)(2,1)S(1)} collective-permute-done((bf16[2,128,1024]{2,1,0:T(8,128)(2,1)S(1)}, bf16[2,128,1024]{2,1,0:T(8,128)(2,1)S(1)}, u32[]{:S(2)}, u32[]{:S(2)}) %collective-permute-start.9) | collective-permute-done | bytes 524320 | tf_op jit(solution)/shard_map/ppermute | solution.py:17
  57.7 2.3 %collective-permute-start.11 = (bf16[2,128,1024]{2,1,0:T(8,128)(2,1)}, bf16[2,128,1024]{2,1,0:T(8,128)(2,1)S(1)}, u32[]{:S(2)}, u32[]{:S(2)}) collective-permute-start(bf16[2,128,1024]{2,1,0:T(8,128)(2,1)} %get-tuple-element.88), channel_id=1, source_target_pairs={{0,3},{1,0},{2,1},{3,2},{4,7},{5,4},{6,5},{7,6},{8,11},{9,8},{10,9... | collective-permute-start | bytes 1572872 | tf_op jit(solution)/shard_map/ppermute | solution.py:17
  63.0 8.5 %shard_map.111 = (bf16[1024,1024]{1,0:T(8,128)(2,1)}, bf16[1024,2048]{1,0:T(8,128)(2,1)}) custom-call(s32[1024,1]{1,0:T(8,128)} %copy.15.second_ref, f32[1024,1]{1,0:T(8,128)} %copy.17.scale_ref, bf16[2,128,1024]{2,1,0:T(8,128)(2,1)} %copy-done, bf16[2,128,1024]{2,1,0:T(8,128)(2,1)} %copy-done.6, bf16[2,128,1024]{2,1,0:T(8,128)(2,1)} %copy-done.7, ...), custom_call_target="tpu_custom_call" | custom-call | flops 107374184 | bytes 268435 | tf_op jit(solution)/shard_map/pallas_call | solution.py:198
  71.5 8.8 %shard_map.112 = (bf16[4,4,32,2048]{3,2,1,0:T(8,128)(2,1)}, bf16[4,4,32,2048]{3,2,1,0:T(8,128)(2,1)}) custom-call(s32[1]{0:T(128)} %bitcast.core_ref, bf16[1024,1024]{1,0:T(8,128)(2,1)} %get-tuple-element.91.left, bf16[1024,2048]{1,0:T(8,128)(2,1)} %get-tuple-element.116.right.gu), custom_call_target="tpu_custom_call" | custom-call | flops 214748368 | bytes 536870 | tf_op jit(solution)/shard_map/pallas_call | solution.py:198
  81.5 3.7 %collective-permute-done.13 = bf16[2,128,1024]{2,1,0:T(8,128)(2,1)} collective-permute-done((bf16[2,128,1024]{2,1,0:T(8,128)(2,1)}, bf16[2,128,1024]{2,1,0:T(8,128)(2,1)}, u32[]{:S(2)}, u32[]{:S(2)}) %collective-permute-start.13) | collective-permute-done | bytes 524320 | tf_op jit(solution)/shard_map/ppermute | solution.py:17
  86.5 6.3 %shard_map.113 = (bf16[4,4,32,1024]{3,2,1,0:T(8,128)(2,1)}, bf16[4,4,32,1024]{3,2,1,0:T(8,128)(2,1)}) custom-call(s32[1]{0:T(128)} %bitcast.core_ref, bf16[1024,1024]{1,0:T(8,128)(2,1)} %get-tuple-element.107.left, bf16[1024,1024]{1,0:T(8,128)(2,1)} %get-tuple-element.108.right), custom_call_target="tpu_custom_call" | custom-call | flops 17179869184 | bytes 42949672 | tf_op jit(solution)/shard_map/pallas_call | solution.py:198
  92.9 4.7 %collective-permute-start.16 = (bf16[128,1024]{1,0:T(8,128)(2,1)S(1)}, bf16[128,1024]{1,0:T(8,128)(2,1)S(1)}, u32[]{:S(2)}, u32[]{:S(2)}) collective-permute-start(bf16[128,1024]{1,0:T(8,128)(2,1)S(1)} %fusion.9), channel_id=1, source_target_pairs={{0,4},{4,0},{1,5},{5,1},{2,6},{6,2},{3,7},{7,3},{8,12},{12,8},{9,1... | collective-permute-start | bytes 786440 | tf_op jit(solution)/shard_map/ppermute | solution.py:17
  100.8 9.5 %shard_map.114 = (f32[2,128,1024]{2,1,0:T(8,128)}, bf16[2,128,1024]{2,1,0:T(8,128)(2,1)}, bf16[2,128,1024]{2,1,0:T(8,128)(2,1)}, bf16[2,128,1024]{2,1,0:T(8,128)(2,1)}) custom-call(bf16[1024,2048]{1,0:T(8,128)(2,1)} %get-tuple-element.116.right.gu, bf16[2,1024,512]{2,1,0:T(8,128)(2,1)} %wg.1, bf16[2,1024,512]{2,1,0:T(8,128)(2,1)} %wu.1), custom_call_target="tpu_custom_call" | custom-call | flops 17179869184 | bytes 42949672 | tf_op jit(solution)/shard_map/pallas_call | solution.py:198
  112.3 12.6 %collective-permute-done.18 = bf16[4,32,2048]{2,1,0:T(8,128)(2,1)S(1)} collective-permute-done((bf16[4,32,2048]{2,1,0:T(8,128)(2,1)S(1)}, bf16[4,32,2048]{2,1,0:T(8,128)(2,1)S(1)}, u32[]{:S(2)}, u32[]{:S(2)}) %collective-permute-start.18) | collective-permute-done | bytes 524320 | tf_op jit(solution)/shard_map/ppermute | solution.py:17
  126.5 3.3 %collective-permute-start.21 = (bf16[2,128,1024]{2,1,0:T(8,128)(2,1)S(1)}, bf16[2,128,1024]{2,1,0:T(8,128)(2,1)S(1)}, u32[]{:S(2)}, u32[]{:S(2)}) collective-permute-start(bf16[2,128,1024]{2,1,0:T(8,128)(2,1)S(1)} %copy-done.11), channel_id=1, source_target_pairs={{0,3},{1,0},{2,1},{3,2},{4,7},{5,4},{6,5},{7,6},{8,11},{9,8},{10,9... | collective-permute-start | bytes 1572872 | tf_op jit(solution)/shard_map/ppermute | solution.py:17
  132.3 16.7 %collective-permute-done.21 = bf16[2,128,1024]{2,1,0:T(8,128)(2,1)S(1)} collective-permute-done((bf16[2,128,1024]{2,1,0:T(8,128)(2,1)S(1)}, bf16[2,128,1024]{2,1,0:T(8,128)(2,1)S(1)}, u32[]{:S(2)}, u32[]{:S(2)}) %collective-permute-start.21) | collective-permute-done | bytes 524320 | tf_op jit(solution)/shard_map/ppermute | solution.py:17
  149.8 2.8 %collective-permute-done.23 = bf16[2,128,1024]{2,1,0:T(8,128)(2,1)S(1)} collective-permute-done((bf16[2,128,1024]{2,1,0:T(8,128)(2,1)S(1)}, bf16[2,128,1024]{2,1,0:T(8,128)(2,1)S(1)}, u32[]{:S(2)}, u32[]{:S(2)}) %collective-permute-start.23) | collective-permute-done | bytes 524320 | tf_op jit(solution)/shard_map/ppermute | solution.py:17
  152.9 4.9 %collective-permute-start.27 = (bf16[32,2048]{1,0:T(8,128)(2,1)S(1)}, bf16[32,2048]{1,0:T(8,128)(2,1)S(1)}, u32[]{:S(2)}, u32[]{:S(2)}) collective-permute-start(bf16[32,2048]{1,0:T(8,128)(2,1)S(1)} %get-tuple-element.152), channel_id=1, source_target_pairs={{0,64},{64,128},{128,192},{192,0},{1,65},{65,129},{129,193},{193,1... | collective-permute-start | bytes 393224 | tf_op jit(solution)/shard_map/ppermute | solution.py:17
  159.5 2.8 %collective-permute-start.29 = (bf16[32,2048]{1,0:T(8,128)(2,1)S(1)}, bf16[32,2048]{1,0:T(8,128)(2,1)S(1)}, u32[]{:S(2)}, u32[]{:S(2)}) collective-permute-start(bf16[32,2048]{1,0:T(8,128)(2,1)S(1)} %get-tuple-element.154), channel_id=1, source_target_pairs={{0,192},{64,0},{128,64},{192,128},{1,193},{65,1},{129,65},{193,129... | collective-permute-start | bytes 393224 | tf_op jit(solution)/shard_map/ppermute | solution.py:17
  163.5 6.3 %collective-permute-done.28 = bf16[32,2048]{1,0:T(8,128)(2,1)S(1)} collective-permute-done((bf16[32,2048]{1,0:T(8,128)(2,1)S(1)}, bf16[32,2048]{1,0:T(8,128)(2,1)S(1)}, u32[]{:S(2)}, u32[]{:S(2)}) %collective-permute-start.28) | collective-permute-done | bytes 131104 | tf_op jit(solution)/shard_map/ppermute | solution.py:17
  169.8 3.0 %collective-permute-done.29 = bf16[32,2048]{1,0:T(8,128)(2,1)S(1)} collective-permute-done((bf16[32,2048]{1,0:T(8,128)(2,1)S(1)}, bf16[32,2048]{1,0:T(8,128)(2,1)S(1)}, u32[]{:S(2)}, u32[]{:S(2)}) %collective-permute-start.29) | collective-permute-done | bytes 131104 | tf_op jit(solution)/shard_map/ppermute | solution.py:17
  172.8 10.1 %collective-permute-start.30 = (bf16[32,1024]{1,0:T(8,128)(2,1)S(1)}, bf16[32,1024]{1,0:T(8,128)(2,1)S(1)}, u32[]{:S(2)}, u32[]{:S(2)}) collective-permute-start(bf16[32,1024]{1,0:T(8,128)(2,1)S(1)} %get-tuple-element.160), channel_id=1, source_target_pairs={{0,64},{64,128},{128,192},{192,0},{1,65},{65,129},{129,193},{193,1... | collective-permute-start | bytes 196616 | tf_op jit(solution)/shard_map/ppermute | solution.py:17
  182.9 3.4 %collective-permute-start.31 = (bf16[32,1024]{1,0:T(8,128)(2,1)S(1)}, bf16[32,1024]{1,0:T(8,128)(2,1)S(1)}, u32[]{:S(2)}, u32[]{:S(2)}) collective-permute-start(bf16[32,1024]{1,0:T(8,128)(2,1)S(1)} %get-tuple-element.161), channel_id=1, source_target_pairs={{0,128},{64,192},{128,0},{192,64},{1,129},{65,193},{129,1},{193,65... | collective-permute-start | bytes 196616 | tf_op jit(solution)/shard_map/ppermute | solution.py:17
  (115 shorter events, 37.6 us)
Async XLA Ops:
  0.6 15.4 %collective-permute-start.3 = (bf16[128,1024]{1,0:T(8,128)(2,1)}, bf16[128,1024]{1,0:T(8,128)(2,1)S(1)}, u32[]{:S(2)}, u32[]{:S(2)}) collective-permute-start(bf16[128,1024]{1,0:T(8,128)(2,1)} %refs_0_.1), channel_id=1, source_target_pairs={{0,4},{4,0},{1,5},{5,1},{2,6},{6,2},{3,7},{7,3},{8,12},{12,8},{9,1... | collective-permute-start | bytes 786440 | tf_op jit(solution)/shard_map/ppermute | solution.py:17
  9.5 13.8 %collective-permute-start.7 = (bf16[128,1024]{1,0:T(8,128)(2,1)}, bf16[128,1024]{1,0:T(8,128)(2,1)S(1)}, u32[]{:S(2)}, u32[]{:S(2)}) collective-permute-start(bf16[128,1024]{1,0:T(8,128)(2,1)} %param.8), channel_id=1, source_target_pairs={{0,4},{4,0},{1,5},{5,1},{2,6},{6,2},{3,7},{7,3},{8,12},{12,8},{9,1... | collective-permute-start | bytes 786440 | tf_op jit(solution)/shard_map/ppermute | solution.py:17
  9.6 18.5 %collective-permute-start.1 = (bf16[128,1024]{1,0:T(8,128)(2,1)}, bf16[128,1024]{1,0:T(8,128)(2,1)S(1)}, u32[]{:S(2)}, u32[]{:S(2)}) collective-permute-start(bf16[128,1024]{1,0:T(8,128)(2,1)} %refs_0_.1), channel_id=1, source_target_pairs={{0,2},{1,3},{2,0},{3,1},{4,6},{5,7},{6,4},{7,5},{8,10},{9,11},{10,... | collective-permute-start | bytes 786440 | tf_op jit(solution)/shard_map/ppermute | solution.py:17
  12.5 16.5 %collective-permute-start.2 = (bf16[128,1024]{1,0:T(8,128)(2,1)}, bf16[128,1024]{1,0:T(8,128)(2,1)S(1)}, u32[]{:S(2)}, u32[]{:S(2)}) collective-permute-start(bf16[128,1024]{1,0:T(8,128)(2,1)} %refs_0_.1), channel_id=1, source_target_pairs={{0,3},{1,0},{2,1},{3,2},{4,7},{5,4},{6,5},{7,6},{8,11},{9,8},{10,9... | collective-permute-start | bytes 786440 | tf_op jit(solution)/shard_map/ppermute | solution.py:17
  16.0 14.2 %collective-permute-start.4 = (bf16[128,1024]{1,0:T(8,128)(2,1)S(1)}, bf16[128,1024]{1,0:T(8,128)(2,1)S(1)}, u32[]{:S(2)}, u32[]{:S(2)}) collective-permute-start(bf16[128,1024]{1,0:T(8,128)(2,1)S(1)} %collective-permute-done.3.refs_4_), channel_id=1, source_target_pairs={{0,1},{1,2},{2,3},{3,0},{4,5},{5,6},{6,7},{7,4},{8,9},{9,10},{10,1... | collective-permute-start | bytes 786440 | tf_op jit(solution)/shard_map/ppermute | solution.py:17
  17.6 19.3 %collective-permute-start.5 = (bf16[128,1024]{1,0:T(8,128)(2,1)S(1)}, bf16[128,1024]{1,0:T(8,128)(2,1)}, u32[]{:S(2)}, u32[]{:S(2)}) collective-permute-start(bf16[128,1024]{1,0:T(8,128)(2,1)S(1)} %collective-permute-done.3.refs_4_), channel_id=1, source_target_pairs={{0,2},{1,3},{2,0},{3,1},{4,6},{5,7},{6,4},{7,5},{8,10},{9,11},{10,... | collective-permute-start | bytes 786440 | tf_op jit(solution)/shard_map/ppermute | solution.py:17
  28.1 23.9 %collective-permute-start.10 = (bf16[2,128,1024]{2,1,0:T(8,128)(2,1)S(1)}, bf16[2,128,1024]{2,1,0:T(8,128)(2,1)S(1)}, u32[]{:S(2)}, u32[]{:S(2)}) collective-permute-start(bf16[2,128,1024]{2,1,0:T(8,128)(2,1)S(1)} %pad_maximum_fusion.refs_0_), channel_id=1, source_target_pairs={{0,3},{1,0},{2,1},{3,2},{4,7},{5,4},{6,5},{7,6},{8,11},{9,8},{10,9... | collective-permute-start | bytes 1572872 | tf_op jit(solution)/shard_map/ppermute | solution.py:17
  28.9 23.1 %collective-permute-start.8 = (bf16[2,128,1024]{2,1,0:T(8,128)(2,1)S(1)}, bf16[2,128,1024]{2,1,0:T(8,128)(2,1)S(1)}, u32[]{:S(2)}, u32[]{:S(2)}) collective-permute-start(bf16[2,128,1024]{2,1,0:T(8,128)(2,1)S(1)} %pad_maximum_fusion.refs_0_), channel_id=1, source_target_pairs={{0,1},{1,2},{2,3},{3,0},{4,5},{5,6},{6,7},{7,4},{8,9},{9,10},{10,1... | collective-permute-start | bytes 1572872 | tf_op jit(solution)/shard_map/ppermute | solution.py:17
  30.2 27.5 %collective-permute-start.9 = (bf16[2,128,1024]{2,1,0:T(8,128)(2,1)S(1)}, bf16[2,128,1024]{2,1,0:T(8,128)(2,1)S(1)}, u32[]{:S(2)}, u32[]{:S(2)}) collective-permute-start(bf16[2,128,1024]{2,1,0:T(8,128)(2,1)S(1)} %pad_maximum_fusion.refs_0_), channel_id=1, source_target_pairs={{0,2},{1,3},{2,0},{3,1},{4,6},{5,7},{6,4},{7,5},{8,10},{9,11},{10,... | collective-permute-start | bytes 1572872 | tf_op jit(solution)/shard_map/ppermute | solution.py:17
  57.7 23.7 %collective-permute-start.11 = (bf16[2,128,1024]{2,1,0:T(8,128)(2,1)}, bf16[2,128,1024]{2,1,0:T(8,128)(2,1)S(1)}, u32[]{:S(2)}, u32[]{:S(2)}) collective-permute-start(bf16[2,128,1024]{2,1,0:T(8,128)(2,1)} %get-tuple-element.88), channel_id=1, source_target_pairs={{0,3},{1,0},{2,1},{3,2},{4,7},{5,4},{6,5},{7,6},{8,11},{9,8},{10,9... | collective-permute-start | bytes 1572872 | tf_op jit(solution)/shard_map/ppermute | solution.py:17
  60.0 21.4 %collective-permute-start.12 = (bf16[2,128,1024]{2,1,0:T(8,128)(2,1)}, bf16[2,128,1024]{2,1,0:T(8,128)(2,1)S(1)}, u32[]{:S(2)}, u32[]{:S(2)}) collective-permute-start(bf16[2,128,1024]{2,1,0:T(8,128)(2,1)} %get-tuple-element.89), channel_id=1, source_target_pairs={{0,2},{1,3},{2,0},{3,1},{4,6},{5,7},{6,4},{7,5},{8,10},{9,11},{10,... | collective-permute-start | bytes 1572872 | tf_op jit(solution)/shard_map/ppermute | solution.py:17
  61.8 23.3 %collective-permute-start.13 = (bf16[2,128,1024]{2,1,0:T(8,128)(2,1)}, bf16[2,128,1024]{2,1,0:T(8,128)(2,1)}, u32[]{:S(2)}, u32[]{:S(2)}) collective-permute-start(bf16[2,128,1024]{2,1,0:T(8,128)(2,1)} %get-tuple-element.90), channel_id=1, source_target_pairs={{0,1},{1,2},{2,3},{3,0},{4,5},{5,6},{6,7},{7,4},{8,9},{9,10},{10,1... | collective-permute-start | bytes 1572872 | tf_op jit(solution)/shard_map/ppermute | solution.py:17
  80.3 17.2 %collective-permute-start.14 = (bf16[4,4,32,2048]{3,2,1,0:T(8,128)(2,1)}, bf16[4,4,32,2048]{3,2,1,0:T(8,128)(2,1)S(1)}, u32[]{:S(2)}, u32[]{:S(2)}) collective-permute-start(bf16[4,4,32,2048]{3,2,1,0:T(8,128)(2,1)} %get-tuple-element.110), channel_id=1, source_target_pairs={{0,8},{8,0},{1,9},{9,1},{2,10},{10,2},{3,11},{11,3},{4,12},{12,4},... | collective-permute-start | bytes 6291464 | tf_op jit(solution)/shard_map/ppermute | solution.py:17
  92.8 18.9 %collective-permute-start.15 = (bf16[4,4,32,1024]{3,2,1,0:T(8,128)(2,1)}, bf16[4,4,32,1024]{3,2,1,0:T(8,128)(2,1)S(1)}, u32[]{:S(2)}, u32[]{:S(2)}) collective-permute-start(bf16[4,4,32,1024]{3,2,1,0:T(8,128)(2,1)} %get-tuple-element.121), channel_id=1, source_target_pairs={{0,8},{8,0},{1,9},{9,1},{2,10},{10,2},{3,11},{11,3},{4,12},{12,4},... | collective-permute-start | bytes 3145736 | tf_op jit(solution)/shard_map/ppermute | solution.py:17
  92.9 18.9 %collective-permute-start.16 = (bf16[128,1024]{1,0:T(8,128)(2,1)S(1)}, bf16[128,1024]{1,0:T(8,128)(2,1)S(1)}, u32[]{:S(2)}, u32[]{:S(2)}) collective-permute-start(bf16[128,1024]{1,0:T(8,128)(2,1)S(1)} %fusion.9), channel_id=1, source_target_pairs={{0,4},{4,0},{1,5},{5,1},{2,6},{6,2},{3,7},{7,3},{8,12},{12,8},{9,1... | collective-permute-start | bytes 786440 | tf_op jit(solution)/shard_map/ppermute | solution.py:17
  99.3 25.7 %collective-permute-start.18 = (bf16[4,32,2048]{2,1,0:T(8,128)(2,1)S(1)}, bf16[4,32,2048]{2,1,0:T(8,128)(2,1)S(1)}, u32[]{:S(2)}, u32[]{:S(2)}) collective-permute-start(bf16[4,32,2048]{2,1,0:T(8,128)(2,1)S(1)} %get-tuple-element.124), channel_id=1, source_target_pairs={{0,48},{16,0},{32,16},{48,32},{1,49},{17,1},{33,17},{49,33},{2,50}... | collective-permute-start | bytes 1572872 | tf_op jit(solution)/shard_map/ppermute | solution.py:17
  110.4 16.0 %collective-permute-start.19 = (bf16[4,32,2048]{2,1,0:T(8,128)(2,1)S(1)}, bf16[4,32,2048]{2,1,0:T(8,128)(2,1)S(1)}, u32[]{:S(2)}, u32[]{:S(2)}) collective-permute-start(bf16[4,32,2048]{2,1,0:T(8,128)(2,1)S(1)} %get-tuple-element.128), channel_id=1, source_target_pairs={{0,32},{16,48},{32,0},{48,16},{1,33},{17,49},{33,1},{49,17},{2,34}... | collective-permute-start | bytes 1572872 | tf_op jit(solution)/shard_map/ppermute | solution.py:17
  126.5 22.6 %collective-permute-start.21 = (bf16[2,128,1024]{2,1,0:T(8,128)(2,1)S(1)}, bf16[2,128,1024]{2,1,0:T(8,128)(2,1)S(1)}, u32[]{:S(2)}, u32[]{:S(2)}) collective-permute-start(bf16[2,128,1024]{2,1,0:T(8,128)(2,1)S(1)} %copy-done.11), channel_id=1, source_target_pairs={{0,3},{1,0},{2,1},{3,2},{4,7},{5,4},{6,5},{7,6},{8,11},{9,8},{10,9... | collective-permute-start | bytes 1572872 | tf_op jit(solution)/shard_map/ppermute | solution.py:17
  129.7 20.0 %collective-permute-start.22 = (bf16[2,128,1024]{2,1,0:T(8,128)(2,1)S(1)}, bf16[2,128,1024]{2,1,0:T(8,128)(2,1)S(1)}, u32[]{:S(2)}, u32[]{:S(2)}) collective-permute-start(bf16[2,128,1024]{2,1,0:T(8,128)(2,1)S(1)} %copy-done.10), channel_id=1, source_target_pairs={{0,2},{1,3},{2,0},{3,1},{4,6},{5,7},{6,4},{7,5},{8,10},{9,11},{10,... | collective-permute-start | bytes 1572872 | tf_op jit(solution)/shard_map/ppermute | solution.py:17
  129.7 22.8 %collective-permute-start.23 = (bf16[2,128,1024]{2,1,0:T(8,128)(2,1)S(1)}, bf16[2,128,1024]{2,1,0:T(8,128)(2,1)S(1)}, u32[]{:S(2)}, u32[]{:S(2)}) collective-permute-start(bf16[2,128,1024]{2,1,0:T(8,128)(2,1)S(1)} %copy-done.9), channel_id=1, source_target_pairs={{0,1},{1,2},{2,3},{3,0},{4,5},{5,6},{6,7},{7,4},{8,9},{9,10},{10,1... | collective-permute-start | bytes 1572872 | tf_op jit(solution)/shard_map/ppermute | solution.py:17
  130.7 22.1 %collective-permute-start.20 = (bf16[4,32,1024]{2,1,0:T(8,128)(2,1)S(1)}, bf16[4,32,1024]{2,1,0:T(8,128)(2,1)S(1)}, u32[]{:S(2)}, u32[]{:S(2)}) collective-permute-start(bf16[4,32,1024]{2,1,0:T(8,128)(2,1)S(1)} %get-tuple-element.132), channel_id=1, source_target_pairs={{0,16},{16,32},{32,48},{48,0},{1,17},{17,33},{33,49},{49,1},{2,18}... | collective-permute-start | bytes 786440 | tf_op jit(solution)/shard_map/ppermute | solution.py:17
  130.8 31.6 %collective-permute-start.25 = (bf16[4,32,1024]{2,1,0:T(8,128)(2,1)S(1)}, bf16[4,32,1024]{2,1,0:T(8,128)(2,1)S(1)}, u32[]{:S(2)}, u32[]{:S(2)}) collective-permute-start(bf16[4,32,1024]{2,1,0:T(8,128)(2,1)S(1)} %get-tuple-element.149), channel_id=1, source_target_pairs={{0,32},{16,48},{32,0},{48,16},{1,33},{17,49},{33,1},{49,17},{2,34}... | collective-permute-start | bytes 786440 | tf_op jit(solution)/shard_map/ppermute | solution.py:17
  162.5 29.0 %collective-permute-start.24 = (bf16[128,1024]{1,0:T(8,128)(2,1)S(1)}, bf16[128,1024]{1,0:T(8,128)(2,1)S(1)}, u32[]{:S(2)}, u32[]{:S(2)}) collective-permute-start(bf16[128,1024]{1,0:T(8,128)(2,1)S(1)} %fusion.10), channel_id=1, source_target_pairs={{0,4},{4,0},{1,5},{5,1},{2,6},{6,2},{3,7},{7,3},{8,12},{12,8},{9,1... | collective-permute-start | bytes 786440 | tf_op jit(solution)/shard_map/ppermute | solution.py:17
  172.8 15.5 %collective-permute-start.30 = (bf16[32,1024]{1,0:T(8,128)(2,1)S(1)}, bf16[32,1024]{1,0:T(8,128)(2,1)S(1)}, u32[]{:S(2)}, u32[]{:S(2)}) collective-permute-start(bf16[32,1024]{1,0:T(8,128)(2,1)S(1)} %get-tuple-element.160), channel_id=1, source_target_pairs={{0,64},{64,128},{128,192},{192,0},{1,65},{65,129},{129,193},{193,1... | collective-permute-start | bytes 196616 | tf_op jit(solution)/shard_map/ppermute | solution.py:17
  (26 other events, 324.4 us)

commit v5 on v4

--- a/solution.py
+++ b/solution.py
@@ -35,6 +35,10 @@
 
 def tie(*values):
     return lax.optimization_barrier(values)
+
+
+def exchange(value, axis):
+    return lax.all_to_all(value, axis, 0, 0, tiled=True)
 
 
 def sends(pieces, axis, way=1):
@@ -235,21 +239,17 @@
     near, in_y, down_c, far_out, both_x[0], both_x[2] = tie(near, in_y, down_c, far_out, both_x[0], both_x[2])
     in_y = sends(in_y, "y", -1)
     down, down_x = pick(add(down.astype(F32), [down_c]), "x")
-    output = ((out[0] + far_out.astype(F32)) * scale[:block]).astype(BF16)
-    down, down_x, both, both_x, output = tie(down, down_x, both, both_x, output)
+    output = (out[0] + far_out.astype(F32)) * scale[:block]
+    down, down_x, both, both_x, output, in_y[0], in_y[2] = tie(down, down_x, both, both_x, output, in_y[0], in_y[2])
     down_x = sends(down_x, "x")
-    both, both_z = pick(add(both, both_x), "zlo")
-    both, both_z, near, in_y = tie(both, both_z, near, in_y)
-    both_z = sends(both_z, "zlo")
+    both = exchange(add(both, both_x).astype(BF16), "zlo")
+    down, down_x, both, near, in_y[1] = tie(down, down_x, both, near, in_y[1])
     near = add(near, in_y)
-    down_x[0], near, down = tie(down_x[0], near, down)
     far = send(near[1].astype(BF16), "zhi", 1)
-    down, down_z = pick(add(down, down_x), "zlo")
-    down, down_z, both, both_z = tie(down, down_z, both, both_z)
-    down_z = sends(down_z, "zlo")
-    both = add(both, both_z).reshape(own_rows, 2, EXP, ff)
+    down = exchange(add(down, down_x).astype(BF16), "zlo")
+    both = add(both[0].astype(F32), both[1:]).reshape(own_rows, 2, EXP, ff)
     input_grad = near[0] + far.astype(F32)
-    grad_down = add(down, down_z).reshape(own_rows, EXP, ff)
+    grad_down = add(down[0].astype(F32), down[1:]).reshape(own_rows, EXP, ff)
     return (
         output.astype(BF16),
         input_grad.astype(BF16),

time: 194 us -> 194 us (level)
  starting transfers between devices: 68.5 us -> 61.9 us
  other arithmetic: 5.93 us -> 10.9 us
  local copies, waits for them, and re-layouts: 5.26 us -> 8.38 us
    ppermute x33 -> x27, starting transfers between devices: 68.5 us -> 42.4 us  [send(): return lax.ppermute(value, axis, [(i, (i + step) % n) for i in range(n)])]
    all_to_all x0 -> x2, starting transfers between devices: none -> 19.4 us  [exchange(): return lax.all_to_all(value, axis, 0, 0, tiled=True)]
    ppermute x33 -> x27, waiting for transfers between devices: 63.2 us -> 57.1 us  [send(): return lax.ppermute(value, axis, [(i, (i + step) % n) for i in range(n)])]
    all_to_all x0 -> x2, waiting for transfers between devices: none -> 6.1 us  [exchange(): return lax.all_to_all(value, axis, 0, 0, tiled=True)]
    unnamed x34 -> x44, local copies, waits for them, and re-layouts: 0.11 us -> 2.49 us
    convert_element_type x1 -> x2, other arithmetic: 0.8 us -> 2.98 us  [the longest x1 1.89 us: per_device(): down = exchange(add(down, down_x).astype(BF16), 'zlo')]
    add x8 -> x6, other arithmetic: 3.37 us -> 4.37 us  [add(): own = own + piece.astype(F32)]
  transfers between devices with their start and end apart: 33 -> 29, of which waited for: 14 -> 13; matrix products, arithmetic and copies ran while one was open for 5% -> 7% of each run, Pallas kernels for 25% -> 25%
where the time goes in v5:
time: 194 us; the launch traced here: 193 us
  waiting for transfers between devices  63.2 us (33%)
  starting transfers between devices  61.9 us (32%)
  Pallas kernels  48.2 us (25%)
  other arithmetic  10.9 us (6%)
  local copies, waits for them, and re-layouts  8.38 us (4%)
    ppermute x27, waiting for transfers between devices, send(): return lax.ppermute(value, axis, [(i, (i + step) % n) for i in range(n)])  57.1 us
    pallas_call x5, Pallas kernels, run(): call(kernel, 4, ins, outs, flops, len(scalars))  48.2 us
    ppermute x27, starting transfers between devices, send(): return lax.ppermute(value, axis, [(i, (i + step) % n) for i in range(n)])  42.4 us
    all_to_all x2, starting transfers between devices, exchange(): return lax.all_to_all(value, axis, 0, 0, tiled=True)  19.4 us
    all_to_all x2, waiting for transfers between devices, exchange(): return lax.all_to_all(value, axis, 0, 0, tiled=True)  6.1 us
    add x6, other arithmetic, add(): own = own + piece.astype(F32)  4.37 us
  transfers between devices with their start and end apart: 29, of which 13 were waited for; matrix products, arithmetic and copies ran while one was open for 7% of the time, Pallas kernels for 25%

profile of v5, /device:TPU:6, one launch (start us, length us, event | category | flops | bytes accessed | tf_op | source)
XLA Modules:
  0.0 193.4 jit_solution(10989712577500395526)
XLA Ops:
  0.6 7.3 %collective-permute-start.3 = (bf16[128,1024]{1,0:T(8,128)(2,1)}, bf16[128,1024]{1,0:T(8,128)(2,1)S(1)}, u32[]{:S(2)}, u32[]{:S(2)}) collective-permute-start(bf16[128,1024]{1,0:T(8,128)(2,1)} %refs_0_.1), channel_id=1, source_target_pairs={{0,4},{4,0},{1,5},{5,1},{2,6},{6,2},{3,7},{7,3},{8,12},{12,8},{9,1... | collective-permute-start | bytes 786440 | tf_op jit(solution)/shard_map/ppermute | solution.py:17
  8.0 3.0 %collective-permute-start.2 = (bf16[128,1024]{1,0:T(8,128)(2,1)}, bf16[128,1024]{1,0:T(8,128)(2,1)S(1)}, u32[]{:S(2)}, u32[]{:S(2)}) collective-permute-start(bf16[128,1024]{1,0:T(8,128)(2,1)} %refs_0_.1), channel_id=1, source_target_pairs={{0,3},{1,0},{2,1},{3,2},{4,7},{5,4},{6,5},{7,6},{8,11},{9,8},{10,9... | collective-permute-start | bytes 786440 | tf_op jit(solution)/shard_map/ppermute | solution.py:17
  12.6 3.8 %collective-permute-done.3.refs_4_ = bf16[128,1024]{1,0:T(8,128)(2,1)S(1)} collective-permute-done((bf16[128,1024]{1,0:T(8,128)(2,1)}, bf16[128,1024]{1,0:T(8,128)(2,1)S(1)}, u32[]{:S(2)}, u32[]{:S(2)}) %collective-permute-start.3) | collective-permute-done | bytes 262176 | tf_op jit(solution)/shard_map/ppermute | solution.py:17
  16.4 3.0 %collective-permute-start.6 = (bf16[128,1024]{1,0:T(8,128)(2,1)S(1)}, bf16[128,1024]{1,0:T(8,128)(2,1)S(1)}, u32[]{:S(2)}, u32[]{:S(2)}) collective-permute-start(bf16[128,1024]{1,0:T(8,128)(2,1)S(1)} %collective-permute-done.3.refs_4_), channel_id=1, source_target_pairs={{0,3},{1,0},{2,1},{3,2},{4,7},{5,4},{6,5},{7,6},{8,11},{9,8},{10,9... | collective-permute-start | bytes 786440 | tf_op jit(solution)/shard_map/ppermute | solution.py:17
  19.4 2.9 %collective-permute-done.7 = bf16[128,1024]{1,0:T(8,128)(2,1)S(1)} collective-permute-done((bf16[128,1024]{1,0:T(8,128)(2,1)}, bf16[128,1024]{1,0:T(8,128)(2,1)S(1)}, u32[]{:S(2)}, u32[]{:S(2)}) %collective-permute-start.7) | collective-permute-done | bytes 262176 | tf_op jit(solution)/shard_map/ppermute | solution.py:17
  22.3 3.2 %collective-permute-start.5 = (bf16[128,1024]{1,0:T(8,128)(2,1)S(1)}, bf16[128,1024]{1,0:T(8,128)(2,1)S(1)}, u32[]{:S(2)}, u32[]{:S(2)}) collective-permute-start(bf16[128,1024]{1,0:T(8,128)(2,1)S(1)} %collective-permute-done.3.refs_4_), channel_id=1, source_target_pairs={{0,2},{1,3},{2,0},{3,1},{4,6},{5,7},{6,4},{7,5},{8,10},{9,11},{10,... | collective-permute-start | bytes 786440 | tf_op jit(solution)/shard_map/ppermute | solution.py:17
  29.0 2.6 %collective-permute-start.10 = (bf16[2,128,1024]{2,1,0:T(8,128)(2,1)S(1)}, bf16[2,128,1024]{2,1,0:T(8,128)(2,1)S(1)}, u32[]{:S(2)}, u32[]{:S(2)}) collective-permute-start(bf16[2,128,1024]{2,1,0:T(8,128)(2,1)S(1)} %pad_maximum_fusion.refs_0_), channel_id=1, source_target_pairs={{0,3},{1,0},{2,1},{3,2},{4,7},{5,4},{6,5},{7,6},{8,11},{9,8},{10,9... | collective-permute-start | bytes 1572872 | tf_op jit(solution)/shard_map/ppermute | solution.py:17
  31.7 3.1 %collective-permute-done.6.refs_7_ = bf16[128,1024]{1,0:T(8,128)(2,1)S(1)} collective-permute-done((bf16[128,1024]{1,0:T(8,128)(2,1)S(1)}, bf16[128,1024]{1,0:T(8,128)(2,1)S(1)}, u32[]{:S(2)}, u32[]{:S(2)}) %collective-permute-start.6) | collective-permute-done | bytes 262176 | tf_op jit(solution)/shard_map/ppermute | solution.py:17
  34.8 12.3 %collective-permute-done.4.refs_5_ = bf16[128,1024]{1,0:T(8,128)(2,1)S(1)} collective-permute-done((bf16[128,1024]{1,0:T(8,128)(2,1)S(1)}, bf16[128,1024]{1,0:T(8,128)(2,1)S(1)}, u32[]{:S(2)}, u32[]{:S(2)}) %collective-permute-start.4) | collective-permute-done | bytes 262176 | tf_op jit(solution)/shard_map/ppermute | solution.py:17
  47.8 15.0 %shard_map.110 = (bf16[1024,1024]{1,0:T(8,128)(2,1)}, bf16[1024,1024]{1,0:T(8,128)(2,1)}, f32[1024,512]{1,0:T(8,128)}, f32[1024,512]{1,0:T(8,128)}, f32[2,128,10...) custom-call(s32[1024,1]{1,0:T(8,128)} %copy.15.second_ref, ...), custom_call_target="tpu_custom_call" | custom-call | flops 6442450944 | bytes 16106127 | tf_op jit(solution)/shard_map/pallas_call | solution.py:202
  68.0 8.5 %shard_map.111 = (bf16[1024,1024]{1,0:T(8,128)(2,1)}, bf16[1024,2048]{1,0:T(8,128)(2,1)}) custom-call(s32[1024,1]{1,0:T(8,128)} %copy.15.second_ref, f32[1024,1]{1,0:T(8,128)} %copy.17.scale_ref, bf16[2,128,1024]{2,1,0:T(8,128)(2,1)} %copy-done, bf16[2,128,1024]{2,1,0:T(8,128)(2,1)} %copy-done.7, bf16[2,128,1024]{2,1,0:T(8,128)(2,1)} %copy-done.6, ...), custom_call_target="tpu_custom_call" | custom-call | flops 107374184 | bytes 268435 | tf_op jit(solution)/shard_map/pallas_call | solution.py:202
  76.5 8.8 %shard_map.112 = (bf16[4,4,32,2048]{3,2,1,0:T(8,128)(2,1)}, bf16[4,4,32,2048]{3,2,1,0:T(8,128)(2,1)}) custom-call(s32[1]{0:T(128)} %bitcast.core_ref, bf16[1024,1024]{1,0:T(8,128)(2,1)} %get-tuple-element.81.left, bf16[1024,2048]{1,0:T(8,128)(2,1)} %get-tuple-element.106.right.gu), custom_call_target="tpu_custom_call" | custom-call | flops 214748368 | bytes 536870 | tf_op jit(solution)/shard_map/pallas_call | solution.py:202
  87.8 5.2 %collective-permute-start.16 = (bf16[128,1024]{1,0:T(8,128)(2,1)S(1)}, bf16[128,1024]{1,0:T(8,128)(2,1)}, u32[]{:S(2)}, u32[]{:S(2)}) collective-permute-start(bf16[128,1024]{1,0:T(8,128)(2,1)S(1)} %fusion.9), channel_id=1, source_target_pairs={{0,4},{4,0},{1,5},{5,1},{2,6},{6,2},{3,7},{7,3},{8,12},{12,8},{9,1... | collective-permute-start | bytes 786440 | tf_op jit(solution)/shard_map/ppermute | solution.py:17
  93.0 6.3 %shard_map.113 = (bf16[4,4,32,1024]{3,2,1,0:T(8,128)(2,1)}, bf16[4,4,32,1024]{3,2,1,0:T(8,128)(2,1)}) custom-call(s32[1]{0:T(128)} %bitcast.core_ref, bf16[1024,1024]{1,0:T(8,128)(2,1)} %get-tuple-element.97.left, bf16[1024,1024]{1,0:T(8,128)(2,1)} %get-tuple-element.98.right), custom_call_target="tpu_custom_call" | custom-call | flops 17179869184 | bytes 42949672 | tf_op jit(solution)/shard_map/pallas_call | solution.py:202
  102.6 9.5 %shard_map.114 = (f32[2,128,1024]{2,1,0:T(8,128)}, bf16[2,128,1024]{2,1,0:T(8,128)(2,1)}, bf16[2,128,1024]{2,1,0:T(8,128)(2,1)}, bf16[2,128,1024]{2,1,0:T(8,128)(2,1)}) custom-call(bf16[1024,2048]{1,0:T(8,128)(2,1)} %get-tuple-element.106.right.gu, bf16[2,1024,512]{2,1,0:T(8,128)(2,1)} %wg.1, bf16[2,1024,512]{2,1,0:T(8,128)(2,1)} %wu.1), custom_call_target="tpu_custom_call" | custom-call | flops 17179869184 | bytes 42949672 | tf_op jit(solution)/shard_map/pallas_call | solution.py:202
  114.9 12.6 %collective-permute-done.18 = bf16[4,32,2048]{2,1,0:T(8,128)(2,1)S(1)} collective-permute-done((bf16[4,32,2048]{2,1,0:T(8,128)(2,1)S(1)}, bf16[4,32,2048]{2,1,0:T(8,128)(2,1)S(1)}, u32[]{:S(2)}, u32[]{:S(2)}) %collective-permute-start.18) | collective-permute-done | bytes 524320 | tf_op jit(solution)/shard_map/ppermute | solution.py:17
  133.1 4.0 %collective-permute-done.20 = bf16[2,128,1024]{2,1,0:T(8,128)(2,1)S(1)} collective-permute-done((bf16[2,128,1024]{2,1,0:T(8,128)(2,1)}, bf16[2,128,1024]{2,1,0:T(8,128)(2,1)S(1)}, u32[]{:S(2)}, u32[]{:S(2)}) %collective-permute-start.20) | collective-permute-done | bytes 524320 | tf_op jit(solution)/shard_map/ppermute | solution.py:17
  137.1 3.6 %collective-permute-done.21 = bf16[2,128,1024]{2,1,0:T(8,128)(2,1)S(1)} collective-permute-done((bf16[2,128,1024]{2,1,0:T(8,128)(2,1)}, bf16[2,128,1024]{2,1,0:T(8,128)(2,1)S(1)}, u32[]{:S(2)}, u32[]{:S(2)}) %collective-permute-start.21) | collective-permute-done | bytes 524320 | tf_op jit(solution)/shard_map/ppermute | solution.py:17
  142.6 16.0 %all-to-all-start = ((bf16[4,32,2048]{2,1,0:T(8,128)(2,1)}), bf16[4,32,2048]{2,1,0:T(8,128)(2,1)S(1)}, u32[]{:S(2)}, u32[]{:S(2)}) async-start(bf16[4,32,2048]{2,1,0:T(8,128)(2,1)} %add_convert_fusion), calls=%async_computation | async-start | bytes 1048576 | tf_op jit(solution)/shard_map/all_to_all | solution.py:41
  160.6 8.9 %collective-permute-done.25 = bf16[2,128,1024]{2,1,0:T(8,128)(2,1)S(1)} collective-permute-done((bf16[2,128,1024]{2,1,0:T(8,128)(2,1)}, bf16[2,128,1024]{2,1,0:T(8,128)(2,1)S(1)}, u32[]{:S(2)}, u32[]{:S(2)}) %collective-permute-start.25) | collective-permute-done | bytes 524320 | tf_op jit(solution)/shard_map/ppermute | solution.py:17
  170.5 4.4 %all-to-all-done = bf16[4,32,2048]{2,1,0:T(8,128)(2,1)S(1)} async-done(((bf16[4,32,2048]{2,1,0:T(8,128)(2,1)}), bf16[4,32,2048]{2,1,0:T(8,128)(2,1)S(1)}, u32[]{:S(2)}, u32[]{:S(2)}) %all-to-all-start) | async-done | bytes 524320 | tf_op jit(solution)/shard_map/all_to_all | solution.py:41
  176.9 3.6 %collective-permute-start.26 = (bf16[128,1024]{1,0:T(8,128)(2,1)S(1)}, bf16[128,1024]{1,0:T(8,128)(2,1)S(1)}, u32[]{:S(2)}, u32[]{:S(2)}) collective-permute-start(bf16[128,1024]{1,0:T(8,128)(2,1)S(1)} %fusion.10), channel_id=1, source_target_pairs={{0,4},{4,0},{1,5},{5,1},{2,6},{6,2},{3,7},{7,3},{8,12},{12,8},{9,1... | collective-permute-start | bytes 786440 | tf_op jit(solution)/shard_map/ppermute | solution.py:17
  182.4 3.4 %all-to-all-start.1 = ((bf16[4,32,1024]{2,1,0:T(8,128)(2,1)}), bf16[4,32,1024]{2,1,0:T(8,128)(2,1)S(1)}, u32[]{:S(2)}, u32[]{:S(2)}) async-start(bf16[4,32,1024]{2,1,0:T(8,128)(2,1)} %add_convert_fusion.1), calls=%async_computation.1 | async-start | bytes 524288 | tf_op jit(solution)/shard_map/all_to_all | solution.py:41
  186.6 3.5 %collective-permute-done.26 = bf16[128,1024]{1,0:T(8,128)(2,1)S(1)} collective-permute-done((bf16[128,1024]{1,0:T(8,128)(2,1)S(1)}, bf16[128,1024]{1,0:T(8,128)(2,1)S(1)}, u32[]{:S(2)}, u32[]{:S(2)}) %collective-permute-start.26) | collective-permute-done | bytes 262176 | tf_op jit(solution)/shard_map/ppermute | solution.py:17
  (114 shorter events, 38.0 us)
Async XLA Ops:
  0.6 15.8 %collective-permute-start.3 = (bf16[128,1024]{1,0:T(8,128)(2,1)}, bf16[128,1024]{1,0:T(8,128)(2,1)S(1)}, u32[]{:S(2)}, u32[]{:S(2)}) collective-permute-start(bf16[128,1024]{1,0:T(8,128)(2,1)} %refs_0_.1), channel_id=1, source_target_pairs={{0,4},{4,0},{1,5},{5,1},{2,6},{6,2},{3,7},{7,3},{8,12},{12,8},{9,1... | collective-permute-start | bytes 786440 | tf_op jit(solution)/shard_map/ppermute | solution.py:17
  7.9 14.4 %collective-permute-start.7 = (bf16[128,1024]{1,0:T(8,128)(2,1)}, bf16[128,1024]{1,0:T(8,128)(2,1)S(1)}, u32[]{:S(2)}, u32[]{:S(2)}) collective-permute-start(bf16[128,1024]{1,0:T(8,128)(2,1)} %param.8), channel_id=1, source_target_pairs={{0,4},{4,0},{1,5},{5,1},{2,6},{6,2},{3,7},{7,3},{8,12},{12,8},{9,1... | collective-permute-start | bytes 786440 | tf_op jit(solution)/shard_map/ppermute | solution.py:17
  8.0 17.5 %collective-permute-start.2 = (bf16[128,1024]{1,0:T(8,128)(2,1)}, bf16[128,1024]{1,0:T(8,128)(2,1)S(1)}, u32[]{:S(2)}, u32[]{:S(2)}) collective-permute-start(bf16[128,1024]{1,0:T(8,128)(2,1)} %refs_0_.1), channel_id=1, source_target_pairs={{0,3},{1,0},{2,1},{3,2},{4,7},{5,4},{6,5},{7,6},{8,11},{9,8},{10,9... | collective-permute-start | bytes 786440 | tf_op jit(solution)/shard_map/ppermute | solution.py:17
  11.0 17.9 %collective-permute-start.1 = (bf16[128,1024]{1,0:T(8,128)(2,1)}, bf16[128,1024]{1,0:T(8,128)(2,1)S(1)}, u32[]{:S(2)}, u32[]{:S(2)}) collective-permute-start(bf16[128,1024]{1,0:T(8,128)(2,1)} %refs_0_.1), channel_id=1, source_target_pairs={{0,2},{1,3},{2,0},{3,1},{4,6},{5,7},{6,4},{7,5},{8,10},{9,11},{10,... | collective-permute-start | bytes 786440 | tf_op jit(solution)/shard_map/ppermute | solution.py:17
  11.7 20.0 %collective-permute-start = (bf16[128,1024]{1,0:T(8,128)(2,1)}, bf16[128,1024]{1,0:T(8,128)(2,1)S(1)}, u32[]{:S(2)}, u32[]{:S(2)}) collective-permute-start(bf16[128,1024]{1,0:T(8,128)(2,1)} %refs_0_.1), channel_id=1, source_target_pairs={{0,1},{1,2},{2,3},{3,0},{4,5},{5,6},{6,7},{7,4},{8,9},{9,10},{10,1... | collective-permute-start | bytes 786440 | tf_op jit(solution)/shard_map/ppermute | solution.py:17
  16.4 18.4 %collective-permute-start.6 = (bf16[128,1024]{1,0:T(8,128)(2,1)S(1)}, bf16[128,1024]{1,0:T(8,128)(2,1)S(1)}, u32[]{:S(2)}, u32[]{:S(2)}) collective-permute-start(bf16[128,1024]{1,0:T(8,128)(2,1)S(1)} %collective-permute-done.3.refs_4_), channel_id=1, source_target_pairs={{0,3},{1,0},{2,1},{3,2},{4,7},{5,4},{6,5},{7,6},{8,11},{9,8},{10,9... | collective-permute-start | bytes 786440 | tf_op jit(solution)/shard_map/ppermute | solution.py:17
  22.3 12.5 %collective-permute-start.5 = (bf16[128,1024]{1,0:T(8,128)(2,1)S(1)}, bf16[128,1024]{1,0:T(8,128)(2,1)S(1)}, u32[]{:S(2)}, u32[]{:S(2)}) collective-permute-start(bf16[128,1024]{1,0:T(8,128)(2,1)S(1)} %collective-permute-done.3.refs_4_), channel_id=1, source_target_pairs={{0,2},{1,3},{2,0},{3,1},{4,6},{5,7},{6,4},{7,5},{8,10},{9,11},{10,... | collective-permute-start | bytes 786440 | tf_op jit(solution)/shard_map/ppermute | solution.py:17
  25.5 21.6 %collective-permute-start.4 = (bf16[128,1024]{1,0:T(8,128)(2,1)S(1)}, bf16[128,1024]{1,0:T(8,128)(2,1)S(1)}, u32[]{:S(2)}, u32[]{:S(2)}) collective-permute-start(bf16[128,1024]{1,0:T(8,128)(2,1)S(1)} %collective-permute-done.3.refs_4_), channel_id=1, source_target_pairs={{0,1},{1,2},{2,3},{3,0},{4,5},{5,6},{6,7},{7,4},{8,9},{9,10},{10,1... | collective-permute-start | bytes 786440 | tf_op jit(solution)/shard_map/ppermute | solution.py:17
  29.0 33.8 %collective-permute-start.10 = (bf16[2,128,1024]{2,1,0:T(8,128)(2,1)S(1)}, bf16[2,128,1024]{2,1,0:T(8,128)(2,1)S(1)}, u32[]{:S(2)}, u32[]{:S(2)}) collective-permute-start(bf16[2,128,1024]{2,1,0:T(8,128)(2,1)S(1)} %pad_maximum_fusion.refs_0_), channel_id=1, source_target_pairs={{0,3},{1,0},{2,1},{3,2},{4,7},{5,4},{6,5},{7,6},{8,11},{9,8},{10,9... | collective-permute-start | bytes 1572872 | tf_op jit(solution)/shard_map/ppermute | solution.py:17
  31.6 31.2 %collective-permute-start.9 = (bf16[2,128,1024]{2,1,0:T(8,128)(2,1)S(1)}, bf16[2,128,1024]{2,1,0:T(8,128)(2,1)S(1)}, u32[]{:S(2)}, u32[]{:S(2)}) collective-permute-start(bf16[2,128,1024]{2,1,0:T(8,128)(2,1)S(1)} %pad_maximum_fusion.refs_0_), channel_id=1, source_target_pairs={{0,2},{1,3},{2,0},{3,1},{4,6},{5,7},{6,4},{7,5},{8,10},{9,11},{10,... | collective-permute-start | bytes 1572872 | tf_op jit(solution)/shard_map/ppermute | solution.py:17
  34.8 28.1 %collective-permute-start.8 = (bf16[2,128,1024]{2,1,0:T(8,128)(2,1)S(1)}, bf16[2,128,1024]{2,1,0:T(8,128)(2,1)S(1)}, u32[]{:S(2)}, u32[]{:S(2)}) collective-permute-start(bf16[2,128,1024]{2,1,0:T(8,128)(2,1)S(1)} %pad_maximum_fusion.refs_0_), channel_id=1, source_target_pairs={{0,1},{1,2},{2,3},{3,0},{4,5},{5,6},{6,7},{7,4},{8,9},{9,10},{10,1... | collective-permute-start | bytes 1572872 | tf_op jit(solution)/shard_map/ppermute | solution.py:17
  62.9 22.5 %collective-permute-start.11 = (bf16[2,128,1024]{2,1,0:T(8,128)(2,1)}, bf16[2,128,1024]{2,1,0:T(8,128)(2,1)S(1)}, u32[]{:S(2)}, u32[]{:S(2)}) collective-permute-start(bf16[2,128,1024]{2,1,0:T(8,128)(2,1)} %get-tuple-element.78), channel_id=1, source_target_pairs={{0,3},{1,0},{2,1},{3,2},{4,7},{5,4},{6,5},{7,6},{8,11},{9,8},{10,9... | collective-permute-start | bytes 1572872 | tf_op jit(solution)/shard_map/ppermute | solution.py:17
  63.0 22.4 %collective-permute-start.12 = (bf16[2,128,1024]{2,1,0:T(8,128)(2,1)}, bf16[2,128,1024]{2,1,0:T(8,128)(2,1)S(1)}, u32[]{:S(2)}, u32[]{:S(2)}) collective-permute-start(bf16[2,128,1024]{2,1,0:T(8,128)(2,1)} %get-tuple-element.79), channel_id=1, source_target_pairs={{0,2},{1,3},{2,0},{3,1},{4,6},{5,7},{6,4},{7,5},{8,10},{9,11},{10,... | collective-permute-start | bytes 1572872 | tf_op jit(solution)/shard_map/ppermute | solution.py:17
  65.5 20.9 %collective-permute-start.13 = (bf16[2,128,1024]{2,1,0:T(8,128)(2,1)}, bf16[2,128,1024]{2,1,0:T(8,128)(2,1)}, u32[]{:S(2)}, u32[]{:S(2)}) collective-permute-start(bf16[2,128,1024]{2,1,0:T(8,128)(2,1)} %get-tuple-element.80), channel_id=1, source_target_pairs={{0,1},{1,2},{2,3},{3,0},{4,5},{5,6},{6,7},{7,4},{8,9},{9,10},{10,1... | collective-permute-start | bytes 1572872 | tf_op jit(solution)/shard_map/ppermute | solution.py:17
  85.3 14.0 %collective-permute-start.14 = (bf16[4,4,32,2048]{3,2,1,0:T(8,128)(2,1)}, bf16[4,4,32,2048]{3,2,1,0:T(8,128)(2,1)S(1)}, u32[]{:S(2)}, u32[]{:S(2)}) collective-permute-start(bf16[4,4,32,2048]{3,2,1,0:T(8,128)(2,1)} %get-tuple-element.100), channel_id=1, source_target_pairs={{0,8},{8,0},{1,9},{9,1},{2,10},{10,2},{3,11},{11,3},{4,12},{12,4},... | collective-permute-start | bytes 6291464 | tf_op jit(solution)/shard_map/ppermute | solution.py:17
  87.8 25.7 %collective-permute-start.16 = (bf16[128,1024]{1,0:T(8,128)(2,1)S(1)}, bf16[128,1024]{1,0:T(8,128)(2,1)}, u32[]{:S(2)}, u32[]{:S(2)}) collective-permute-start(bf16[128,1024]{1,0:T(8,128)(2,1)S(1)} %fusion.9), channel_id=1, source_target_pairs={{0,4},{4,0},{1,5},{5,1},{2,6},{6,2},{3,7},{7,3},{8,12},{12,8},{9,1... | collective-permute-start | bytes 786440 | tf_op jit(solution)/shard_map/ppermute | solution.py:17
  99.3 14.2 %collective-permute-start.15 = (bf16[4,4,32,1024]{3,2,1,0:T(8,128)(2,1)}, bf16[4,4,32,1024]{3,2,1,0:T(8,128)(2,1)S(1)}, u32[]{:S(2)}, u32[]{:S(2)}) collective-permute-start(bf16[4,4,32,1024]{3,2,1,0:T(8,128)(2,1)} %get-tuple-element.111), channel_id=1, source_target_pairs={{0,8},{8,0},{1,9},{9,1},{2,10},{10,2},{3,11},{11,3},{4,12},{12,4},... | collective-permute-start | bytes 3145736 | tf_op jit(solution)/shard_map/ppermute | solution.py:17
  100.5 14.4 %collective-permute-start.17 = (bf16[4,32,2048]{2,1,0:T(8,128)(2,1)S(1)}, bf16[4,32,2048]{2,1,0:T(8,128)(2,1)S(1)}, u32[]{:S(2)}, u32[]{:S(2)}) collective-permute-start(bf16[4,32,2048]{2,1,0:T(8,128)(2,1)S(1)} %get-tuple-element.113), channel_id=1, source_target_pairs={{0,16},{16,32},{32,48},{48,0},{1,17},{17,33},{33,49},{49,1},{2,18}... | collective-permute-start | bytes 1572872 | tf_op jit(solution)/shard_map/ppermute | solution.py:17
  101.0 26.5 %collective-permute-start.18 = (bf16[4,32,2048]{2,1,0:T(8,128)(2,1)S(1)}, bf16[4,32,2048]{2,1,0:T(8,128)(2,1)S(1)}, u32[]{:S(2)}, u32[]{:S(2)}) collective-permute-start(bf16[4,32,2048]{2,1,0:T(8,128)(2,1)S(1)} %get-tuple-element.114), channel_id=1, source_target_pairs={{0,48},{16,0},{32,16},{48,32},{1,49},{17,1},{33,17},{49,33},{2,50}... | collective-permute-start | bytes 1572872 | tf_op jit(solution)/shard_map/ppermute | solution.py:17
  112.1 21.1 %collective-permute-start.19 = (bf16[4,32,2048]{2,1,0:T(8,128)(2,1)S(1)}, bf16[4,32,2048]{2,1,0:T(8,128)(2,1)S(1)}, u32[]{:S(2)}, u32[]{:S(2)}) collective-permute-start(bf16[4,32,2048]{2,1,0:T(8,128)(2,1)S(1)} %get-tuple-element.118), channel_id=1, source_target_pairs={{0,32},{16,48},{32,0},{48,16},{1,33},{17,49},{33,1},{49,17},{2,34}... | collective-permute-start | bytes 1572872 | tf_op jit(solution)/shard_map/ppermute | solution.py:17
  142.6 32.3 %all-to-all-start = ((bf16[4,32,2048]{2,1,0:T(8,128)(2,1)}), bf16[4,32,2048]{2,1,0:T(8,128)(2,1)S(1)}, u32[]{:S(2)}, u32[]{:S(2)}) async-start(bf16[4,32,2048]{2,1,0:T(8,128)(2,1)} %add_convert_fusion), calls=%async_computation | async-start | bytes 1048576 | tf_op jit(solution)/shard_map/all_to_all | solution.py:41
  158.6 10.9 %collective-permute-start.22 = (bf16[4,32,1024]{2,1,0:T(8,128)(2,1)}, bf16[4,32,1024]{2,1,0:T(8,128)(2,1)S(1)}, u32[]{:S(2)}, u32[]{:S(2)}) collective-permute-start(bf16[4,32,1024]{2,1,0:T(8,128)(2,1)} %get-tuple-element.125), channel_id=1, source_target_pairs={{0,16},{16,32},{32,48},{48,0},{1,17},{17,33},{33,49},{49,1},{2,18}... | collective-permute-start | bytes 786440 | tf_op jit(solution)/shard_map/ppermute | solution.py:17
  158.7 11.5 %collective-permute-start.24 = (bf16[4,32,1024]{2,1,0:T(8,128)(2,1)S(1)}, bf16[4,32,1024]{2,1,0:T(8,128)(2,1)}, u32[]{:S(2)}, u32[]{:S(2)}) collective-permute-start(bf16[4,32,1024]{2,1,0:T(8,128)(2,1)S(1)} %get-tuple-element.127), channel_id=1, source_target_pairs={{0,48},{16,0},{32,16},{48,32},{1,49},{17,1},{33,17},{49,33},{2,50}... | collective-permute-start | bytes 786440 | tf_op jit(solution)/shard_map/ppermute | solution.py:17
  176.9 13.2 %collective-permute-start.26 = (bf16[128,1024]{1,0:T(8,128)(2,1)S(1)}, bf16[128,1024]{1,0:T(8,128)(2,1)S(1)}, u32[]{:S(2)}, u32[]{:S(2)}) collective-permute-start(bf16[128,1024]{1,0:T(8,128)(2,1)S(1)} %fusion.10), channel_id=1, source_target_pairs={{0,4},{4,0},{1,5},{5,1},{2,6},{6,2},{3,7},{7,3},{8,12},{12,8},{9,1... | collective-permute-start | bytes 786440 | tf_op jit(solution)/shard_map/ppermute | solution.py:17
  (27 other events, 323.5 us)

commit v6 on v5

--- a/solution.py
+++ b/solution.py
@@ -23,14 +23,6 @@
     doubled = jnp.tile(blocks, (2, 2, 1))
     start = (lax.axis_index("zhi"), 3 - lax.axis_index("y"), 0)
     return lax.dynamic_slice(doubled, start, (2, 4, rows)).reshape(-1, 1)
-
-
-def gather_group(block):
-    far = send(block, "zhi", 1)
-    parts = []
-    for b in (block, far):
-        parts += [b, send(b, "y", 1), send(b, "y", 2), send(b, "y", 3)]
-    return parts
 
 
 def tie(*values):
@@ -117,15 +109,15 @@
 
 
 def back_kernel(second_ref, scale_ref, *refs):
-    a_ref, s_ref, wd, dout, gu_ref = refs[4:]
+    a_ref, s_ref, wd, dout, gu_ref = refs[8:]
     i = pl.program_id(0)
-    n = refs[0].shape[1]
+    n = refs[0].shape[0]
 
     @pl.when(i == 0)
     def _():
-        for b in range(8):
+        for b, block in enumerate(refs[:8]):
             at = slice(b * n, (b + 1) * n)
-            dout[at] = (scale_ref[at] * refs[b % 4][b // 4].astype(F32)).astype(BF16)
+            dout[at] = (scale_ref[at] * block[...].astype(F32)).astype(BF16)
 
     rows = pl.ds(pl.multiple_of(i * TILE, TILE), TILE)
     second = second_ref[...] > 0
@@ -191,9 +183,13 @@
     second = relative(assign)
     scale = relative(prob)
     core = lax.axis_index("core").astype(jnp.int32).reshape(1)
-    xs = gather_group(tokens)
-    pair = jnp.stack([cotangent, send(cotangent, "zhi", 1)])
-    ds = [pair, *sends([pair] * 3, "y")]
+    far_tokens, far_cot = send(tokens, "zhi", 1), send(cotangent, "zhi", 1)
+    x0 = sends([tokens] * 3, "y")
+    d0 = [send(cotangent, "y", 1)]
+    far_tokens, d0[0] = tie(far_tokens, d0[0])
+    d0 += [send(cotangent, "y", k) for k in (2, 3)]
+    xs = [tokens, *x0, far_tokens, *sends([far_tokens] * 3, "y")]
+    ds = [cotangent, *d0, far_cot, *sends([far_cot] * 3, "y")]
     wg2, wu2 = (w.reshape(EXP * width, ff) for w in (w_gate, w_up))
     wd2 = w_down.reshape(wide, width)
     pieces = [whole(sds((2, block, width), t)) for t in (F32, BF16, BF16, BF16)]

time: 194 us -> 185 us (0.954)
  waiting for transfers between devices: 63.2 us -> 53.3 us
  starting transfers between devices: 61.9 us -> 66.4 us
  other arithmetic: 10.9 us -> 8.78 us
    ppermute x27 -> x30, starting transfers between devices: 42.4 us -> 56.5 us  [send(): return lax.ppermute(value, axis, [(i, (i + step) % n) for i in range(n)])]
    ppermute x27 -> x30, waiting for transfers between devices: 57.1 us -> 44.9 us  [send(): return lax.ppermute(value, axis, [(i, (i + step) % n) for i in range(n)])]
    all_to_all x2, starting transfers between devices: 19.4 us -> 9.98 us  [exchange(): return lax.all_to_all(value, axis, 0, 0, tiled=True)]
    all_to_all x2, waiting for transfers between devices: 6.1 us -> 8.4 us  [exchange(): return lax.all_to_all(value, axis, 0, 0, tiled=True)]
  transfers between devices with their start and end apart: 29 -> 32, of which waited for: 13 -> 11; matrix products, arithmetic and copies ran while one was open for 7% -> 5% of each run, Pallas kernels for 25% -> 26%
where the time goes in v6:
time: 185 us
  starting transfers between devices  66.4 us (36%)
  waiting for transfers between devices  53.3 us (29%)
  Pallas kernels  48.4 us (26%)
  other arithmetic  8.78 us (5%)
  local copies, waits for them, and re-layouts  6.75 us (4%)
    ppermute x30, starting transfers between devices, send(): return lax.ppermute(value, axis, [(i, (i + step) % n) for i in range(n)])  56.5 us
    pallas_call x5, Pallas kernels, run(): call(kernel, 4, ins, outs, flops, len(scalars))  48.4 us
    ppermute x30, waiting for transfers between devices, send(): return lax.ppermute(value, axis, [(i, (i + step) % n) for i in range(n)])  44.9 us
    all_to_all x2, starting transfers between devices, exchange(): return lax.all_to_all(value, axis, 0, 0, tiled=True)  9.98 us
    all_to_all x2, waiting for transfers between devices, exchange(): return lax.all_to_all(value, axis, 0, 0, tiled=True)  8.4 us
  transfers between devices with their start and end apart: 32, of which 11 were waited for; matrix products, arithmetic and copies ran while one was open for 5% of the time, Pallas kernels for 26%

profile of v6, /device:TPU:6, one launch (start us, length us, event | category | flops | bytes accessed | tf_op | source)
XLA Modules:
  0.0 184.7 jit_solution(8648812037372694240)
XLA Ops:
  0.6 7.3 %collective-permute-start.3 = (bf16[128,1024]{1,0:T(8,128)(2,1)}, bf16[128,1024]{1,0:T(8,128)(2,1)S(1)}, u32[]{:S(2)}, u32[]{:S(2)}) collective-permute-start(bf16[128,1024]{1,0:T(8,128)(2,1)} %refs_0_.1), channel_id=1, source_target_pairs={{0,4},{4,0},{1,5},{5,1},{2,6},{6,2},{3,7},{7,3},{8,12},{12,8},{9,1... | collective-permute-start | bytes 786440 | tf_op jit(solution)/shard_map/ppermute | solution.py:17
  15.6 9.5 %collective-permute-start.10 = (bf16[128,1024]{1,0:T(8,128)(2,1)}, bf16[128,1024]{1,0:T(8,128)(2,1)S(1)}, u32[]{:S(2)}, u32[]{:S(2)}) collective-permute-start(bf16[128,1024]{1,0:T(8,128)(2,1)} %refs_0_.2), channel_id=1, source_target_pairs={{0,4},{4,0},{1,5},{5,1},{2,6},{6,2},{3,7},{7,3},{8,12},{12,8},{9,1... | collective-permute-start | bytes 786440 | tf_op jit(solution)/shard_map/ppermute | solution.py:17
  25.0 3.0 %collective-permute-start.7 = (bf16[128,1024]{1,0:T(8,128)(2,1)S(1)}, bf16[128,1024]{1,0:T(8,128)(2,1)S(1)}, u32[]{:S(2)}, u32[]{:S(2)}) collective-permute-start(bf16[128,1024]{1,0:T(8,128)(2,1)S(1)} %collective-permute-done.3.refs_4_), channel_id=1, source_target_pairs={{0,3},{1,0},{2,1},{3,2},{4,7},{5,4},{6,5},{7,6},{8,11},{9,8},{10,9... | collective-permute-start | bytes 786440 | tf_op jit(solution)/shard_map/ppermute | solution.py:17
  31.5 2.3 %collective-permute-start.9 = (bf16[128,1024]{1,0:T(8,128)(2,1)}, bf16[128,1024]{1,0:T(8,128)(2,1)S(1)}, u32[]{:S(2)}, u32[]{:S(2)}) collective-permute-start(bf16[128,1024]{1,0:T(8,128)(2,1)} %refs_0_.2), channel_id=1, source_target_pairs={{0,3},{1,0},{2,1},{3,2},{4,7},{5,4},{6,5},{7,6},{8,11},{9,8},{10,9... | collective-permute-start | bytes 786440 | tf_op jit(solution)/shard_map/ppermute | solution.py:17
  34.8 3.2 %collective-permute-start.8 = (bf16[128,1024]{1,0:T(8,128)(2,1)}, bf16[128,1024]{1,0:T(8,128)(2,1)S(1)}, u32[]{:S(2)}, u32[]{:S(2)}) collective-permute-start(bf16[128,1024]{1,0:T(8,128)(2,1)} %refs_0_.2), channel_id=1, source_target_pairs={{0,2},{1,3},{2,0},{3,1},{4,6},{5,7},{6,4},{7,5},{8,10},{9,11},{10,... | collective-permute-start | bytes 786440 | tf_op jit(solution)/shard_map/ppermute | solution.py:17
  39.8 4.2 %collective-permute-start.13 = (bf16[128,1024]{1,0:T(8,128)(2,1)S(1)}, bf16[128,1024]{1,0:T(8,128)(2,1)S(1)}, u32[]{:S(2)}, u32[]{:S(2)}) collective-permute-start(bf16[128,1024]{1,0:T(8,128)(2,1)S(1)} %collective-permute-done.10.refs_4_), channel_id=1, source_target_pairs={{0,3},{1,0},{2,1},{3,2},{4,7},{5,4},{6,5},{7,6},{8,11},{9,8},{10,9... | collective-permute-start | bytes 786440 | tf_op jit(solution)/shard_map/ppermute | solution.py:17
  45.1 15.1 %shard_map.110 = (bf16[1024,1024]{1,0:T(8,128)(2,1)}, bf16[1024,1024]{1,0:T(8,128)(2,1)}, f32[1024,512]{1,0:T(8,128)}, f32[1024,512]{1,0:T(8,128)}, f32[2,128,10...) custom-call(s32[1024,1]{1,0:T(8,128)} %copy.15.second_ref, ...), custom_call_target="tpu_custom_call" | custom-call | flops 6442450944 | bytes 16106127 | tf_op jit(solution)/shard_map/pallas_call | solution.py:198
  61.1 2.4 %collective-permute-start.14 = (bf16[2,128,1024]{2,1,0:T(8,128)(2,1)}, bf16[2,128,1024]{2,1,0:T(8,128)(2,1)S(1)}, u32[]{:S(2)}, u32[]{:S(2)}) collective-permute-start(bf16[2,128,1024]{2,1,0:T(8,128)(2,1)} %get-tuple-element.86), channel_id=1, source_target_pairs={{0,3},{1,0},{2,1},{3,2},{4,7},{5,4},{6,5},{7,6},{8,11},{9,8},{10,9... | collective-permute-start | bytes 1572872 | tf_op jit(solution)/shard_map/ppermute | solution.py:17
  63.4 2.2 %collective-permute-start.15 = (bf16[2,128,1024]{2,1,0:T(8,128)(2,1)}, bf16[2,128,1024]{2,1,0:T(8,128)(2,1)S(1)}, u32[]{:S(2)}, u32[]{:S(2)}) collective-permute-start(bf16[2,128,1024]{2,1,0:T(8,128)(2,1)} %get-tuple-element.87), channel_id=1, source_target_pairs={{0,2},{1,3},{2,0},{3,1},{4,6},{5,7},{6,4},{7,5},{8,10},{9,11},{10,... | collective-permute-start | bytes 1572872 | tf_op jit(solution)/shard_map/ppermute | solution.py:17
  66.8 8.7 %shard_map.111 = (bf16[1024,1024]{1,0:T(8,128)(2,1)}, bf16[1024,2048]{1,0:T(8,128)(2,1)}) custom-call(s32[1024,1]{1,0:T(8,128)} %copy.15.second_ref, f32[1024,1]{1,0:T(8,128)} %copy.17.scale_ref, bf16[128,1024]{1,0:T(8,128)(2,1)} %refs_0_.2, bf16[128,1024]{1,0:T(8,128)(2,1)} %copy-done.4, bf16[128,1024]{1,0:T(8,128)(2,1)} %copy-done.7, ...), custom_call_target="tpu_custom_call" | custom-call | flops 107374184 | bytes 268435 | tf_op jit(solution)/shard_map/pallas_call | solution.py:198
  75.5 8.9 %shard_map.112 = (bf16[4,4,32,2048]{3,2,1,0:T(8,128)(2,1)}, bf16[4,4,32,2048]{3,2,1,0:T(8,128)(2,1)}) custom-call(s32[1]{0:T(128)} %bitcast.core_ref, bf16[1024,1024]{1,0:T(8,128)(2,1)} %get-tuple-element.89.left, bf16[1024,2048]{1,0:T(8,128)(2,1)} %get-tuple-element.118.right.gu), custom_call_target="tpu_custom_call" | custom-call | flops 214748368 | bytes 536870 | tf_op jit(solution)/shard_map/pallas_call | solution.py:198
  84.7 2.4 %collective-permute-start.19 = (bf16[128,1024]{1,0:T(8,128)(2,1)S(1)}, bf16[128,1024]{1,0:T(8,128)(2,1)}, u32[]{:S(2)}, u32[]{:S(2)}) collective-permute-start(bf16[128,1024]{1,0:T(8,128)(2,1)S(1)} %fusion.9), channel_id=1, source_target_pairs={{0,4},{4,0},{1,5},{5,1},{2,6},{6,2},{3,7},{7,3},{8,12},{12,8},{9,1... | collective-permute-start | bytes 786440 | tf_op jit(solution)/shard_map/ppermute | solution.py:17
  87.1 6.3 %shard_map.113 = (bf16[4,4,32,1024]{3,2,1,0:T(8,128)(2,1)}, bf16[4,4,32,1024]{3,2,1,0:T(8,128)(2,1)}) custom-call(s32[1]{0:T(128)} %bitcast.core_ref, bf16[1024,1024]{1,0:T(8,128)(2,1)} %get-tuple-element.109.left, bf16[1024,1024]{1,0:T(8,128)(2,1)} %get-tuple-element.110.right), custom_call_target="tpu_custom_call" | custom-call | flops 17179869184 | bytes 42949672 | tf_op jit(solution)/shard_map/pallas_call | solution.py:198
  96.9 9.5 %shard_map.114 = (f32[2,128,1024]{2,1,0:T(8,128)}, bf16[2,128,1024]{2,1,0:T(8,128)(2,1)}, bf16[2,128,1024]{2,1,0:T(8,128)(2,1)}, bf16[2,128,1024]{2,1,0:T(8,128)(2,1)}) custom-call(bf16[1024,2048]{1,0:T(8,128)(2,1)} %get-tuple-element.118.right.gu, bf16[2,1024,512]{2,1,0:T(8,128)(2,1)} %wg.1, bf16[2,1024,512]{2,1,0:T(8,128)(2,1)} %wu.1), custom_call_target="tpu_custom_call" | custom-call | flops 17179869184 | bytes 42949672 | tf_op jit(solution)/shard_map/pallas_call | solution.py:198
  109.0 12.7 %collective-permute-done.21 = bf16[4,32,2048]{2,1,0:T(8,128)(2,1)S(1)} collective-permute-done((bf16[4,32,2048]{2,1,0:T(8,128)(2,1)S(1)}, bf16[4,32,2048]{2,1,0:T(8,128)(2,1)S(1)}, u32[]{:S(2)}, u32[]{:S(2)}) %collective-permute-start.21) | collective-permute-done | bytes 524320 | tf_op jit(solution)/shard_map/ppermute | solution.py:17
  121.6 2.3 %collective-permute-start.23 = (bf16[2,128,1024]{2,1,0:T(8,128)(2,1)}, bf16[2,128,1024]{2,1,0:T(8,128)(2,1)}, u32[]{:S(2)}, u32[]{:S(2)}) collective-permute-start(bf16[2,128,1024]{2,1,0:T(8,128)(2,1)} %get-tuple-element.133), channel_id=1, source_target_pairs={{0,3},{1,0},{2,1},{3,2},{4,7},{5,4},{6,5},{7,6},{8,11},{9,8},{10,9... | collective-permute-start | bytes 1572872 | tf_op jit(solution)/shard_map/ppermute | solution.py:17
  126.2 4.9 %collective-permute-done.23 = bf16[2,128,1024]{2,1,0:T(8,128)(2,1)} collective-permute-done((bf16[2,128,1024]{2,1,0:T(8,128)(2,1)}, bf16[2,128,1024]{2,1,0:T(8,128)(2,1)}, u32[]{:S(2)}, u32[]{:S(2)}) %collective-permute-start.23) | collective-permute-done | bytes 524320 | tf_op jit(solution)/shard_map/ppermute | solution.py:17
  131.1 9.1 %collective-permute-done.24 = bf16[2,128,1024]{2,1,0:T(8,128)(2,1)} collective-permute-done((bf16[2,128,1024]{2,1,0:T(8,128)(2,1)}, bf16[2,128,1024]{2,1,0:T(8,128)(2,1)}, u32[]{:S(2)}, u32[]{:S(2)}) %collective-permute-start.24) | collective-permute-done | bytes 524320 | tf_op jit(solution)/shard_map/ppermute | solution.py:17
  141.3 6.6 %all-to-all-start = ((bf16[4,32,2048]{2,1,0:T(8,128)(2,1)}), bf16[4,32,2048]{2,1,0:T(8,128)(2,1)S(1)}, u32[]{:S(2)}, u32[]{:S(2)}) async-start(bf16[4,32,2048]{2,1,0:T(8,128)(2,1)} %add_convert_fusion), calls=%async_computation | async-start | bytes 1048576 | tf_op jit(solution)/shard_map/all_to_all | solution.py:33
  149.9 9.0 %collective-permute-done.28 = bf16[2,128,1024]{2,1,0:T(8,128)(2,1)} collective-permute-done((bf16[2,128,1024]{2,1,0:T(8,128)(2,1)}, bf16[2,128,1024]{2,1,0:T(8,128)(2,1)}, u32[]{:S(2)}, u32[]{:S(2)}) %collective-permute-start.28) | collective-permute-done | bytes 524320 | tf_op jit(solution)/shard_map/ppermute | solution.py:17
  159.6 6.6 %all-to-all-done = bf16[4,32,2048]{2,1,0:T(8,128)(2,1)S(1)} async-done(((bf16[4,32,2048]{2,1,0:T(8,128)(2,1)}), bf16[4,32,2048]{2,1,0:T(8,128)(2,1)S(1)}, u32[]{:S(2)}, u32[]{:S(2)}) %all-to-all-start) | async-done | bytes 524320 | tf_op jit(solution)/shard_map/all_to_all | solution.py:33
  168.2 3.6 %collective-permute-start.29 = (bf16[128,1024]{1,0:T(8,128)(2,1)S(1)}, bf16[128,1024]{1,0:T(8,128)(2,1)S(1)}, u32[]{:S(2)}, u32[]{:S(2)}) collective-permute-start(bf16[128,1024]{1,0:T(8,128)(2,1)S(1)} %fusion.10), channel_id=1, source_target_pairs={{0,4},{4,0},{1,5},{5,1},{2,6},{6,2},{3,7},{7,3},{8,12},{12,8},{9,1... | collective-permute-start | bytes 786440 | tf_op jit(solution)/shard_map/ppermute | solution.py:17
  173.7 3.4 %all-to-all-start.1 = ((bf16[4,32,1024]{2,1,0:T(8,128)(2,1)}), bf16[4,32,1024]{2,1,0:T(8,128)(2,1)S(1)}, u32[]{:S(2)}, u32[]{:S(2)}) async-start(bf16[4,32,1024]{2,1,0:T(8,128)(2,1)} %add_convert_fusion.1), calls=%async_computation.1 | async-start | bytes 524288 | tf_op jit(solution)/shard_map/all_to_all | solution.py:33
  177.9 3.5 %collective-permute-done.29 = bf16[128,1024]{1,0:T(8,128)(2,1)S(1)} collective-permute-done((bf16[128,1024]{1,0:T(8,128)(2,1)S(1)}, bf16[128,1024]{1,0:T(8,128)(2,1)S(1)}, u32[]{:S(2)}, u32[]{:S(2)}) %collective-permute-start.29) | collective-permute-done | bytes 262176 | tf_op jit(solution)/shard_map/ppermute | solution.py:17
  (115 shorter events, 37.4 us)
Async XLA Ops:
  0.6 14.9 %collective-permute-start.3 = (bf16[128,1024]{1,0:T(8,128)(2,1)}, bf16[128,1024]{1,0:T(8,128)(2,1)S(1)}, u32[]{:S(2)}, u32[]{:S(2)}) collective-permute-start(bf16[128,1024]{1,0:T(8,128)(2,1)} %refs_0_.1), channel_id=1, source_target_pairs={{0,4},{4,0},{1,5},{5,1},{2,6},{6,2},{3,7},{7,3},{8,12},{12,8},{9,1... | collective-permute-start | bytes 786440 | tf_op jit(solution)/shard_map/ppermute | solution.py:17
  7.9 17.1 %collective-permute-start.4 = (bf16[128,1024]{1,0:T(8,128)(2,1)}, bf16[128,1024]{1,0:T(8,128)(2,1)S(1)}, u32[]{:S(2)}, u32[]{:S(2)}) collective-permute-start(bf16[128,1024]{1,0:T(8,128)(2,1)} %refs_0_.2), channel_id=1, source_target_pairs={{0,1},{1,2},{2,3},{3,0},{4,5},{5,6},{6,7},{7,4},{8,9},{9,10},{10,1... | collective-permute-start | bytes 786440 | tf_op jit(solution)/shard_map/ppermute | solution.py:17
  9.5 18.6 %collective-permute-start.2 = (bf16[128,1024]{1,0:T(8,128)(2,1)}, bf16[128,1024]{1,0:T(8,128)(2,1)S(1)}, u32[]{:S(2)}, u32[]{:S(2)}) collective-permute-start(bf16[128,1024]{1,0:T(8,128)(2,1)} %refs_0_.1), channel_id=1, source_target_pairs={{0,3},{1,0},{2,1},{3,2},{4,7},{5,4},{6,5},{7,6},{8,11},{9,8},{10,9... | collective-permute-start | bytes 786440 | tf_op jit(solution)/shard_map/ppermute | solution.py:17
  11.1 17.6 %collective-permute-start.1 = (bf16[128,1024]{1,0:T(8,128)(2,1)}, bf16[128,1024]{1,0:T(8,128)(2,1)S(1)}, u32[]{:S(2)}, u32[]{:S(2)}) collective-permute-start(bf16[128,1024]{1,0:T(8,128)(2,1)} %refs_0_.1), channel_id=1, source_target_pairs={{0,2},{1,3},{2,0},{3,1},{4,6},{5,7},{6,4},{7,5},{8,10},{9,11},{10,... | collective-permute-start | bytes 786440 | tf_op jit(solution)/shard_map/ppermute | solution.py:17
  13.1 18.3 %collective-permute-start = (bf16[128,1024]{1,0:T(8,128)(2,1)}, bf16[128,1024]{1,0:T(8,128)(2,1)S(1)}, u32[]{:S(2)}, u32[]{:S(2)}) collective-permute-start(bf16[128,1024]{1,0:T(8,128)(2,1)} %refs_0_.1), channel_id=1, source_target_pairs={{0,1},{1,2},{2,3},{3,0},{4,5},{5,6},{6,7},{7,4},{8,9},{9,10},{10,1... | collective-permute-start | bytes 786440 | tf_op jit(solution)/shard_map/ppermute | solution.py:17
  15.6 19.2 %collective-permute-start.10 = (bf16[128,1024]{1,0:T(8,128)(2,1)}, bf16[128,1024]{1,0:T(8,128)(2,1)S(1)}, u32[]{:S(2)}, u32[]{:S(2)}) collective-permute-start(bf16[128,1024]{1,0:T(8,128)(2,1)} %refs_0_.2), channel_id=1, source_target_pairs={{0,4},{4,0},{1,5},{5,1},{2,6},{6,2},{3,7},{7,3},{8,12},{12,8},{9,1... | collective-permute-start | bytes 786440 | tf_op jit(solution)/shard_map/ppermute | solution.py:17
  25.0 14.8 %collective-permute-start.7 = (bf16[128,1024]{1,0:T(8,128)(2,1)S(1)}, bf16[128,1024]{1,0:T(8,128)(2,1)S(1)}, u32[]{:S(2)}, u32[]{:S(2)}) collective-permute-start(bf16[128,1024]{1,0:T(8,128)(2,1)S(1)} %collective-permute-done.3.refs_4_), channel_id=1, source_target_pairs={{0,3},{1,0},{2,1},{3,2},{4,7},{5,4},{6,5},{7,6},{8,11},{9,8},{10,9... | collective-permute-start | bytes 786440 | tf_op jit(solution)/shard_map/ppermute | solution.py:17
  28.1 16.0 %collective-permute-start.6 = (bf16[128,1024]{1,0:T(8,128)(2,1)S(1)}, bf16[128,1024]{1,0:T(8,128)(2,1)S(1)}, u32[]{:S(2)}, u32[]{:S(2)}) collective-permute-start(bf16[128,1024]{1,0:T(8,128)(2,1)S(1)} %collective-permute-done.3.refs_4_), channel_id=1, source_target_pairs={{0,2},{1,3},{2,0},{3,1},{4,6},{5,7},{6,4},{7,5},{8,10},{9,11},{10,... | collective-permute-start | bytes 786440 | tf_op jit(solution)/shard_map/ppermute | solution.py:17
  28.7 15.3 %collective-permute-start.5 = (bf16[128,1024]{1,0:T(8,128)(2,1)S(1)}, bf16[128,1024]{1,0:T(8,128)(2,1)S(1)}, u32[]{:S(2)}, u32[]{:S(2)}) collective-permute-start(bf16[128,1024]{1,0:T(8,128)(2,1)S(1)} %collective-permute-done.3.refs_4_), channel_id=1, source_target_pairs={{0,1},{1,2},{2,3},{3,0},{4,5},{5,6},{6,7},{7,4},{8,9},{9,10},{10,1... | collective-permute-start | bytes 786440 | tf_op jit(solution)/shard_map/ppermute | solution.py:17
  31.5 28.7 %collective-permute-start.9 = (bf16[128,1024]{1,0:T(8,128)(2,1)}, bf16[128,1024]{1,0:T(8,128)(2,1)S(1)}, u32[]{:S(2)}, u32[]{:S(2)}) collective-permute-start(bf16[128,1024]{1,0:T(8,128)(2,1)} %refs_0_.2), channel_id=1, source_target_pairs={{0,3},{1,0},{2,1},{3,2},{4,7},{5,4},{6,5},{7,6},{8,11},{9,8},{10,9... | collective-permute-start | bytes 786440 | tf_op jit(solution)/shard_map/ppermute | solution.py:17
  34.8 25.4 %collective-permute-start.8 = (bf16[128,1024]{1,0:T(8,128)(2,1)}, bf16[128,1024]{1,0:T(8,128)(2,1)S(1)}, u32[]{:S(2)}, u32[]{:S(2)}) collective-permute-start(bf16[128,1024]{1,0:T(8,128)(2,1)} %refs_0_.2), channel_id=1, source_target_pairs={{0,2},{1,3},{2,0},{3,1},{4,6},{5,7},{6,4},{7,5},{8,10},{9,11},{10,... | collective-permute-start | bytes 786440 | tf_op jit(solution)/shard_map/ppermute | solution.py:17
  39.8 20.3 %collective-permute-start.13 = (bf16[128,1024]{1,0:T(8,128)(2,1)S(1)}, bf16[128,1024]{1,0:T(8,128)(2,1)S(1)}, u32[]{:S(2)}, u32[]{:S(2)}) collective-permute-start(bf16[128,1024]{1,0:T(8,128)(2,1)S(1)} %collective-permute-done.10.refs_4_), channel_id=1, source_target_pairs={{0,3},{1,0},{2,1},{3,2},{4,7},{5,4},{6,5},{7,6},{8,11},{9,8},{10,9... | collective-permute-start | bytes 786440 | tf_op jit(solution)/shard_map/ppermute | solution.py:17
  44.0 16.2 %collective-permute-start.12 = (bf16[128,1024]{1,0:T(8,128)(2,1)S(1)}, bf16[128,1024]{1,0:T(8,128)(2,1)S(1)}, u32[]{:S(2)}, u32[]{:S(2)}) collective-permute-start(bf16[128,1024]{1,0:T(8,128)(2,1)S(1)} %collective-permute-done.10.refs_4_), channel_id=1, source_target_pairs={{0,2},{1,3},{2,0},{3,1},{4,6},{5,7},{6,4},{7,5},{8,10},{9,11},{10,... | collective-permute-start | bytes 786440 | tf_op jit(solution)/shard_map/ppermute | solution.py:17
  44.1 16.2 %collective-permute-start.11 = (bf16[128,1024]{1,0:T(8,128)(2,1)S(1)}, bf16[128,1024]{1,0:T(8,128)(2,1)S(1)}, u32[]{:S(2)}, u32[]{:S(2)}) collective-permute-start(bf16[128,1024]{1,0:T(8,128)(2,1)S(1)} %collective-permute-done.10.refs_4_), channel_id=1, source_target_pairs={{0,1},{1,2},{2,3},{3,0},{4,5},{5,6},{6,7},{7,4},{8,9},{9,10},{10,1... | collective-permute-start | bytes 786440 | tf_op jit(solution)/shard_map/ppermute | solution.py:17
  61.1 23.3 %collective-permute-start.14 = (bf16[2,128,1024]{2,1,0:T(8,128)(2,1)}, bf16[2,128,1024]{2,1,0:T(8,128)(2,1)S(1)}, u32[]{:S(2)}, u32[]{:S(2)}) collective-permute-start(bf16[2,128,1024]{2,1,0:T(8,128)(2,1)} %get-tuple-element.86), channel_id=1, source_target_pairs={{0,3},{1,0},{2,1},{3,2},{4,7},{5,4},{6,5},{7,6},{8,11},{9,8},{10,9... | collective-permute-start | bytes 1572872 | tf_op jit(solution)/shard_map/ppermute | solution.py:17
  63.4 20.9 %collective-permute-start.15 = (bf16[2,128,1024]{2,1,0:T(8,128)(2,1)}, bf16[2,128,1024]{2,1,0:T(8,128)(2,1)S(1)}, u32[]{:S(2)}, u32[]{:S(2)}) collective-permute-start(bf16[2,128,1024]{2,1,0:T(8,128)(2,1)} %get-tuple-element.87), channel_id=1, source_target_pairs={{0,2},{1,3},{2,0},{3,1},{4,6},{5,7},{6,4},{7,5},{8,10},{9,11},{10,... | collective-permute-start | bytes 1572872 | tf_op jit(solution)/shard_map/ppermute | solution.py:17
  65.7 18.7 %collective-permute-start.16 = (bf16[2,128,1024]{2,1,0:T(8,128)(2,1)}, bf16[2,128,1024]{2,1,0:T(8,128)(2,1)S(1)}, u32[]{:S(2)}, u32[]{:S(2)}) collective-permute-start(bf16[2,128,1024]{2,1,0:T(8,128)(2,1)} %get-tuple-element.88), channel_id=1, source_target_pairs={{0,1},{1,2},{2,3},{3,0},{4,5},{5,6},{6,7},{7,4},{8,9},{9,10},{10,1... | collective-permute-start | bytes 1572872 | tf_op jit(solution)/shard_map/ppermute | solution.py:17
  84.7 23.1 %collective-permute-start.19 = (bf16[128,1024]{1,0:T(8,128)(2,1)S(1)}, bf16[128,1024]{1,0:T(8,128)(2,1)}, u32[]{:S(2)}, u32[]{:S(2)}) collective-permute-start(bf16[128,1024]{1,0:T(8,128)(2,1)S(1)} %fusion.9), channel_id=1, source_target_pairs={{0,4},{4,0},{1,5},{5,1},{2,6},{6,2},{3,7},{7,3},{8,12},{12,8},{9,1... | collective-permute-start | bytes 786440 | tf_op jit(solution)/shard_map/ppermute | solution.py:17
  93.4 14.4 %collective-permute-start.18 = (bf16[4,4,32,1024]{3,2,1,0:T(8,128)(2,1)}, bf16[4,4,32,1024]{3,2,1,0:T(8,128)(2,1)S(1)}, u32[]{:S(2)}, u32[]{:S(2)}) collective-permute-start(bf16[4,4,32,1024]{3,2,1,0:T(8,128)(2,1)} %get-tuple-element.123), channel_id=1, source_target_pairs={{0,8},{8,0},{1,9},{9,1},{2,10},{10,2},{3,11},{11,3},{4,12},{12,4},... | collective-permute-start | bytes 3145736 | tf_op jit(solution)/shard_map/ppermute | solution.py:17
  94.8 14.2 %collective-permute-start.20 = (bf16[4,32,2048]{2,1,0:T(8,128)(2,1)S(1)}, bf16[4,32,2048]{2,1,0:T(8,128)(2,1)S(1)}, u32[]{:S(2)}, u32[]{:S(2)}) collective-permute-start(bf16[4,32,2048]{2,1,0:T(8,128)(2,1)S(1)} %get-tuple-element.125), channel_id=1, source_target_pairs={{0,16},{16,32},{32,48},{48,0},{1,17},{17,33},{33,49},{49,1},{2,18}... | collective-permute-start | bytes 1572872 | tf_op jit(solution)/shard_map/ppermute | solution.py:17
  95.3 26.3 %collective-permute-start.21 = (bf16[4,32,2048]{2,1,0:T(8,128)(2,1)S(1)}, bf16[4,32,2048]{2,1,0:T(8,128)(2,1)S(1)}, u32[]{:S(2)}, u32[]{:S(2)}) collective-permute-start(bf16[4,32,2048]{2,1,0:T(8,128)(2,1)S(1)} %get-tuple-element.126), channel_id=1, source_target_pairs={{0,48},{16,0},{32,16},{48,32},{1,49},{17,1},{33,17},{49,33},{2,50}... | collective-permute-start | bytes 1572872 | tf_op jit(solution)/shard_map/ppermute | solution.py:17
  106.4 19.8 %collective-permute-start.22 = (bf16[4,32,2048]{2,1,0:T(8,128)(2,1)S(1)}, bf16[4,32,2048]{2,1,0:T(8,128)(2,1)S(1)}, u32[]{:S(2)}, u32[]{:S(2)}) collective-permute-start(bf16[4,32,2048]{2,1,0:T(8,128)(2,1)S(1)} %get-tuple-element.130), channel_id=1, source_target_pairs={{0,32},{16,48},{32,0},{48,16},{1,33},{17,49},{33,1},{49,17},{2,34}... | collective-permute-start | bytes 1572872 | tf_op jit(solution)/shard_map/ppermute | solution.py:17
  123.9 16.3 %collective-permute-start.24 = (bf16[2,128,1024]{2,1,0:T(8,128)(2,1)}, bf16[2,128,1024]{2,1,0:T(8,128)(2,1)}, u32[]{:S(2)}, u32[]{:S(2)}) collective-permute-start(bf16[2,128,1024]{2,1,0:T(8,128)(2,1)} %get-tuple-element.134), channel_id=1, source_target_pairs={{0,1},{1,2},{2,3},{3,0},{4,5},{5,6},{6,7},{7,4},{8,9},{9,10},{10,1... | collective-permute-start | bytes 1572872 | tf_op jit(solution)/shard_map/ppermute | solution.py:17
  141.3 24.9 %all-to-all-start = ((bf16[4,32,2048]{2,1,0:T(8,128)(2,1)}), bf16[4,32,2048]{2,1,0:T(8,128)(2,1)S(1)}, u32[]{:S(2)}, u32[]{:S(2)}) async-start(bf16[4,32,2048]{2,1,0:T(8,128)(2,1)} %add_convert_fusion), calls=%async_computation | async-start | bytes 1048576 | tf_op jit(solution)/shard_map/all_to_all | solution.py:33
  (28 other events, 348.9 us)

commit v7 on v6

--- a/solution.py
+++ b/solution.py
@@ -9,7 +9,7 @@
 AXES = ("zlo", "x", "core", "zhi", "y")
 SIZES = {"zlo": 4, "x": 4, "core": 2, "zhi": 2, "y": 4}
 F32, BF16 = jnp.float32, jnp.bfloat16
-TILE = 256
+TILE = 512
 
 
 def send(value, axis, step):
@@ -61,24 +61,19 @@
 
 def put_rows(value, own, s1, s2, s3):
     i = pl.program_id(0)
-    half = value.shape[0] // 2
-
-    @pl.when(i % 2 == 0)
-    def _():
-        own[pl.ds(i // 2, 1)] = value[:half][None]
-        s1[pl.ds(i // 2, 1)] = value[half:].astype(BF16)[None]
-
-    @pl.when(i % 2 == 1)
-    def _():
-        s2[pl.ds(i // 2, 1)] = value[:half].astype(BF16)[None]
-        s3[pl.ds(i // 2, 1)] = value[half:].astype(BF16)[None]
+    n = own.shape[1]
+    own[pl.ds(i, 1)] = value[:n][None]
+    for k, piece in enumerate((s1, s2, s3), 1):
+        piece[pl.ds(i, 1)] = value[k * n : (k + 1) * n].astype(BF16)[None]
 
 
 def put_grad(value, core, own, other):
-    v = value.reshape(4, 2, value.shape[0] // 8, value.shape[1])
     first = core == 0
-    own[...] = jnp.where(first, v[:, 0], v[:, 1]).astype(BF16)[:, None]
-    other[...] = jnp.where(first, v[:, 1], v[:, 0]).astype(BF16)[:, None]
+    zs = own.shape[1]
+    v = value.reshape(zs, 4, 2, value.shape[0] // (8 * zs), value.shape[1])
+    for z in range(zs):
+        own[:, z] = jnp.where(first, v[z, :, 0], v[z, :, 1]).astype(BF16)
+        other[:, z] = jnp.where(first, v[z, :, 1], v[z, :, 0]).astype(BF16)
 
 
 def forward_kernel(second_ref, *refs):
@@ -195,11 +190,11 @@
     pieces = [whole(sds((2, block, width), t)) for t in (F32, BF16, BF16, BF16)]
 
     def run(kernel, ins, outs, flops, *scalars):
-        return call(kernel, 4, ins, outs, flops, len(scalars))(*scalars, *(a for *_, a in ins))
+        return call(kernel, steps, ins, outs, flops, len(scalars))(*scalars, *(a for *_, a in ins))
 
     def outer(left, right, cost):
         columns = right.shape[1]
-        outs = [tiled(sds((4, 4, own_rows, columns), BF16), 1, 1)] * 2
+        outs = [tiled(sds((4, 4, own_rows, columns), BF16), 1, 4 // steps)] * 2
         own, other = run(outer_kernel, [tiled(left, 1, TILE), whole(right)], outs, cost, core)
         return own, send(other, "core", 1)
 
@@ -236,8 +231,8 @@
     in_y = sends(in_y, "y", -1)
     down, down_x = pick(add(down.astype(F32), [down_c]), "x")
     output = (out[0] + far_out.astype(F32)) * scale[:block]
-    down, down_x, both, both_x, output, in_y[0], in_y[2] = tie(down, down_x, both, both_x, output, in_y[0], in_y[2])
     down_x = sends(down_x, "x")
+    both, both_x, output, in_y[0], in_y[2], down_x[0], down_x[2] = tie(both, both_x, output, in_y[0], in_y[2], down_x[0], down_x[2])
     both = exchange(add(both, both_x).astype(BF16), "zlo")
     down, down_x, both, near, in_y[1] = tie(down, down_x, both, near, in_y[1])
     near = add(near, in_y)

time: 185 us -> 177 us (0.957)
  the two profiles are of different devices: /device:TPU:6 before, /device:TPU:8 now
where the time goes in v7:
time: 177 us
  starting transfers between devices  73 us (41%)
  Pallas kernels  45.4 us (26%)
  waiting for transfers between devices  42.4 us (24%)
  other arithmetic  9.13 us (5%)
  local copies, waits for them, and re-layouts  6.07 us (3%)
    ppermute x30, starting transfers between devices, send(): return lax.ppermute(value, axis, [(i, (i + step) % n) for i in range(n)])  61.1 us
    pallas_call x5, Pallas kernels, run(): call(kernel, steps, ins, outs, flops, len(scalars))  45.4 us
    ppermute x30, waiting for transfers between devices, send(): return lax.ppermute(value, axis, [(i, (i + step) % n) for i in range(n)])  34.9 us
    all_to_all x2, starting transfers between devices, exchange(): return lax.all_to_all(value, axis, 0, 0, tiled=True)  11.9 us
    all_to_all x2, waiting for transfers between devices, exchange(): return lax.all_to_all(value, axis, 0, 0, tiled=True)  7.49 us
    add x6, other arithmetic, add(): own = own + piece.astype(F32)  3.56 us
  transfers between devices with their start and end apart: 32, of which 12 were waited for; matrix products, arithmetic and copies ran while one was open for 5% of the time, Pallas kernels for 26%

profile of v7, /device:TPU:8, one launch (start us, length us, event | category | flops | bytes accessed | tf_op | source)
XLA Modules:
  0.0 177.1 jit_solution(138266282109994260)
XLA Ops:
  0.6 7.3 %collective-permute-start.3 = (bf16[128,1024]{1,0:T(8,128)(2,1)}, bf16[128,1024]{1,0:T(8,128)(2,1)S(1)}, u32[]{:S(2)}, u32[]{:S(2)}) collective-permute-start(bf16[128,1024]{1,0:T(8,128)(2,1)} %refs_0_.1), channel_id=1, source_target_pairs={{0,4},{4,0},{1,5},{5,1},{2,6},{6,2},{3,7},{7,3},{8,12},{12,8},{9,1... | collective-permute-start | bytes 786440 | tf_op jit(solution)/shard_map/ppermute | solution.py:17
  13.1 2.5 %collective-permute-done.3.refs_4_ = bf16[128,1024]{1,0:T(8,128)(2,1)S(1)} collective-permute-done((bf16[128,1024]{1,0:T(8,128)(2,1)}, bf16[128,1024]{1,0:T(8,128)(2,1)S(1)}, u32[]{:S(2)}, u32[]{:S(2)}) %collective-permute-start.3) | collective-permute-done | bytes 262176 | tf_op jit(solution)/shard_map/ppermute | solution.py:17
  15.6 9.5 %collective-permute-start.10 = (bf16[128,1024]{1,0:T(8,128)(2,1)}, bf16[128,1024]{1,0:T(8,128)(2,1)S(1)}, u32[]{:S(2)}, u32[]{:S(2)}) collective-permute-start(bf16[128,1024]{1,0:T(8,128)(2,1)} %refs_0_.2), channel_id=1, source_target_pairs={{0,4},{4,0},{1,5},{5,1},{2,6},{6,2},{3,7},{7,3},{8,12},{12,8},{9,1... | collective-permute-start | bytes 786440 | tf_op jit(solution)/shard_map/ppermute | solution.py:17
  25.5 2.6 %collective-permute-start.6 = (bf16[128,1024]{1,0:T(8,128)(2,1)S(1)}, bf16[128,1024]{1,0:T(8,128)(2,1)}, u32[]{:S(2)}, u32[]{:S(2)}) collective-permute-start(bf16[128,1024]{1,0:T(8,128)(2,1)S(1)} %collective-permute-done.3.refs_4_), channel_id=1, source_target_pairs={{0,2},{1,3},{2,0},{3,1},{4,6},{5,7},{6,4},{7,5},{8,10},{9,11},{10,... | collective-permute-start | bytes 786440 | tf_op jit(solution)/shard_map/ppermute | solution.py:17
  31.9 2.9 %collective-permute-done.10.refs_4_ = bf16[128,1024]{1,0:T(8,128)(2,1)S(1)} collective-permute-done((bf16[128,1024]{1,0:T(8,128)(2,1)}, bf16[128,1024]{1,0:T(8,128)(2,1)S(1)}, u32[]{:S(2)}, u32[]{:S(2)}) %collective-permute-start.10) | collective-permute-done | bytes 262176 | tf_op jit(solution)/shard_map/ppermute | solution.py:17
  37.1 3.2 %collective-permute-start.13 = (bf16[128,1024]{1,0:T(8,128)(2,1)S(1)}, bf16[128,1024]{1,0:T(8,128)(2,1)S(1)}, u32[]{:S(2)}, u32[]{:S(2)}) collective-permute-start(bf16[128,1024]{1,0:T(8,128)(2,1)S(1)} %collective-permute-done.10.refs_4_), channel_id=1, source_target_pairs={{0,3},{1,0},{2,1},{3,2},{4,7},{5,4},{6,5},{7,6},{8,11},{9,8},{10,9... | collective-permute-start | bytes 786440 | tf_op jit(solution)/shard_map/ppermute | solution.py:17
  43.4 2.5 %collective-permute-start.11 = (bf16[128,1024]{1,0:T(8,128)(2,1)S(1)}, bf16[128,1024]{1,0:T(8,128)(2,1)S(1)}, u32[]{:S(2)}, u32[]{:S(2)}) collective-permute-start(bf16[128,1024]{1,0:T(8,128)(2,1)S(1)} %collective-permute-done.10.refs_4_), channel_id=1, source_target_pairs={{0,1},{1,2},{2,3},{3,0},{4,5},{5,6},{6,7},{7,4},{8,9},{9,10},{10,1... | collective-permute-start | bytes 786440 | tf_op jit(solution)/shard_map/ppermute | solution.py:17
  46.0 13.6 %shard_map.110 = (bf16[1024,1024]{1,0:T(8,128)(2,1)}, bf16[1024,1024]{1,0:T(8,128)(2,1)}, f32[1024,512]{1,0:T(8,128)}, f32[1024,512]{1,0:T(8,128)}, f32[2,128,10...) custom-call(s32[1024,1]{1,0:T(8,128)} %copy.15.second_ref, ...), custom_call_target="tpu_custom_call" | custom-call | flops 6442450944 | bytes 16106127 | tf_op jit(solution)/shard_map/pallas_call | solution.py:193
  61.7 2.5 %collective-permute-start.16 = (bf16[2,128,1024]{2,1,0:T(8,128)(2,1)}, bf16[2,128,1024]{2,1,0:T(8,128)(2,1)S(1)}, u32[]{:S(2)}, u32[]{:S(2)}) collective-permute-start(bf16[2,128,1024]{2,1,0:T(8,128)(2,1)} %get-tuple-element.86), channel_id=1, source_target_pairs={{0,1},{1,2},{2,3},{3,0},{4,5},{5,6},{6,7},{7,4},{8,9},{9,10},{10,1... | collective-permute-start | bytes 1572872 | tf_op jit(solution)/shard_map/ppermute | solution.py:17
  65.3 8.3 %shard_map.111 = (bf16[1024,1024]{1,0:T(8,128)(2,1)}, bf16[1024,2048]{1,0:T(8,128)(2,1)}) custom-call(s32[1024,1]{1,0:T(8,128)} %copy.15.second_ref, f32[1024,1]{1,0:T(8,128)} %copy.17.scale_ref, bf16[128,1024]{1,0:T(8,128)(2,1)} %refs_0_.2, bf16[128,1024]{1,0:T(8,128)(2,1)} %copy-done.7, bf16[128,1024]{1,0:T(8,128)(2,1)} %copy-done.10, ...), custom_call_target="tpu_custom_call" | custom-call | flops 107374184 | bytes 268435 | tf_op jit(solution)/shard_map/pallas_call | solution.py:193
  73.6 8.8 %shard_map.112 = (bf16[4,4,32,2048]{3,2,1,0:T(8,128)(2,1)}, bf16[4,4,32,2048]{3,2,1,0:T(8,128)(2,1)}) custom-call(s32[1]{0:T(128)} %bitcast.core_ref, bf16[1024,1024]{1,0:T(8,128)(2,1)} %get-tuple-element.87.left, bf16[1024,2048]{1,0:T(8,128)(2,1)} %get-tuple-element.116.right.gu), custom_call_target="tpu_custom_call" | custom-call | flops 214748368 | bytes 536870 | tf_op jit(solution)/shard_map/pallas_call | solution.py:193
  84.7 5.7 %shard_map.113 = (bf16[4,4,32,1024]{3,2,1,0:T(8,128)(2,1)}, bf16[4,4,32,1024]{3,2,1,0:T(8,128)(2,1)}) custom-call(s32[1]{0:T(128)} %bitcast.core_ref, bf16[1024,1024]{1,0:T(8,128)(2,1)} %get-tuple-element.107.left, bf16[1024,1024]{1,0:T(8,128)(2,1)} %get-tuple-element.108.right), custom_call_target="tpu_custom_call" | custom-call | flops 17179869184 | bytes 42949672 | tf_op jit(solution)/shard_map/pallas_call | solution.py:193
  96.9 9.0 %shard_map.114 = (f32[2,128,1024]{2,1,0:T(8,128)}, bf16[2,128,1024]{2,1,0:T(8,128)(2,1)}, bf16[2,128,1024]{2,1,0:T(8,128)(2,1)}, bf16[2,128,1024]{2,1,0:T(8,128)(2,1)}) custom-call(bf16[1024,2048]{1,0:T(8,128)(2,1)} %get-tuple-element.116.right.gu, bf16[2,1024,512]{2,1,0:T(8,128)(2,1)} %wg.1, bf16[2,1024,512]{2,1,0:T(8,128)(2,1)} %wu.1), custom_call_target="tpu_custom_call" | custom-call | flops 17179869184 | bytes 42949672 | tf_op jit(solution)/shard_map/pallas_call | solution.py:193
  107.2 9.6 %collective-permute-done.21 = bf16[4,32,2048]{2,1,0:T(8,128)(2,1)S(1)} collective-permute-done((bf16[4,32,2048]{2,1,0:T(8,128)(2,1)S(1)}, bf16[4,32,2048]{2,1,0:T(8,128)(2,1)S(1)}, u32[]{:S(2)}, u32[]{:S(2)}) %collective-permute-start.21) | collective-permute-done | bytes 524320 | tf_op jit(solution)/shard_map/ppermute | solution.py:17
  119.5 4.2 %collective-permute-start.26 = (bf16[4,32,1024]{2,1,0:T(8,128)(2,1)S(1)}, bf16[4,32,1024]{2,1,0:T(8,128)(2,1)S(1)}, u32[]{:S(2)}, u32[]{:S(2)}) collective-permute-start(bf16[4,32,1024]{2,1,0:T(8,128)(2,1)S(1)} %get-tuple-element.155), channel_id=1, source_target_pairs={{0,48},{16,0},{32,16},{48,32},{1,49},{17,1},{33,17},{49,33},{2,50}... | collective-permute-start | bytes 786440 | tf_op jit(solution)/shard_map/ppermute | solution.py:17
  124.5 3.1 %collective-permute-done.26 = bf16[4,32,1024]{2,1,0:T(8,128)(2,1)S(1)} collective-permute-done((bf16[4,32,1024]{2,1,0:T(8,128)(2,1)S(1)}, bf16[4,32,1024]{2,1,0:T(8,128)(2,1)S(1)}, u32[]{:S(2)}, u32[]{:S(2)}) %collective-permute-start.26) | collective-permute-done | bytes 262176 | tf_op jit(solution)/shard_map/ppermute | solution.py:17
  127.6 3.7 %collective-permute-done.25 = bf16[4,32,1024]{2,1,0:T(8,128)(2,1)S(1)} collective-permute-done((bf16[4,32,1024]{2,1,0:T(8,128)(2,1)S(1)}, bf16[4,32,1024]{2,1,0:T(8,128)(2,1)S(1)}, u32[]{:S(2)}, u32[]{:S(2)}) %collective-permute-start.25) | collective-permute-done | bytes 262176 | tf_op jit(solution)/shard_map/ppermute | solution.py:17
  133.5 8.5 %all-to-all-start = ((bf16[4,32,2048]{2,1,0:T(8,128)(2,1)}), bf16[4,32,2048]{2,1,0:T(8,128)(2,1)S(1)}, u32[]{:S(2)}, u32[]{:S(2)}) async-start(bf16[4,32,2048]{2,1,0:T(8,128)(2,1)} %add_convert_fusion), calls=%async_computation | async-start | bytes 1048576 | tf_op jit(solution)/shard_map/all_to_all | solution.py:33
  142.0 2.8 %collective-permute-start.28 = (bf16[2,128,1024]{2,1,0:T(8,128)(2,1)}, bf16[2,128,1024]{2,1,0:T(8,128)(2,1)}, u32[]{:S(2)}, u32[]{:S(2)}) collective-permute-start(bf16[2,128,1024]{2,1,0:T(8,128)(2,1)} %get-tuple-element.141), channel_id=1, source_target_pairs={{0,2},{1,3},{2,0},{3,1},{4,6},{5,7},{6,4},{7,5},{8,10},{9,11},{10,... | collective-permute-start | bytes 1572872 | tf_op jit(solution)/shard_map/ppermute | solution.py:17
  144.8 7.9 %collective-permute-done.27 = bf16[4,32,1024]{2,1,0:T(8,128)(2,1)} collective-permute-done((bf16[4,32,1024]{2,1,0:T(8,128)(2,1)S(1)}, bf16[4,32,1024]{2,1,0:T(8,128)(2,1)}, u32[]{:S(2)}, u32[]{:S(2)}) %collective-permute-start.27) | collective-permute-done | bytes 262176 | tf_op jit(solution)/shard_map/ppermute | solution.py:17
  153.0 5.2 %all-to-all-done = bf16[4,32,2048]{2,1,0:T(8,128)(2,1)S(1)} async-done(((bf16[4,32,2048]{2,1,0:T(8,128)(2,1)}), bf16[4,32,2048]{2,1,0:T(8,128)(2,1)S(1)}, u32[]{:S(2)}, u32[]{:S(2)}) %all-to-all-start) | async-done | bytes 524320 | tf_op jit(solution)/shard_map/all_to_all | solution.py:33
  160.5 3.8 %collective-permute-start.29 = (bf16[128,1024]{1,0:T(8,128)(2,1)S(1)}, bf16[128,1024]{1,0:T(8,128)(2,1)S(1)}, u32[]{:S(2)}, u32[]{:S(2)}) collective-permute-start(bf16[128,1024]{1,0:T(8,128)(2,1)S(1)} %fusion.10), channel_id=1, source_target_pairs={{0,4},{4,0},{1,5},{5,1},{2,6},{6,2},{3,7},{7,3},{8,12},{12,8},{9,1... | collective-permute-start | bytes 786440 | tf_op jit(solution)/shard_map/ppermute | solution.py:17
  166.1 3.4 %all-to-all-start.1 = ((bf16[4,32,1024]{2,1,0:T(8,128)(2,1)}), bf16[4,32,1024]{2,1,0:T(8,128)(2,1)S(1)}, u32[]{:S(2)}, u32[]{:S(2)}) async-start(bf16[4,32,1024]{2,1,0:T(8,128)(2,1)} %add_convert_fusion.1), calls=%async_computation.1 | async-start | bytes 524288 | tf_op jit(solution)/shard_map/all_to_all | solution.py:33
  170.3 3.0 %collective-permute-done.29 = bf16[128,1024]{1,0:T(8,128)(2,1)S(1)} collective-permute-done((bf16[128,1024]{1,0:T(8,128)(2,1)S(1)}, bf16[128,1024]{1,0:T(8,128)(2,1)S(1)}, u32[]{:S(2)}, u32[]{:S(2)}) %collective-permute-start.29) | collective-permute-done | bytes 262176 | tf_op jit(solution)/shard_map/ppermute | solution.py:17
  (127 shorter events, 42.5 us)
Async XLA Ops:
  0.6 14.9 %collective-permute-start.3 = (bf16[128,1024]{1,0:T(8,128)(2,1)}, bf16[128,1024]{1,0:T(8,128)(2,1)S(1)}, u32[]{:S(2)}, u32[]{:S(2)}) collective-permute-start(bf16[128,1024]{1,0:T(8,128)(2,1)} %refs_0_.1), channel_id=1, source_target_pairs={{0,4},{4,0},{1,5},{5,1},{2,6},{6,2},{3,7},{7,3},{8,12},{12,8},{9,1... | collective-permute-start | bytes 786440 | tf_op jit(solution)/shard_map/ppermute | solution.py:17
  7.9 17.1 %collective-permute-start.4 = (bf16[128,1024]{1,0:T(8,128)(2,1)}, bf16[128,1024]{1,0:T(8,128)(2,1)S(1)}, u32[]{:S(2)}, u32[]{:S(2)}) collective-permute-start(bf16[128,1024]{1,0:T(8,128)(2,1)} %refs_0_.2), channel_id=1, source_target_pairs={{0,1},{1,2},{2,3},{3,0},{4,5},{5,6},{6,7},{7,4},{8,9},{9,10},{10,1... | collective-permute-start | bytes 786440 | tf_op jit(solution)/shard_map/ppermute | solution.py:17
  9.5 16.0 %collective-permute-start.2 = (bf16[128,1024]{1,0:T(8,128)(2,1)}, bf16[128,1024]{1,0:T(8,128)(2,1)S(1)}, u32[]{:S(2)}, u32[]{:S(2)}) collective-permute-start(bf16[128,1024]{1,0:T(8,128)(2,1)} %refs_0_.1), channel_id=1, source_target_pairs={{0,3},{1,0},{2,1},{3,2},{4,7},{5,4},{6,5},{7,6},{8,11},{9,8},{10,9... | collective-permute-start | bytes 786440 | tf_op jit(solution)/shard_map/ppermute | solution.py:17
  9.9 18.2 %collective-permute-start.1 = (bf16[128,1024]{1,0:T(8,128)(2,1)}, bf16[128,1024]{1,0:T(8,128)(2,1)S(1)}, u32[]{:S(2)}, u32[]{:S(2)}) collective-permute-start(bf16[128,1024]{1,0:T(8,128)(2,1)} %refs_0_.1), channel_id=1, source_target_pairs={{0,2},{1,3},{2,0},{3,1},{4,6},{5,7},{6,4},{7,5},{8,10},{9,11},{10,... | collective-permute-start | bytes 786440 | tf_op jit(solution)/shard_map/ppermute | solution.py:17
  12.2 19.5 %collective-permute-start = (bf16[128,1024]{1,0:T(8,128)(2,1)}, bf16[128,1024]{1,0:T(8,128)(2,1)S(1)}, u32[]{:S(2)}, u32[]{:S(2)}) collective-permute-start(bf16[128,1024]{1,0:T(8,128)(2,1)} %refs_0_.1), channel_id=1, source_target_pairs={{0,1},{1,2},{2,3},{3,0},{4,5},{5,6},{6,7},{7,4},{8,9},{9,10},{10,1... | collective-permute-start | bytes 786440 | tf_op jit(solution)/shard_map/ppermute | solution.py:17
  15.6 19.2 %collective-permute-start.10 = (bf16[128,1024]{1,0:T(8,128)(2,1)}, bf16[128,1024]{1,0:T(8,128)(2,1)S(1)}, u32[]{:S(2)}, u32[]{:S(2)}) collective-permute-start(bf16[128,1024]{1,0:T(8,128)(2,1)} %refs_0_.2), channel_id=1, source_target_pairs={{0,4},{4,0},{1,5},{5,1},{2,6},{6,2},{3,7},{7,3},{8,12},{12,8},{9,1... | collective-permute-start | bytes 786440 | tf_op jit(solution)/shard_map/ppermute | solution.py:17
  25.5 15.5 %collective-permute-start.6 = (bf16[128,1024]{1,0:T(8,128)(2,1)S(1)}, bf16[128,1024]{1,0:T(8,128)(2,1)}, u32[]{:S(2)}, u32[]{:S(2)}) collective-permute-start(bf16[128,1024]{1,0:T(8,128)(2,1)S(1)} %collective-permute-done.3.refs_4_), channel_id=1, source_target_pairs={{0,2},{1,3},{2,0},{3,1},{4,6},{5,7},{6,4},{7,5},{8,10},{9,11},{10,... | collective-permute-start | bytes 786440 | tf_op jit(solution)/shard_map/ppermute | solution.py:17
  28.1 15.3 %collective-permute-start.5 = (bf16[128,1024]{1,0:T(8,128)(2,1)S(1)}, bf16[128,1024]{1,0:T(8,128)(2,1)}, u32[]{:S(2)}, u32[]{:S(2)}) collective-permute-start(bf16[128,1024]{1,0:T(8,128)(2,1)S(1)} %collective-permute-done.3.refs_4_), channel_id=1, source_target_pairs={{0,1},{1,2},{2,3},{3,0},{4,5},{5,6},{6,7},{7,4},{8,9},{9,10},{10,1... | collective-permute-start | bytes 786440 | tf_op jit(solution)/shard_map/ppermute | solution.py:17
  31.7 27.9 %collective-permute-start.9 = (bf16[128,1024]{1,0:T(8,128)(2,1)}, bf16[128,1024]{1,0:T(8,128)(2,1)S(1)}, u32[]{:S(2)}, u32[]{:S(2)}) collective-permute-start(bf16[128,1024]{1,0:T(8,128)(2,1)} %refs_0_.2), channel_id=1, source_target_pairs={{0,3},{1,0},{2,1},{3,2},{4,7},{5,4},{6,5},{7,6},{8,11},{9,8},{10,9... | collective-permute-start | bytes 786440 | tf_op jit(solution)/shard_map/ppermute | solution.py:17
  34.8 24.8 %collective-permute-start.8 = (bf16[128,1024]{1,0:T(8,128)(2,1)}, bf16[128,1024]{1,0:T(8,128)(2,1)S(1)}, u32[]{:S(2)}, u32[]{:S(2)}) collective-permute-start(bf16[128,1024]{1,0:T(8,128)(2,1)} %refs_0_.2), channel_id=1, source_target_pairs={{0,2},{1,3},{2,0},{3,1},{4,6},{5,7},{6,4},{7,5},{8,10},{9,11},{10,... | collective-permute-start | bytes 786440 | tf_op jit(solution)/shard_map/ppermute | solution.py:17
  37.1 22.6 %collective-permute-start.13 = (bf16[128,1024]{1,0:T(8,128)(2,1)S(1)}, bf16[128,1024]{1,0:T(8,128)(2,1)S(1)}, u32[]{:S(2)}, u32[]{:S(2)}) collective-permute-start(bf16[128,1024]{1,0:T(8,128)(2,1)S(1)} %collective-permute-done.10.refs_4_), channel_id=1, source_target_pairs={{0,3},{1,0},{2,1},{3,2},{4,7},{5,4},{6,5},{7,6},{8,11},{9,8},{10,9... | collective-permute-start | bytes 786440 | tf_op jit(solution)/shard_map/ppermute | solution.py:17
  41.0 18.6 %collective-permute-start.12 = (bf16[128,1024]{1,0:T(8,128)(2,1)S(1)}, bf16[128,1024]{1,0:T(8,128)(2,1)S(1)}, u32[]{:S(2)}, u32[]{:S(2)}) collective-permute-start(bf16[128,1024]{1,0:T(8,128)(2,1)S(1)} %collective-permute-done.10.refs_4_), channel_id=1, source_target_pairs={{0,2},{1,3},{2,0},{3,1},{4,6},{5,7},{6,4},{7,5},{8,10},{9,11},{10,... | collective-permute-start | bytes 786440 | tf_op jit(solution)/shard_map/ppermute | solution.py:17
  43.4 16.3 %collective-permute-start.11 = (bf16[128,1024]{1,0:T(8,128)(2,1)S(1)}, bf16[128,1024]{1,0:T(8,128)(2,1)S(1)}, u32[]{:S(2)}, u32[]{:S(2)}) collective-permute-start(bf16[128,1024]{1,0:T(8,128)(2,1)S(1)} %collective-permute-done.10.refs_4_), channel_id=1, source_target_pairs={{0,1},{1,2},{2,3},{3,0},{4,5},{5,6},{6,7},{7,4},{8,9},{9,10},{10,1... | collective-permute-start | bytes 786440 | tf_op jit(solution)/shard_map/ppermute | solution.py:17
  59.7 22.7 %collective-permute-start.14 = (bf16[2,128,1024]{2,1,0:T(8,128)(2,1)}, bf16[2,128,1024]{2,1,0:T(8,128)(2,1)S(1)}, u32[]{:S(2)}, u32[]{:S(2)}) collective-permute-start(bf16[2,128,1024]{2,1,0:T(8,128)(2,1)} %get-tuple-element.84), channel_id=1, source_target_pairs={{0,3},{1,0},{2,1},{3,2},{4,7},{5,4},{6,5},{7,6},{8,11},{9,8},{10,9... | collective-permute-start | bytes 1572872 | tf_op jit(solution)/shard_map/ppermute | solution.py:17
  59.8 22.6 %collective-permute-start.15 = (bf16[2,128,1024]{2,1,0:T(8,128)(2,1)}, bf16[2,128,1024]{2,1,0:T(8,128)(2,1)S(1)}, u32[]{:S(2)}, u32[]{:S(2)}) collective-permute-start(bf16[2,128,1024]{2,1,0:T(8,128)(2,1)} %get-tuple-element.85), channel_id=1, source_target_pairs={{0,2},{1,3},{2,0},{3,1},{4,6},{5,7},{6,4},{7,5},{8,10},{9,11},{10,... | collective-permute-start | bytes 1572872 | tf_op jit(solution)/shard_map/ppermute | solution.py:17
  61.7 20.7 %collective-permute-start.16 = (bf16[2,128,1024]{2,1,0:T(8,128)(2,1)}, bf16[2,128,1024]{2,1,0:T(8,128)(2,1)S(1)}, u32[]{:S(2)}, u32[]{:S(2)}) collective-permute-start(bf16[2,128,1024]{2,1,0:T(8,128)(2,1)} %get-tuple-element.86), channel_id=1, source_target_pairs={{0,1},{1,2},{2,3},{3,0},{4,5},{5,6},{6,7},{7,4},{8,9},{9,10},{10,1... | collective-permute-start | bytes 1572872 | tf_op jit(solution)/shard_map/ppermute | solution.py:17
  82.8 23.2 %collective-permute-start.19 = (bf16[128,1024]{1,0:T(8,128)(2,1)S(1)}, bf16[128,1024]{1,0:T(8,128)(2,1)S(1)}, u32[]{:S(2)}, u32[]{:S(2)}) collective-permute-start(bf16[128,1024]{1,0:T(8,128)(2,1)S(1)} %fusion.9), channel_id=1, source_target_pairs={{0,4},{4,0},{1,5},{5,1},{2,6},{6,2},{3,7},{7,3},{8,12},{12,8},{9,1... | collective-permute-start | bytes 786440 | tf_op jit(solution)/shard_map/ppermute | solution.py:17
  90.4 15.5 %collective-permute-start.18 = (bf16[4,4,32,1024]{3,2,1,0:T(8,128)(2,1)}, bf16[4,4,32,1024]{3,2,1,0:T(8,128)(2,1)S(1)}, u32[]{:S(2)}, u32[]{:S(2)}) collective-permute-start(bf16[4,4,32,1024]{3,2,1,0:T(8,128)(2,1)} %get-tuple-element.121), channel_id=1, source_target_pairs={{0,8},{8,0},{1,9},{9,1},{2,10},{10,2},{3,11},{11,3},{4,12},{12,4},... | collective-permute-start | bytes 3145736 | tf_op jit(solution)/shard_map/ppermute | solution.py:17
  91.8 15.4 %collective-permute-start.20 = (bf16[4,32,2048]{2,1,0:T(8,128)(2,1)S(1)}, bf16[4,32,2048]{2,1,0:T(8,128)(2,1)S(1)}, u32[]{:S(2)}, u32[]{:S(2)}) collective-permute-start(bf16[4,32,2048]{2,1,0:T(8,128)(2,1)S(1)} %get-tuple-element.123), channel_id=1, source_target_pairs={{0,16},{16,32},{32,48},{48,0},{1,17},{17,33},{33,49},{49,1},{2,18}... | collective-permute-start | bytes 1572872 | tf_op jit(solution)/shard_map/ppermute | solution.py:17
  93.4 23.4 %collective-permute-start.21 = (bf16[4,32,2048]{2,1,0:T(8,128)(2,1)S(1)}, bf16[4,32,2048]{2,1,0:T(8,128)(2,1)S(1)}, u32[]{:S(2)}, u32[]{:S(2)}) collective-permute-start(bf16[4,32,2048]{2,1,0:T(8,128)(2,1)S(1)} %get-tuple-element.124), channel_id=1, source_target_pairs={{0,48},{16,0},{32,16},{48,32},{1,49},{17,1},{33,17},{49,33},{2,50}... | collective-permute-start | bytes 1572872 | tf_op jit(solution)/shard_map/ppermute | solution.py:17
  95.1 29.4 %collective-permute-start.22 = (bf16[4,32,2048]{2,1,0:T(8,128)(2,1)S(1)}, bf16[4,32,2048]{2,1,0:T(8,128)(2,1)}, u32[]{:S(2)}, u32[]{:S(2)}) collective-permute-start(bf16[4,32,2048]{2,1,0:T(8,128)(2,1)S(1)} %get-tuple-element.126), channel_id=1, source_target_pairs={{0,32},{16,48},{32,0},{48,16},{1,33},{17,49},{33,1},{49,17},{2,34}... | collective-permute-start | bytes 1572872 | tf_op jit(solution)/shard_map/ppermute | solution.py:17
  116.8 14.4 %collective-permute-start.23 = (bf16[2,128,1024]{2,1,0:T(8,128)(2,1)}, bf16[2,128,1024]{2,1,0:T(8,128)(2,1)}, u32[]{:S(2)}, u32[]{:S(2)}) collective-permute-start(bf16[2,128,1024]{2,1,0:T(8,128)(2,1)} %get-tuple-element.129), channel_id=1, source_target_pairs={{0,3},{1,0},{2,1},{3,2},{4,7},{5,4},{6,5},{7,6},{8,11},{9,8},{10,9... | collective-permute-start | bytes 1572872 | tf_op jit(solution)/shard_map/ppermute | solution.py:17
  117.7 13.6 %collective-permute-start.24 = (bf16[2,128,1024]{2,1,0:T(8,128)(2,1)}, bf16[2,128,1024]{2,1,0:T(8,128)(2,1)}, u32[]{:S(2)}, u32[]{:S(2)}) collective-permute-start(bf16[2,128,1024]{2,1,0:T(8,128)(2,1)} %get-tuple-element.130), channel_id=1, source_target_pairs={{0,1},{1,2},{2,3},{3,0},{4,5},{5,6},{6,7},{7,4},{8,9},{9,10},{10,1... | collective-permute-start | bytes 1572872 | tf_op jit(solution)/shard_map/ppermute | solution.py:17
  133.5 24.7 %all-to-all-start = ((bf16[4,32,2048]{2,1,0:T(8,128)(2,1)}), bf16[4,32,2048]{2,1,0:T(8,128)(2,1)S(1)}, u32[]{:S(2)}, u32[]{:S(2)}) async-start(bf16[4,32,2048]{2,1,0:T(8,128)(2,1)} %add_convert_fusion), calls=%async_computation | async-start | bytes 1048576 | tf_op jit(solution)/shard_map/all_to_all | solution.py:33
  (34 other events, 406.4 us)

commit v8 on v7

--- a/solution.py
+++ b/solution.py
@@ -233,12 +233,13 @@
     output = (out[0] + far_out.astype(F32)) * scale[:block]
     down_x = sends(down_x, "x")
     both, both_x, output, in_y[0], in_y[2], down_x[0], down_x[2] = tie(both, both_x, output, in_y[0], in_y[2], down_x[0], down_x[2])
-    both = exchange(add(both, both_x).astype(BF16), "zlo")
-    down, down_x, both, near, in_y[1] = tie(down, down_x, both, near, in_y[1])
+    both, both_z = pick(add(both, both_x), "zlo")
+    both_z = sends(both_z, "zlo")
+    down, down_x, both_z, near, in_y[1] = tie(down, down_x, both_z, near, in_y[1])
     near = add(near, in_y)
     far = send(near[1].astype(BF16), "zhi", 1)
     down = exchange(add(down, down_x).astype(BF16), "zlo")
-    both = add(both[0].astype(F32), both[1:]).reshape(own_rows, 2, EXP, ff)
+    both = add(both, both_z).reshape(own_rows, 2, EXP, ff)
     input_grad = near[0] + far.astype(F32)
     grad_down = add(down[0].astype(F32), down[1:]).reshape(own_rows, EXP, ff)
     return (

time: 177 us -> 193 us (1.090)
  the two profiles are of different devices: /device:TPU:8 before, /device:TPU:6 now
where the time goes in v8:
time: 193 us; the launch traced here: 190 us
  starting transfers between devices  66.2 us (34%)
  waiting for transfers between devices  56.7 us (29%)
  Pallas kernels  45.6 us (24%)
  other arithmetic  12.1 us (6%)
  local copies, waits for them, and re-layouts  8.66 us (4%)
    ppermute x33, starting transfers between devices, send(): return lax.ppermute(value, axis, [(i, (i + step) % n) for i in range(n)])  62.2 us
    ppermute x33, waiting for transfers between devices, send(): return lax.ppermute(value, axis, [(i, (i + step) % n) for i in range(n)])  56.7 us
    pallas_call x5, Pallas kernels, run(): call(kernel, steps, ins, outs, flops, len(scalars))  45.6 us
    add x7, other arithmetic, add(): own = own + piece.astype(F32)  7.35 us
    all_to_all x1, starting transfers between devices, exchange(): return lax.all_to_all(value, axis, 0, 0, tiled=True)  4.03 us
  transfers between devices with their start and end apart: 34, of which 15 were waited for; matrix products, arithmetic and copies ran while one was open for 9% of the time, Pallas kernels for 24%

profile of v8, /device:TPU:6, one launch (start us, length us, event | category | flops | bytes accessed | tf_op | source)
XLA Modules:
  0.0 190.3 jit_solution(77101494570325609)
XLA Ops:
  0.6 7.3 %collective-permute-start.3 = (bf16[128,1024]{1,0:T(8,128)(2,1)}, bf16[128,1024]{1,0:T(8,128)(2,1)S(1)}, u32[]{:S(2)}, u32[]{:S(2)}) collective-permute-start(bf16[128,1024]{1,0:T(8,128)(2,1)} %refs_0_.1), channel_id=1, source_target_pairs={{0,4},{4,0},{1,5},{5,1},{2,6},{6,2},{3,7},{7,3},{8,12},{12,8},{9,1... | collective-permute-start | bytes 786440 | tf_op jit(solution)/shard_map/ppermute | solution.py:17
  12.6 2.4 %collective-permute-start.2 = (bf16[128,1024]{1,0:T(8,128)(2,1)}, bf16[128,1024]{1,0:T(8,128)(2,1)S(1)}, u32[]{:S(2)}, u32[]{:S(2)}) collective-permute-start(bf16[128,1024]{1,0:T(8,128)(2,1)} %refs_0_.1), channel_id=1, source_target_pairs={{0,3},{1,0},{2,1},{3,2},{4,7},{5,4},{6,5},{7,6},{8,11},{9,8},{10,9... | collective-permute-start | bytes 786440 | tf_op jit(solution)/shard_map/ppermute | solution.py:17
  15.6 9.5 %collective-permute-start.10 = (bf16[128,1024]{1,0:T(8,128)(2,1)}, bf16[128,1024]{1,0:T(8,128)(2,1)S(1)}, u32[]{:S(2)}, u32[]{:S(2)}) collective-permute-start(bf16[128,1024]{1,0:T(8,128)(2,1)} %refs_0_.2), channel_id=1, source_target_pairs={{0,4},{4,0},{1,5},{5,1},{2,6},{6,2},{3,7},{7,3},{8,12},{12,8},{9,1... | collective-permute-start | bytes 786440 | tf_op jit(solution)/shard_map/ppermute | solution.py:17
  26.6 2.9 %collective-permute-start.6 = (bf16[128,1024]{1,0:T(8,128)(2,1)S(1)}, bf16[128,1024]{1,0:T(8,128)(2,1)}, u32[]{:S(2)}, u32[]{:S(2)}) collective-permute-start(bf16[128,1024]{1,0:T(8,128)(2,1)S(1)} %collective-permute-done.3.refs_4_), channel_id=1, source_target_pairs={{0,2},{1,3},{2,0},{3,1},{4,6},{5,7},{6,4},{7,5},{8,10},{9,11},{10,... | collective-permute-start | bytes 786440 | tf_op jit(solution)/shard_map/ppermute | solution.py:17
  34.8 3.0 %collective-permute-start.9 = (bf16[128,1024]{1,0:T(8,128)(2,1)}, bf16[128,1024]{1,0:T(8,128)(2,1)S(1)}, u32[]{:S(2)}, u32[]{:S(2)}) collective-permute-start(bf16[128,1024]{1,0:T(8,128)(2,1)} %refs_0_.2), channel_id=1, source_target_pairs={{0,3},{1,0},{2,1},{3,2},{4,7},{5,4},{6,5},{7,6},{8,11},{9,8},{10,9... | collective-permute-start | bytes 786440 | tf_op jit(solution)/shard_map/ppermute | solution.py:17
  37.8 4.7 %collective-permute-done.6.refs_6_ = bf16[128,1024]{1,0:T(8,128)(2,1)} collective-permute-done((bf16[128,1024]{1,0:T(8,128)(2,1)S(1)}, bf16[128,1024]{1,0:T(8,128)(2,1)}, u32[]{:S(2)}, u32[]{:S(2)}) %collective-permute-start.6) | collective-permute-done | bytes 262176 | tf_op jit(solution)/shard_map/ppermute | solution.py:17
  42.5 3.5 %collective-permute-start.12 = (bf16[128,1024]{1,0:T(8,128)(2,1)S(1)}, bf16[128,1024]{1,0:T(8,128)(2,1)S(1)}, u32[]{:S(2)}, u32[]{:S(2)}) collective-permute-start(bf16[128,1024]{1,0:T(8,128)(2,1)S(1)} %collective-permute-done.10.refs_4_), channel_id=1, source_target_pairs={{0,2},{1,3},{2,0},{3,1},{4,6},{5,7},{6,4},{7,5},{8,10},{9,11},{10,... | collective-permute-start | bytes 786440 | tf_op jit(solution)/shard_map/ppermute | solution.py:17
  46.1 2.5 %collective-permute-start.13 = (bf16[128,1024]{1,0:T(8,128)(2,1)S(1)}, bf16[128,1024]{1,0:T(8,128)(2,1)S(1)}, u32[]{:S(2)}, u32[]{:S(2)}) collective-permute-start(bf16[128,1024]{1,0:T(8,128)(2,1)S(1)} %collective-permute-done.10.refs_4_), channel_id=1, source_target_pairs={{0,3},{1,0},{2,1},{3,2},{4,7},{5,4},{6,5},{7,6},{8,11},{9,8},{10,9... | collective-permute-start | bytes 786440 | tf_op jit(solution)/shard_map/ppermute | solution.py:17
  48.6 13.6 %shard_map.110 = (bf16[1024,1024]{1,0:T(8,128)(2,1)}, bf16[1024,1024]{1,0:T(8,128)(2,1)}, f32[1024,512]{1,0:T(8,128)}, f32[1024,512]{1,0:T(8,128)}, f32[2,128,10...) custom-call(s32[1024,1]{1,0:T(8,128)} %copy.15.second_ref, ...), custom_call_target="tpu_custom_call" | custom-call | flops 6442450944 | bytes 16106127 | tf_op jit(solution)/shard_map/pallas_call | solution.py:193
  65.6 8.3 %shard_map.111 = (bf16[1024,1024]{1,0:T(8,128)(2,1)}, bf16[1024,2048]{1,0:T(8,128)(2,1)}) custom-call(s32[1024,1]{1,0:T(8,128)} %copy.15.second_ref, f32[1024,1]{1,0:T(8,128)} %copy.17.scale_ref, bf16[128,1024]{1,0:T(8,128)(2,1)} %refs_0_.2, bf16[128,1024]{1,0:T(8,128)(2,1)} %copy-done.8, bf16[128,1024]{1,0:T(8,128)(2,1)} %copy-done.10, ...), custom_call_target="tpu_custom_call" | custom-call | flops 107374184 | bytes 268435 | tf_op jit(solution)/shard_map/pallas_call | solution.py:193
  73.9 8.8 %shard_map.112 = (bf16[4,4,32,2048]{3,2,1,0:T(8,128)(2,1)}, bf16[4,4,32,2048]{3,2,1,0:T(8,128)(2,1)}) custom-call(s32[1]{0:T(128)} %bitcast.core_ref, bf16[1024,1024]{1,0:T(8,128)(2,1)} %get-tuple-element.89.left, bf16[1024,2048]{1,0:T(8,128)(2,1)} %get-tuple-element.118.right.gu), custom_call_target="tpu_custom_call" | custom-call | flops 214748368 | bytes 536870 | tf_op jit(solution)/shard_map/pallas_call | solution.py:193
  83.8 3.6 %collective-permute-done.16 = bf16[2,128,1024]{2,1,0:T(8,128)(2,1)} collective-permute-done((bf16[2,128,1024]{2,1,0:T(8,128)(2,1)}, bf16[2,128,1024]{2,1,0:T(8,128)(2,1)}, u32[]{:S(2)}, u32[]{:S(2)}) %collective-permute-start.16) | collective-permute-done | bytes 524320 | tf_op jit(solution)/shard_map/ppermute | solution.py:17
  89.0 5.9 %shard_map.113 = (bf16[4,4,32,1024]{3,2,1,0:T(8,128)(2,1)}, bf16[4,4,32,1024]{3,2,1,0:T(8,128)(2,1)}) custom-call(s32[1]{0:T(128)} %bitcast.core_ref, bf16[1024,1024]{1,0:T(8,128)(2,1)} %get-tuple-element.109.left, bf16[1024,1024]{1,0:T(8,128)(2,1)} %get-tuple-element.110.right), custom_call_target="tpu_custom_call" | custom-call | flops 17179869184 | bytes 42949672 | tf_op jit(solution)/shard_map/pallas_call | solution.py:193
  100.0 9.0 %shard_map.114 = (f32[2,128,1024]{2,1,0:T(8,128)}, bf16[2,128,1024]{2,1,0:T(8,128)(2,1)}, bf16[2,128,1024]{2,1,0:T(8,128)(2,1)}, bf16[2,128,1024]{2,1,0:T(8,128)(2,1)}) custom-call(bf16[1024,2048]{1,0:T(8,128)(2,1)} %get-tuple-element.118.right.gu, bf16[2,1024,512]{2,1,0:T(8,128)(2,1)} %wg.1, bf16[2,1024,512]{2,1,0:T(8,128)(2,1)} %wu.1), custom_call_target="tpu_custom_call" | custom-call | flops 17179869184 | bytes 42949672 | tf_op jit(solution)/shard_map/pallas_call | solution.py:193
  112.0 11.9 %collective-permute-done.21 = bf16[4,32,2048]{2,1,0:T(8,128)(2,1)S(1)} collective-permute-done((bf16[4,32,2048]{2,1,0:T(8,128)(2,1)S(1)}, bf16[4,32,2048]{2,1,0:T(8,128)(2,1)S(1)}, u32[]{:S(2)}, u32[]{:S(2)}) %collective-permute-start.21) | collective-permute-done | bytes 524320 | tf_op jit(solution)/shard_map/ppermute | solution.py:17
  131.3 2.7 %collective-permute-done.25 = bf16[4,32,1024]{2,1,0:T(8,128)(2,1)} collective-permute-done((bf16[4,32,1024]{2,1,0:T(8,128)(2,1)}, bf16[4,32,1024]{2,1,0:T(8,128)(2,1)}, u32[]{:S(2)}, u32[]{:S(2)}) %collective-permute-start.25) | collective-permute-done | bytes 262176 | tf_op jit(solution)/shard_map/ppermute | solution.py:17
  135.3 3.0 %collective-permute-done.23 = bf16[2,128,1024]{2,1,0:T(8,128)(2,1)} collective-permute-done((bf16[2,128,1024]{2,1,0:T(8,128)(2,1)}, bf16[2,128,1024]{2,1,0:T(8,128)(2,1)}, u32[]{:S(2)}, u32[]{:S(2)}) %collective-permute-start.23) | collective-permute-done | bytes 524320 | tf_op jit(solution)/shard_map/ppermute | solution.py:17
  138.2 8.6 %collective-permute-done.24 = bf16[2,128,1024]{2,1,0:T(8,128)(2,1)} collective-permute-done((bf16[2,128,1024]{2,1,0:T(8,128)(2,1)}, bf16[2,128,1024]{2,1,0:T(8,128)(2,1)}, u32[]{:S(2)}, u32[]{:S(2)}) %collective-permute-start.24) | collective-permute-done | bytes 524320 | tf_op jit(solution)/shard_map/ppermute | solution.py:17
  150.2 5.7 %collective-permute-start.28 = (bf16[32,2048]{1,0:T(8,128)(2,1)}, bf16[32,2048]{1,0:T(8,128)(2,1)S(1)}, u32[]{:S(2)}, u32[]{:S(2)}) collective-permute-start(bf16[32,2048]{1,0:T(8,128)(2,1)} %get-tuple-element.163), channel_id=1, source_target_pairs={{0,64},{64,128},{128,192},{192,0},{1,65},{65,129},{129,193},{193,1... | collective-permute-start | bytes 393224 | tf_op jit(solution)/shard_map/ppermute | solution.py:17
  155.9 2.9 %collective-permute-start.30 = (bf16[32,2048]{1,0:T(8,128)(2,1)}, bf16[32,2048]{1,0:T(8,128)(2,1)S(1)}, u32[]{:S(2)}, u32[]{:S(2)}) collective-permute-start(bf16[32,2048]{1,0:T(8,128)(2,1)} %get-tuple-element.161), channel_id=1, source_target_pairs={{0,192},{64,0},{128,64},{192,128},{1,193},{65,1},{129,65},{193,129... | collective-permute-start | bytes 393224 | tf_op jit(solution)/shard_map/ppermute | solution.py:17
  159.4 9.6 %collective-permute-done.29 = bf16[32,2048]{1,0:T(8,128)(2,1)S(1)} collective-permute-done((bf16[32,2048]{1,0:T(8,128)(2,1)}, bf16[32,2048]{1,0:T(8,128)(2,1)S(1)}, u32[]{:S(2)}, u32[]{:S(2)}) %collective-permute-start.29) | collective-permute-done | bytes 131104 | tf_op jit(solution)/shard_map/ppermute | solution.py:17
  171.1 4.0 %all-to-all-start = ((bf16[4,32,1024]{2,1,0:T(8,128)(2,1)}), bf16[4,32,1024]{2,1,0:T(8,128)(2,1)S(1)}, u32[]{:S(2)}, u32[]{:S(2)}) async-start(bf16[4,32,1024]{2,1,0:T(8,128)(2,1)} %add_convert_fusion), calls=%async_computation | async-start | bytes 524288 | tf_op jit(solution)/shard_map/all_to_all | solution.py:33
  178.2 3.8 %collective-permute-start.32 = (bf16[128,1024]{1,0:T(8,128)(2,1)S(1)}, bf16[128,1024]{1,0:T(8,128)(2,1)S(1)}, u32[]{:S(2)}, u32[]{:S(2)}) collective-permute-start(bf16[128,1024]{1,0:T(8,128)(2,1)S(1)} %fusion.10), channel_id=1, source_target_pairs={{0,4},{4,0},{1,5},{5,1},{2,6},{6,2},{3,7},{7,3},{8,12},{12,8},{9,1... | collective-permute-start | bytes 786440 | tf_op jit(solution)/shard_map/ppermute | solution.py:17
  182.8 5.9 %collective-permute-done.32 = bf16[128,1024]{1,0:T(8,128)(2,1)S(1)} collective-permute-done((bf16[128,1024]{1,0:T(8,128)(2,1)S(1)}, bf16[128,1024]{1,0:T(8,128)(2,1)S(1)}, u32[]{:S(2)}, u32[]{:S(2)}) %collective-permute-start.32) | collective-permute-done | bytes 262176 | tf_op jit(solution)/shard_map/ppermute | solution.py:17
  (128 shorter events, 46.1 us)
Async XLA Ops:
  0.6 14.9 %collective-permute-start.3 = (bf16[128,1024]{1,0:T(8,128)(2,1)}, bf16[128,1024]{1,0:T(8,128)(2,1)S(1)}, u32[]{:S(2)}, u32[]{:S(2)}) collective-permute-start(bf16[128,1024]{1,0:T(8,128)(2,1)} %refs_0_.1), channel_id=1, source_target_pairs={{0,4},{4,0},{1,5},{5,1},{2,6},{6,2},{3,7},{7,3},{8,12},{12,8},{9,1... | collective-permute-start | bytes 786440 | tf_op jit(solution)/shard_map/ppermute | solution.py:17
  7.9 17.1 %collective-permute-start.4 = (bf16[128,1024]{1,0:T(8,128)(2,1)}, bf16[128,1024]{1,0:T(8,128)(2,1)S(1)}, u32[]{:S(2)}, u32[]{:S(2)}) collective-permute-start(bf16[128,1024]{1,0:T(8,128)(2,1)} %refs_0_.2), channel_id=1, source_target_pairs={{0,1},{1,2},{2,3},{3,0},{4,5},{5,6},{6,7},{7,4},{8,9},{9,10},{10,1... | collective-permute-start | bytes 786440 | tf_op jit(solution)/shard_map/ppermute | solution.py:17
  9.5 17.1 %collective-permute-start = (bf16[128,1024]{1,0:T(8,128)(2,1)}, bf16[128,1024]{1,0:T(8,128)(2,1)S(1)}, u32[]{:S(2)}, u32[]{:S(2)}) collective-permute-start(bf16[128,1024]{1,0:T(8,128)(2,1)} %refs_0_.1), channel_id=1, source_target_pairs={{0,1},{1,2},{2,3},{3,0},{4,5},{5,6},{6,7},{7,4},{8,9},{9,10},{10,1... | collective-permute-start | bytes 786440 | tf_op jit(solution)/shard_map/ppermute | solution.py:17
  11.1 20.0 %collective-permute-start.1 = (bf16[128,1024]{1,0:T(8,128)(2,1)}, bf16[128,1024]{1,0:T(8,128)(2,1)S(1)}, u32[]{:S(2)}, u32[]{:S(2)}) collective-permute-start(bf16[128,1024]{1,0:T(8,128)(2,1)} %refs_0_.1), channel_id=1, source_target_pairs={{0,2},{1,3},{2,0},{3,1},{4,6},{5,7},{6,4},{7,5},{8,10},{9,11},{10,... | collective-permute-start | bytes 786440 | tf_op jit(solution)/shard_map/ppermute | solution.py:17
  12.6 20.3 %collective-permute-start.2 = (bf16[128,1024]{1,0:T(8,128)(2,1)}, bf16[128,1024]{1,0:T(8,128)(2,1)S(1)}, u32[]{:S(2)}, u32[]{:S(2)}) collective-permute-start(bf16[128,1024]{1,0:T(8,128)(2,1)} %refs_0_.1), channel_id=1, source_target_pairs={{0,3},{1,0},{2,1},{3,2},{4,7},{5,4},{6,5},{7,6},{8,11},{9,8},{10,9... | collective-permute-start | bytes 786440 | tf_op jit(solution)/shard_map/ppermute | solution.py:17
  15.6 19.2 %collective-permute-start.10 = (bf16[128,1024]{1,0:T(8,128)(2,1)}, bf16[128,1024]{1,0:T(8,128)(2,1)S(1)}, u32[]{:S(2)}, u32[]{:S(2)}) collective-permute-start(bf16[128,1024]{1,0:T(8,128)(2,1)} %refs_0_.2), channel_id=1, source_target_pairs={{0,4},{4,0},{1,5},{5,1},{2,6},{6,2},{3,7},{7,3},{8,12},{12,8},{9,1... | collective-permute-start | bytes 786440 | tf_op jit(solution)/shard_map/ppermute | solution.py:17
  26.6 15.9 %collective-permute-start.6 = (bf16[128,1024]{1,0:T(8,128)(2,1)S(1)}, bf16[128,1024]{1,0:T(8,128)(2,1)}, u32[]{:S(2)}, u32[]{:S(2)}) collective-permute-start(bf16[128,1024]{1,0:T(8,128)(2,1)S(1)} %collective-permute-done.3.refs_4_), channel_id=1, source_target_pairs={{0,2},{1,3},{2,0},{3,1},{4,6},{5,7},{6,4},{7,5},{8,10},{9,11},{10,... | collective-permute-start | bytes 786440 | tf_op jit(solution)/shard_map/ppermute | solution.py:17
  31.1 15.0 %collective-permute-start.7 = (bf16[128,1024]{1,0:T(8,128)(2,1)S(1)}, bf16[128,1024]{1,0:T(8,128)(2,1)}, u32[]{:S(2)}, u32[]{:S(2)}) collective-permute-start(bf16[128,1024]{1,0:T(8,128)(2,1)S(1)} %collective-permute-done.3.refs_4_), channel_id=1, source_target_pairs={{0,3},{1,0},{2,1},{3,2},{4,7},{5,4},{6,5},{7,6},{8,11},{9,8},{10,9... | collective-permute-start | bytes 786440 | tf_op jit(solution)/shard_map/ppermute | solution.py:17
  32.9 29.4 %collective-permute-start.8 = (bf16[128,1024]{1,0:T(8,128)(2,1)}, bf16[128,1024]{1,0:T(8,128)(2,1)S(1)}, u32[]{:S(2)}, u32[]{:S(2)}) collective-permute-start(bf16[128,1024]{1,0:T(8,128)(2,1)} %refs_0_.2), channel_id=1, source_target_pairs={{0,2},{1,3},{2,0},{3,1},{4,6},{5,7},{6,4},{7,5},{8,10},{9,11},{10,... | collective-permute-start | bytes 786440 | tf_op jit(solution)/shard_map/ppermute | solution.py:17
  34.8 27.5 %collective-permute-start.9 = (bf16[128,1024]{1,0:T(8,128)(2,1)}, bf16[128,1024]{1,0:T(8,128)(2,1)S(1)}, u32[]{:S(2)}, u32[]{:S(2)}) collective-permute-start(bf16[128,1024]{1,0:T(8,128)(2,1)} %refs_0_.2), channel_id=1, source_target_pairs={{0,3},{1,0},{2,1},{3,2},{4,7},{5,4},{6,5},{7,6},{8,11},{9,8},{10,9... | collective-permute-start | bytes 786440 | tf_op jit(solution)/shard_map/ppermute | solution.py:17
  37.8 24.5 %collective-permute-start.11 = (bf16[128,1024]{1,0:T(8,128)(2,1)S(1)}, bf16[128,1024]{1,0:T(8,128)(2,1)S(1)}, u32[]{:S(2)}, u32[]{:S(2)}) collective-permute-start(bf16[128,1024]{1,0:T(8,128)(2,1)S(1)} %collective-permute-done.10.refs_4_), channel_id=1, source_target_pairs={{0,1},{1,2},{2,3},{3,0},{4,5},{5,6},{6,7},{7,4},{8,9},{9,10},{10,1... | collective-permute-start | bytes 786440 | tf_op jit(solution)/shard_map/ppermute | solution.py:17
  42.5 19.8 %collective-permute-start.12 = (bf16[128,1024]{1,0:T(8,128)(2,1)S(1)}, bf16[128,1024]{1,0:T(8,128)(2,1)S(1)}, u32[]{:S(2)}, u32[]{:S(2)}) collective-permute-start(bf16[128,1024]{1,0:T(8,128)(2,1)S(1)} %collective-permute-done.10.refs_4_), channel_id=1, source_target_pairs={{0,2},{1,3},{2,0},{3,1},{4,6},{5,7},{6,4},{7,5},{8,10},{9,11},{10,... | collective-permute-start | bytes 786440 | tf_op jit(solution)/shard_map/ppermute | solution.py:17
  46.1 16.3 %collective-permute-start.13 = (bf16[128,1024]{1,0:T(8,128)(2,1)S(1)}, bf16[128,1024]{1,0:T(8,128)(2,1)S(1)}, u32[]{:S(2)}, u32[]{:S(2)}) collective-permute-start(bf16[128,1024]{1,0:T(8,128)(2,1)S(1)} %collective-permute-done.10.refs_4_), channel_id=1, source_target_pairs={{0,3},{1,0},{2,1},{3,2},{4,7},{5,4},{6,5},{7,6},{8,11},{9,8},{10,9... | collective-permute-start | bytes 786440 | tf_op jit(solution)/shard_map/ppermute | solution.py:17
  62.4 21.4 %collective-permute-start.14 = (bf16[2,128,1024]{2,1,0:T(8,128)(2,1)}, bf16[2,128,1024]{2,1,0:T(8,128)(2,1)}, u32[]{:S(2)}, u32[]{:S(2)}) collective-permute-start(bf16[2,128,1024]{2,1,0:T(8,128)(2,1)} %get-tuple-element.86), channel_id=1, source_target_pairs={{0,3},{1,0},{2,1},{3,2},{4,7},{5,4},{6,5},{7,6},{8,11},{9,8},{10,9... | collective-permute-start | bytes 1572872 | tf_op jit(solution)/shard_map/ppermute | solution.py:17
  63.3 20.5 %collective-permute-start.15 = (bf16[2,128,1024]{2,1,0:T(8,128)(2,1)}, bf16[2,128,1024]{2,1,0:T(8,128)(2,1)}, u32[]{:S(2)}, u32[]{:S(2)}) collective-permute-start(bf16[2,128,1024]{2,1,0:T(8,128)(2,1)} %get-tuple-element.87), channel_id=1, source_target_pairs={{0,2},{1,3},{2,0},{3,1},{4,6},{5,7},{6,4},{7,5},{8,10},{9,11},{10,... | collective-permute-start | bytes 1572872 | tf_op jit(solution)/shard_map/ppermute | solution.py:17
  64.0 23.3 %collective-permute-start.16 = (bf16[2,128,1024]{2,1,0:T(8,128)(2,1)}, bf16[2,128,1024]{2,1,0:T(8,128)(2,1)}, u32[]{:S(2)}, u32[]{:S(2)}) collective-permute-start(bf16[2,128,1024]{2,1,0:T(8,128)(2,1)} %get-tuple-element.88), channel_id=1, source_target_pairs={{0,1},{1,2},{2,3},{3,0},{4,5},{5,6},{6,7},{7,4},{8,9},{9,10},{10,1... | collective-permute-start | bytes 1572872 | tf_op jit(solution)/shard_map/ppermute | solution.py:17
  94.9 15.5 %collective-permute-start.18 = (bf16[4,4,32,1024]{3,2,1,0:T(8,128)(2,1)}, bf16[4,4,32,1024]{3,2,1,0:T(8,128)(2,1)S(1)}, u32[]{:S(2)}, u32[]{:S(2)}) collective-permute-start(bf16[4,4,32,1024]{3,2,1,0:T(8,128)(2,1)} %get-tuple-element.123), channel_id=1, source_target_pairs={{0,8},{8,0},{1,9},{9,1},{2,10},{10,2},{3,11},{11,3},{4,12},{12,4},... | collective-permute-start | bytes 3145736 | tf_op jit(solution)/shard_map/ppermute | solution.py:17
  95.0 15.4 %collective-permute-start.19 = (bf16[128,1024]{1,0:T(8,128)(2,1)S(1)}, bf16[128,1024]{1,0:T(8,128)(2,1)S(1)}, u32[]{:S(2)}, u32[]{:S(2)}) collective-permute-start(bf16[128,1024]{1,0:T(8,128)(2,1)S(1)} %fusion.9), channel_id=1, source_target_pairs={{0,4},{4,0},{1,5},{5,1},{2,6},{6,2},{3,7},{7,3},{8,12},{12,8},{9,1... | collective-permute-start | bytes 786440 | tf_op jit(solution)/shard_map/ppermute | solution.py:17
  98.4 25.5 %collective-permute-start.21 = (bf16[4,32,2048]{2,1,0:T(8,128)(2,1)S(1)}, bf16[4,32,2048]{2,1,0:T(8,128)(2,1)S(1)}, u32[]{:S(2)}, u32[]{:S(2)}) collective-permute-start(bf16[4,32,2048]{2,1,0:T(8,128)(2,1)S(1)} %get-tuple-element.126), channel_id=1, source_target_pairs={{0,48},{16,0},{32,16},{48,32},{1,49},{17,1},{33,17},{49,33},{2,50}... | collective-permute-start | bytes 1572872 | tf_op jit(solution)/shard_map/ppermute | solution.py:17
  109.0 22.3 %collective-permute-start.22 = (bf16[4,32,2048]{2,1,0:T(8,128)(2,1)}, bf16[4,32,2048]{2,1,0:T(8,128)(2,1)}, u32[]{:S(2)}, u32[]{:S(2)}) collective-permute-start(bf16[4,32,2048]{2,1,0:T(8,128)(2,1)} %get-tuple-element.128), channel_id=1, source_target_pairs={{0,32},{16,48},{32,0},{48,16},{1,33},{17,49},{33,1},{49,17},{2,34}... | collective-permute-start | bytes 1572872 | tf_op jit(solution)/shard_map/ppermute | solution.py:17
  124.9 21.9 %collective-permute-start.24 = (bf16[2,128,1024]{2,1,0:T(8,128)(2,1)}, bf16[2,128,1024]{2,1,0:T(8,128)(2,1)}, u32[]{:S(2)}, u32[]{:S(2)}) collective-permute-start(bf16[2,128,1024]{2,1,0:T(8,128)(2,1)} %get-tuple-element.132), channel_id=1, source_target_pairs={{0,1},{1,2},{2,3},{3,0},{4,5},{5,6},{6,7},{7,4},{8,9},{9,10},{10,1... | collective-permute-start | bytes 1572872 | tf_op jit(solution)/shard_map/ppermute | solution.py:17
  131.3 27.6 %collective-permute-start.27 = (bf16[4,32,1024]{2,1,0:T(8,128)(2,1)S(1)}, bf16[4,32,1024]{2,1,0:T(8,128)(2,1)}, u32[]{:S(2)}, u32[]{:S(2)}) collective-permute-start(bf16[4,32,1024]{2,1,0:T(8,128)(2,1)S(1)} %get-tuple-element.158), channel_id=1, source_target_pairs={{0,32},{16,48},{32,0},{48,16},{1,33},{17,49},{33,1},{49,17},{2,34}... | collective-permute-start | bytes 786440 | tf_op jit(solution)/shard_map/ppermute | solution.py:17
  134.0 24.8 %collective-permute-start.31 = (bf16[2,128,1024]{2,1,0:T(8,128)(2,1)}, bf16[2,128,1024]{2,1,0:T(8,128)(2,1)}, u32[]{:S(2)}, u32[]{:S(2)}) collective-permute-start(bf16[2,128,1024]{2,1,0:T(8,128)(2,1)} %get-tuple-element.143), channel_id=1, source_target_pairs={{0,2},{1,3},{2,0},{3,1},{4,6},{5,7},{6,4},{7,5},{8,10},{9,11},{10,... | collective-permute-start | bytes 1572872 | tf_op jit(solution)/shard_map/ppermute | solution.py:17
  171.1 18.4 %all-to-all-start = ((bf16[4,32,1024]{2,1,0:T(8,128)(2,1)}), bf16[4,32,1024]{2,1,0:T(8,128)(2,1)S(1)}, u32[]{:S(2)}, u32[]{:S(2)}) async-start(bf16[4,32,1024]{2,1,0:T(8,128)(2,1)} %add_convert_fusion), calls=%async_computation | async-start | bytes 524288 | tf_op jit(solution)/shard_map/all_to_all | solution.py:33
  (34 other events, 417.7 us)
